TPU v7x, 32 devices: a whole 2x2x4 slice. The times are simulated.
32 devices in a mesh: fsdp: 8 (over y, x, core), seq: 4 (over z).
Axes of the slice: x: 2, y: 2, z: 4, core: 2. Of those that a mesh axis runs over, the one named last changes fastest.
Arguments:
- inputs: bfloat16 [8, 1568, 1024], P('fsdp', 'seq'), may hold values from -6 to 6
- clip_mask: int32 [8], P('fsdp'), may hold values 0 or 1
- ln1_gain: float32 [1024], replicated, may hold values from 0.5 to 1.5
- ln1_bias: float32 [1024], replicated, may hold values from -1 to 1
- w_query: bfloat16 [1024, 1024], P('fsdp'), may hold values from -0.1875 to 0.1875
- b_query: float32 [1024], replicated, may hold values from -1 to 1
- w_key: bfloat16 [1024, 1024], P('fsdp'), may hold values from -0.1875 to 0.1875
- w_value: bfloat16 [1024, 1024], P('fsdp'), may hold values from -0.1875 to 0.1875
- b_value: float32 [1024], replicated, may hold values from -1 to 1
- w_out: bfloat16 [1024, 1024], P('fsdp'), may hold values from -3 to 3
- b_out: float32 [1024], replicated, may hold values from -1 to 1
- ln2_gain: float32 [1024], replicated, may hold values from 0.5 to 1.5
- ln2_bias: float32 [1024], replicated, may hold values from -1 to 1
- w_fc1: bfloat16 [1024, 4096], P('fsdp'), may hold values from -0.1875 to 0.1875
- b_fc1: float32 [4096], replicated, may hold values from -1 to 1
- w_fc2: bfloat16 [4096, 1024], P('fsdp'), may hold values from -0.09375 to 0.09375
- b_fc2: float32 [1024], replicated, may hold values from -1 to 1
- cotangent: bfloat16 [8, 1568, 1024], P('fsdp', 'seq'), may hold values from -6 to 6
Outputs:
- output: bfloat16 [8, 1568, 1024], P('fsdp', 'seq')
- grad_inputs: float32 [8, 1568, 1024], P('fsdp', 'seq')
- grad_ln1_gain: float32 [1024], P(('fsdp', 'seq'))
- grad_ln1_bias: float32 [1024], P(('fsdp', 'seq'))
- grad_w_query: float32 [1024, 1024], P(('fsdp', 'seq'))
- grad_b_query: float32 [1024], P(('fsdp', 'seq'))
- grad_w_key: float32 [1024, 1024], P(('fsdp', 'seq'))
- grad_w_value: float32 [1024, 1024], P(('fsdp', 'seq'))
- grad_b_value: float32 [1024], P(('fsdp', 'seq'))
- grad_w_out: float32 [1024, 1024], P(('fsdp', 'seq'))
- grad_b_out: float32 [1024], P(('fsdp', 'seq'))
- grad_ln2_gain: float32 [1024], P(('fsdp', 'seq'))
- grad_ln2_bias: float32 [1024], P(('fsdp', 'seq'))
- grad_w_fc1: float32 [1024, 4096], P(('fsdp', 'seq'))
- grad_b_fc1: float32 [4096], P(('fsdp', 'seq'))
- grad_w_fc2: float32 [4096, 1024], P(('fsdp', 'seq'))
- grad_b_fc2: float32 [1024], P(('fsdp', 'seq'))
Inputs may be any that keep to these rules, and one draw needn't show every extreme that they name: `clip_mask`: 1 where the clip's slot holds a clip, 0 where it holds none.
All inputs are finite; a program needn't handle non-finite values. No bound on the sum of `clip_mask` on one device may be relied on, other than what follows from the above.
Results may differ from a plain program's by a relative error of at most 0.011.
Values may be sent and summed in bfloat16 or wider, within the bound.
No kernel may reach another device: no remote copies, remote signals or barrier semaphores. Data moves between devices by JAX's collectives and lax.ppermute only.
A program may use at most 256 MiB of HBM per device.

v0:
```python
import jax
import jax.numpy as jnp
from jax import lax
from jax.sharding import PartitionSpec as P

HEADS = 16
HD = 64


EPSILON = 1e-06


def normalize(rows, gain, shift):
    center = rows - jnp.mean(rows, -1, keepdims=True)
    inverse = lax.rsqrt(jnp.mean(center * center, -1, keepdims=True) + EPSILON)
    normed = center * inverse
    return (normed * gain + shift, normed, inverse)


def norm_grad(grad, normed, inverse, gain):
    scaled = grad * gain
    inner = (
        scaled
        - jnp.mean(scaled, -1, keepdims=True)
        - normed * jnp.mean(scaled * normed, -1, keepdims=True)
    )
    return inner * inverse


def to_pairs(array):
    clips, length, heads_here, size = array.shape
    return array.transpose(0, 2, 1, 3).reshape(clips * heads_here, length, size)


def from_pairs(array, clips):
    pairs, length, size = array.shape
    return array.reshape(clips, pairs // clips, length, size).transpose(0, 2, 1, 3)


def head_forward(blocks):
    query, keys, values = blocks
    scale = query.shape[-1] ** (-0.5)
    scores = jnp.dot(query, keys.T, preferred_element_type=jnp.float32) * scale
    peak = jnp.max(scores, -1, keepdims=True)
    expo = jnp.exp(scores - peak)
    total = jnp.sum(expo, -1, keepdims=True)
    weights = (expo / total).astype(jnp.bfloat16)
    mixed = jnp.dot(weights, values, preferred_element_type=jnp.float32).astype(jnp.bfloat16)
    return (mixed, (peak + jnp.log(total))[:, 0])


def head_backward(blocks):
    query, keys, values, grad_out, logsum = blocks
    scale = query.shape[-1] ** (-0.5)
    scores = jnp.dot(query, keys.T, preferred_element_type=jnp.float32) * scale
    probs = jnp.exp(scores - logsum[:, None])
    grad_probs = jnp.dot(grad_out, values.T, preferred_element_type=jnp.float32)
    inner = jnp.sum(probs * grad_probs, -1, keepdims=True)
    grad_scores = (probs * (grad_probs - inner)).astype(jnp.bfloat16)
    grad_query = (jnp.dot(grad_scores, keys, preferred_element_type=jnp.float32) * scale).astype(
        jnp.bfloat16
    )
    grad_keys = (jnp.dot(grad_scores.T, query, preferred_element_type=jnp.float32) * scale).astype(
        jnp.bfloat16
    )
    grad_values = jnp.dot(
        probs.astype(jnp.bfloat16).T, grad_out, preferred_element_type=jnp.float32
    ).astype(jnp.bfloat16)
    return (grad_query, grad_keys, grad_values)


def run_forward(inputs, mask_rows, vectors, attn_mats, mlp_mats):
    ln1_gain, ln1_bias, b_query, b_value, b_out, ln2_gain, ln2_bias, b_fc1, b_fc2 = vectors
    w_query, w_key, w_value, w_out = attn_mats
    w_fc1, w_fc2 = mlp_mats
    clips, local_len, width = inputs.shape
    rows = inputs.reshape(clips * local_len, width).astype(jnp.float32)
    normed1, hat1, inv1 = normalize(rows, ln1_gain, ln1_bias)
    first_in = normed1.astype(jnp.bfloat16)
    head_shape = (clips, local_len, HEADS, HD)
    query = (jnp.dot(first_in, w_query, preferred_element_type=jnp.float32) + b_query).astype(
        jnp.bfloat16
    )
    keys = jnp.dot(first_in, w_key, preferred_element_type=jnp.float32).astype(jnp.bfloat16)
    values = (jnp.dot(first_in, w_value, preferred_element_type=jnp.float32) + b_value).astype(
        jnp.bfloat16
    )
    query_heads, keys_heads, values_heads = (
        lax.all_to_all(query.reshape(head_shape), "seq", split_axis=2, concat_axis=1, tiled=True),
        lax.all_to_all(keys.reshape(head_shape), "seq", split_axis=2, concat_axis=1, tiled=True),
        lax.all_to_all(values.reshape(head_shape), "seq", split_axis=2, concat_axis=1, tiled=True),
    )
    query_pairs = to_pairs(query_heads)
    keys_pairs = to_pairs(keys_heads)
    values_pairs = to_pairs(values_heads)
    mixed_pairs, logsum = lax.map(head_forward, (query_pairs, keys_pairs, values_pairs))
    mixed_tokens = lax.all_to_all(
        from_pairs(mixed_pairs, clips), "seq", split_axis=1, concat_axis=2, tiled=True
    )
    attended = mixed_tokens.reshape(clips * local_len, width)
    branch = jnp.dot(attended, w_out, preferred_element_type=jnp.float32) + b_out
    middle = rows + branch
    normed2, hat2, inv2 = normalize(middle, ln2_gain, ln2_bias)
    second_in = normed2.astype(jnp.bfloat16)
    hidden = jnp.dot(second_in, w_fc1, preferred_element_type=jnp.float32) + b_fc1
    activ = jax.nn.gelu(hidden, approximate=False).astype(jnp.bfloat16)
    final = jnp.dot(activ, w_fc2, preferred_element_type=jnp.float32) + b_fc2
    result = (middle + final) * mask_rows
    saved = (
        first_in,
        hat1,
        inv1,
        query_pairs,
        keys_pairs,
        values_pairs,
        logsum,
        attended,
        second_in,
        hat2,
        inv2,
        hidden,
        activ,
    )
    return (result, saved)


def on_device(
    inputs,
    clip_mask,
    ln1_gain,
    ln1_bias,
    w_query,
    b_query,
    w_key,
    w_value,
    b_value,
    w_out,
    b_out,
    ln2_gain,
    ln2_bias,
    w_fc1,
    b_fc1,
    w_fc2,
    b_fc2,
    cotangent,
):
    clips, local_len, width = inputs.shape
    mask_rows = jnp.repeat(clip_mask.astype(jnp.float32), local_len)[:, None]
    vectors = (ln1_gain, ln1_bias, b_query, b_value, b_out, ln2_gain, ln2_bias, b_fc1, b_fc2)
    attn_mats = (
        lax.all_gather(w_query, "fsdp", axis=0, tiled=True),
        lax.all_gather(w_key, "fsdp", axis=0, tiled=True),
        lax.all_gather(w_value, "fsdp", axis=0, tiled=True),
        lax.all_gather(w_out, "fsdp", axis=0, tiled=True),
    )
    mlp_mats = (
        lax.all_gather(w_fc1, "fsdp", axis=0, tiled=True),
        lax.all_gather(w_fc2, "fsdp", axis=0, tiled=True),
    )
    result, unused = run_forward(inputs, mask_rows, vectors, attn_mats, mlp_mats)
    output = result.reshape(clips, local_len, width).astype(jnp.bfloat16)
    attn_back = (
        lax.all_gather(w_query, "fsdp", axis=0, tiled=True),
        lax.all_gather(w_key, "fsdp", axis=0, tiled=True),
        lax.all_gather(w_value, "fsdp", axis=0, tiled=True),
        lax.all_gather(w_out, "fsdp", axis=0, tiled=True),
    )
    mlp_back = (
        lax.all_gather(w_fc1, "fsdp", axis=0, tiled=True),
        lax.all_gather(w_fc2, "fsdp", axis=0, tiled=True),
    )
    full_query, full_key, full_value, full_out = attn_back
    full_fc1, full_fc2 = mlp_back
    unused_result, saved = run_forward(inputs, mask_rows, vectors, attn_back, mlp_back)
    (
        first_in,
        hat1,
        inv1,
        query_pairs,
        keys_pairs,
        values_pairs,
        logsum,
        attended,
        second_in,
        hat2,
        inv2,
        hidden,
        activ,
    ) = saved
    grad_rows = cotangent.reshape(clips * local_len, width).astype(jnp.float32) * mask_rows
    grad_low = grad_rows.astype(jnp.bfloat16)
    grad_b_fc2 = jnp.sum(grad_rows, 0)
    grad_w_fc2 = jnp.dot(activ.T, grad_low, preferred_element_type=jnp.float32)
    grad_activ = jnp.dot(grad_low, full_fc2.T, preferred_element_type=jnp.float32)
    unused_gelu, gelu_pull = jax.vjp(lambda value: jax.nn.gelu(value, approximate=False), hidden)
    grad_hidden = gelu_pull(grad_activ)[0].astype(jnp.bfloat16)
    grad_w_fc1 = jnp.dot(second_in.T, grad_hidden, preferred_element_type=jnp.float32)
    grad_b_fc1 = jnp.sum(grad_hidden.astype(jnp.float32), 0)
    grad_second = jnp.dot(grad_hidden, full_fc1.T, preferred_element_type=jnp.float32)
    grad_ln2_gain = jnp.sum(grad_second * hat2, 0)
    grad_ln2_bias = jnp.sum(grad_second, 0)
    grad_middle = grad_rows + norm_grad(grad_second, hat2, inv2, ln2_gain)
    grad_branch = grad_middle.astype(jnp.bfloat16)
    grad_w_out = jnp.dot(attended.T, grad_branch, preferred_element_type=jnp.float32)
    grad_b_out = jnp.sum(grad_branch.astype(jnp.float32), 0)
    grad_mixed = jnp.dot(grad_branch, full_out.T, preferred_element_type=jnp.float32).astype(
        jnp.bfloat16
    )
    grad_mixed_heads = lax.all_to_all(
        grad_mixed.reshape(clips, local_len, HEADS, HD),
        "seq",
        split_axis=2,
        concat_axis=1,
        tiled=True,
    )
    grad_q_pairs, grad_k_pairs, grad_v_pairs = lax.map(
        head_backward, (query_pairs, keys_pairs, values_pairs, to_pairs(grad_mixed_heads), logsum)
    )
    grad_query, grad_keys, grad_values = (
        lax.all_to_all(
            from_pairs(grad_q_pairs, clips), "seq", split_axis=1, concat_axis=2, tiled=True
        ),
        lax.all_to_all(
            from_pairs(grad_k_pairs, clips), "seq", split_axis=1, concat_axis=2, tiled=True
        ),
        lax.all_to_all(
            from_pairs(grad_v_pairs, clips), "seq", split_axis=1, concat_axis=2, tiled=True
        ),
    )
    grad_query = grad_query.reshape(clips * local_len, width)
    grad_keys = grad_keys.reshape(clips * local_len, width)
    grad_values = grad_values.reshape(clips * local_len, width)
    grad_w_query = jnp.dot(first_in.T, grad_query, preferred_element_type=jnp.float32)
    grad_w_key = jnp.dot(first_in.T, grad_keys, preferred_element_type=jnp.float32)
    grad_w_value = jnp.dot(first_in.T, grad_values, preferred_element_type=jnp.float32)
    grad_b_query = jnp.sum(grad_query.astype(jnp.float32), 0)
    grad_b_value = jnp.sum(grad_values.astype(jnp.float32), 0)
    grad_first = (
        jnp.dot(grad_query, full_query.T, preferred_element_type=jnp.float32)
        + jnp.dot(grad_keys, full_key.T, preferred_element_type=jnp.float32)
        + jnp.dot(grad_values, full_value.T, preferred_element_type=jnp.float32)
    )
    grad_ln1_gain = jnp.sum(grad_first * hat1, 0)
    grad_ln1_bias = jnp.sum(grad_first, 0)
    grad_inputs = grad_middle + norm_grad(grad_first, hat1, inv1, ln1_gain)
    grad_inputs = grad_inputs.reshape(clips, local_len, width)
    all_grads = (
        grad_ln1_gain,
        grad_ln1_bias,
        grad_w_query,
        grad_b_query,
        grad_w_key,
        grad_w_value,
        grad_b_value,
        grad_w_out,
        grad_b_out,
        grad_ln2_gain,
        grad_ln2_bias,
        grad_w_fc1,
        grad_b_fc1,
        grad_w_fc2,
        grad_b_fc2,
    )
    owned = (
        lax.psum_scatter(all_grads[0], ("fsdp", "seq"), scatter_dimension=0, tiled=True),
        lax.psum_scatter(all_grads[1], ("fsdp", "seq"), scatter_dimension=0, tiled=True),
        lax.psum_scatter(all_grads[2], ("fsdp", "seq"), scatter_dimension=0, tiled=True),
        lax.psum_scatter(all_grads[3], ("fsdp", "seq"), scatter_dimension=0, tiled=True),
        lax.psum_scatter(all_grads[4], ("fsdp", "seq"), scatter_dimension=0, tiled=True),
        lax.psum_scatter(all_grads[5], ("fsdp", "seq"), scatter_dimension=0, tiled=True),
        lax.psum_scatter(all_grads[6], ("fsdp", "seq"), scatter_dimension=0, tiled=True),
        lax.psum_scatter(all_grads[7], ("fsdp", "seq"), scatter_dimension=0, tiled=True),
        lax.psum_scatter(all_grads[8], ("fsdp", "seq"), scatter_dimension=0, tiled=True),
        lax.psum_scatter(all_grads[9], ("fsdp", "seq"), scatter_dimension=0, tiled=True),
        lax.psum_scatter(all_grads[10], ("fsdp", "seq"), scatter_dimension=0, tiled=True),
        lax.psum_scatter(all_grads[11], ("fsdp", "seq"), scatter_dimension=0, tiled=True),
        lax.psum_scatter(all_grads[12], ("fsdp", "seq"), scatter_dimension=0, tiled=True),
        lax.psum_scatter(all_grads[13], ("fsdp", "seq"), scatter_dimension=0, tiled=True),
        lax.psum_scatter(all_grads[14], ("fsdp", "seq"), scatter_dimension=0, tiled=True),
    )
    return (
        output,
        grad_inputs,
        owned[0],
        owned[1],
        owned[2],
        owned[3],
        owned[4],
        owned[5],
        owned[6],
        owned[7],
        owned[8],
        owned[9],
        owned[10],
        owned[11],
        owned[12],
        owned[13],
        owned[14],
    )


def solution(mesh):
    return jax.shard_map(
        on_device,
        mesh=mesh,
        in_specs=(
            P("fsdp", "seq", None),
            P("fsdp"),
            P(),
            P(),
            P("fsdp", None),
            P(),
            P("fsdp", None),
            P("fsdp", None),
            P(),
            P("fsdp", None),
            P(),
            P(),
            P(),
            P("fsdp", None),
            P(),
            P("fsdp", None),
            P(),
            P("fsdp", "seq", None),
        ),
        out_specs=(
            P("fsdp", "seq", None),
            P("fsdp", "seq", None),
            P(("fsdp", "seq")),
            P(("fsdp", "seq")),
            P(("fsdp", "seq"), None),
            P(("fsdp", "seq")),
            P(("fsdp", "seq"), None),
            P(("fsdp", "seq"), None),
            P(("fsdp", "seq")),
            P(("fsdp", "seq"), None),
            P(("fsdp", "seq")),
            P(("fsdp", "seq")),
            P(("fsdp", "seq")),
            P(("fsdp", "seq"), None),
            P(("fsdp", "seq")),
            P(("fsdp", "seq"), None),
            P(("fsdp", "seq")),
        ),
        check_vma=False,
    )
```

profile of v0, /device:TPU:0, one launch (start us, length us, event | category | flops | bytes accessed | tf_op | source)
XLA Modules:
  0.0 1689.4 jit_solution(14784483086480142402)
XLA Ops:
  13.5 27.1 %all-gather.7.cloned.1.call-done = bf16[1024,1024]{1,0:T(8,128)(2,1)} async-done(((bf16[128,1024]{1,0:T(8,128)(2,1)}), bf16[1024,1024]{1,0:T(8,128)(2,1)}) %all-gather.7.cloned.1.call-update) | async-done | bytes 2097168 | tf_op jit(solution)/shard_map/all_gather | solution.py:151
  44.8 4.6 all-to-all-start
  49.5 20.9 %all-gather.9.cloned.1.call-done = bf16[1024,1024]{1,0:T(8,128)(2,1)} async-done(((bf16[128,1024]{1,0:T(8,128)(2,1)}), bf16[1024,1024]{1,0:T(8,128)(2,1)}) %all-gather.9.cloned.1.call-update) | async-done | bytes 2097168 | tf_op jit(solution)/shard_map/all_gather | solution.py:152
  79.9 20.3 %all-gather.11.cloned.1.call-done = bf16[1024,1024]{1,0:T(8,128)(2,1)} async-done(((bf16[128,1024]{1,0:T(8,128)(2,1)}), bf16[1024,1024]{1,0:T(8,128)(2,1)}) %all-gather.11.cloned.1.call-update) | async-done | bytes 2097168 | tf_op jit(solution)/shard_map/all_gather | solution.py:153
  105.3 4.3 all-to-all-start.2
  113.0 22.1 %all-to-all-done.2 = bf16[1,392,16,64]{1,3,0,2:T(8,128)(2,1)} async-done(((bf16[1,392,16,64]{1,3,0,2:T(8,128)(2,1)}), bf16[1,392,16,64]{1,3,0,2:T(8,128)(2,1)}, u32[]{:S(2)}, u32[]{:S(2)}) %all-to-all-start.2) | async-done | bytes 802848 | tf_op jit(solution)/shard_map/all_to_all | solution.py:91
  138.7 29.4 %while.37 = (s32[]{:T(128)}, bf16[4,1568,64]{1,2,0:T(8,128)(2,1)}, f32[4,1568]{1,0:T(4,128)S(1)}, bf16[4,1568,64]{2,1,0:T(8,128)(2,1)S(1)}, bf16[4,1568,64]{2,1,...) while((s32[]{:T(128)}, bf16[4,1568,64]{1,2,0:T(8,128)(2,1)}, ...), condition=%wide.region_11.12_spmd, body=%wide.region_8.0_spmd.sunk | while | flops 651634176 | bytes 30998112 | solution.py:96
  178.4 4.7 all-to-all-start.4
  183.8 19.4 %all-to-all-done.4 = bf16[4,2,50176]{2,1,0:T(2,128)(2,1)} async-done(((bf16[4,2,50176]{2,1,0:T(2,128)(2,1)}), bf16[4,2,50176]{2,1,0:T(2,128)(2,1)}, u32[]{:S(2)}, u32[]{:S(2)}) %all-to-all-start.4) | async-done | bytes 802848 | tf_op jit(solution)/shard_map/all_to_all | solution.py:97
  216.0 21.3 %fusion.70 = (f32[392,4096]{1,0:T(8,128)}, f32[392,4096]{1,0:T(8,128)}) fusion(f32[4096]{0:T(1024)S(1)} %copy-done.16, bf16[1024,4096]{1,0:T(8,128)(2,1)} %all-gather.15.cloned.1.call-done, f32[392,1024]{1,0:T(8,128)} %copy-done.4, f32[392]{0:T(512)S(1)} %add_rsqrt_fusion, f32[392]{0:T(512)S(1)} %broadcast_multiply_fusion.4, f32[1024]{0:T(1024)S(1)} %copy-done.45, ...), kind=kOutput, calls=%fused_computation.79 | convolution fusion | flops 3391496192 | bytes 22867008 | tf_op jit(solution)/shard_map/dot_general | solution.py:105
  237.3 4.9 all-gather.17.cloned.1.call-done
  242.2 11.8 convert_reduce_fusion
  253.9 4.4 multiply_reduce_fusion.3
  265.0 4.6 all-to-all-start.5
  269.6 5.0 fusion.148
  274.7 34.4 %all-to-all-done.5 = bf16[1,392,16,64]{1,3,0,2:T(8,128)(2,1)} async-done(((bf16[1,392,16,64]{1,3,0,2:T(8,128)(2,1)}), bf16[1,392,16,64]{1,3,0,2:T(8,128)(2,1)}, u32[]{:S(2)}, u32[]{:S(2)}) %all-to-all-start.5) | async-done | bytes 802848 | tf_op jit(solution)/shard_map/all_to_all | solution.py:209
  314.8 131.6 %while.38 = (s32[]{:T(128)}, bf16[4,1568,64]{1,2,0:T(8,128)(2,1)}, bf16[4,1568,64]{1,2,0:T(8,128)(2,1)}, bf16[4,1568,64]{1,2,0:T(8,128)(2,1)}, bf16[4,1568,64]{2...) while((s32[]{:T(128)}, bf16[4,1568,64]{1,2,0:T(8,128)(2,1)}, ...), condition=%wide.region_18.19_spmd, body=%wide.region_16.18_spmd.sunk | while | flops 1593688576 | bytes 157126304 | solution.py:216
  317.5 5.7 multiply_reduce_fusion.14
  324.5 10.5 multiply_convert_fusion.5
  335.0 4.3 fusion.257
  339.3 5.1 fusion.258
  350.4 5.8 multiply_reduce_fusion.14
  357.4 10.5 multiply_convert_fusion.5
  367.9 4.3 fusion.257
  372.2 5.1 fusion.258
  383.4 5.8 multiply_reduce_fusion.14
  390.3 10.5 multiply_convert_fusion.5
  400.8 4.3 fusion.257
  405.1 5.1 fusion.258
  416.3 5.7 multiply_reduce_fusion.14
  423.3 10.5 multiply_convert_fusion.5
  433.8 4.3 fusion.257
  438.1 5.1 fusion.258
  456.8 21.2 %all_to_all.162 = bf16[4,2,50176]{2,1,0:T(2,128)(2,1)} all-to-all(bf16[4,2,50176]{2,1,0:T(2,128)(2,1)} %reshape.302), channel_id=1, replica_groups=mesh['fsdp'=8,'seq'=4] {'seq'}, dimensions={0} | all-to-all | bytes 1605632 | tf_op jit(solution)/shard_map/all_to_all | solution.py:220
  486.0 5.1 fusion.188
  501.4 40.8 %all_to_all.163 = bf16[4,2,50176]{2,1,0:T(2,128)(2,1)} all-to-all(bf16[4,2,50176]{2,1,0:T(2,128)(2,1)} %reshape.304), channel_id=1, replica_groups=mesh['fsdp'=8,'seq'=4] {'seq'}, dimensions={0} | all-to-all | bytes 1605632 | tf_op jit(solution)/shard_map/all_to_all | solution.py:223
  550.2 5.1 fusion.186
  565.7 38.7 %all_to_all.164 = bf16[4,2,50176]{2,1,0:T(2,128)(2,1)} all-to-all(bf16[4,2,50176]{2,1,0:T(2,128)(2,1)} %reshape.306), channel_id=1, replica_groups=mesh['fsdp'=8,'seq'=4] {'seq'}, dimensions={0} | all-to-all | bytes 1605632 | tf_op jit(solution)/shard_map/all_to_all | solution.py:226
  612.3 5.1 fusion.184
  618.2 13.0 fusion.182
  631.9 15.5 fusion.83
  648.3 28.9 %while.36 = (s32[]{:T(128)}, bf16[4,1568,64]{1,2,0:T(8,128)(2,1)}, bf16[4,1568,64]{2,1,0:T(8,128)(2,1)S(1)}, bf16[4,1568,64]{2,1,0:T(8,128)(2,1)S(1)}, bf16[4,1568,64]{2,1,0:T(8,128)(2,1)}, /*index=5*/s32[]{:T(128)}) while((s32[]{:T(128)}, bf16[4,1568,64]{1,2,0:T(8,128)(2,1)}, bf16[4,1568,64]{2,1,0:T(8,128)(2,1)S(1)}, ...), condition=%wide.region_5.6_spmd, body=%wide.region_2.5_spmd.sunk | while | flops 651632576 | bytes 30954188 | solution.py:96
  690.1 33.7 %all-to-all-done.3 = bf16[4,2,50176]{2,1,0:T(2,128)(2,1)S(1)} async-done(((bf16[4,2,50176]{2,1,0:T(2,128)(2,1)}), bf16[4,2,50176]{2,1,0:T(2,128)(2,1)S(1)}, u32[]{:S(2)}, u32[]{:S(2)}) %all-to-all-start.3) | async-done | bytes 802848 | tf_op jit(solution)/shard_map/all_to_all | solution.py:97
  729.7 26.3 %fusion.137 = bf16[1,392,1024]{2,1,0:T(8,128)(2,1)} fusion(f32[392,1024]{1,0:T(8,128)S(1)} %get-tuple-element.198, bf16[4096,1024]{1,0:T(8,128)(2,1)} %all-gather.17.cloned.1.call-done, bf16[1024,4096]{1,0:T(8,128)(2,1)} %all-gather.15.cloned.1.call-done, f32[4096]{0:T(1024)S(1)} %copy-done.17, f32[]{:T(128)} %bitcast.42, f32[1024]{0:T(1024)S(1)} %copy-done.44, ...), kind=kOutput, calls=%fused_computation.189 | convolution fusion | flops 6686253056 | bytes 19217476 | tf_op jit(solution)/shard_map/dot_general | solution.py:107
  766.1 40.2 %all-reduce.9 = (f32[1024]{0:T(1024)S(1)}, f32[1024]{0:T(1024)S(1)}, f32[1024]{0:T(1024)S(1)}, f32[1024]{0:T(1024)S(1)}, f32[1024]{0:T(1024)S(1)}, /*index=5*/f3...) all-reduce(f32[1024]{0:T(1024)S(1)} %get-tuple-element.134, ...), channel_id=2, replica_groups=mesh['fsdp'=8,'seq'=4] {'fsdp','seq'}, use_global_device_ids=true, to_apply=%region_22.23.clone | all-reduce | flops 12288 | bytes 98304
  814.6 136.9 %reduce-scatter.11.cloned.1.call-done = f32[32,1024]{1,0:T(8,128)} async-done(((f32[1024,1024]{1,0:T(8,128)}), f32[32,1024]{1,0:T(8,128)}) %reduce-scatter.11.cloned.1.call-update) | async-done | bytes 131088 | tf_op jit(solution)/shard_map/reduce_scatter | solution.py:270
  951.5 365.9 %reduce-scatter.15.cloned.1.call-done = f32[32,4096]{1,0:T(8,128)} async-done(((f32[1024,4096]{1,0:T(8,128)}), f32[32,4096]{1,0:T(8,128)}) %reduce-scatter.15.cloned.1.call-update) | async-done | bytes 524304 | tf_op jit(solution)/shard_map/reduce_scatter | solution.py:276
  1317.5 364.9 %reduce-scatter.17.cloned.1.call-done = f32[128,1024]{1,0:T(8,128)} async-done(((f32[4096,1024]{1,0:T(8,128)}), f32[128,1024]{1,0:T(8,128)}) %reduce-scatter.17.cloned.1.call-update) | async-done | bytes 524304 | tf_op jit(solution)/shard_map/reduce_scatter | solution.py:278
  (268 shorter events, 248.7 us)
Async XLA Ops:
  7.2 33.4 %all-gather.7.cloned.1.call-start = ((), (), s32[]{:S(2)}) async-start(), calls=%async_computation.15 | async-start | bytes 2359296 | tf_op jit(solution)/shard_map/all_gather | solution.py:151
  7.9 62.4 %all-gather.9.cloned.1.call-start = ((), (), s32[]{:S(2)}) async-start(), calls=%async_computation.16 | async-start | bytes 2359296 | tf_op jit(solution)/shard_map/all_gather | solution.py:152
  8.7 91.5 %all-gather.11.cloned.1.call-start = ((), (), s32[]{:S(2)}) async-start(), calls=%async_computation.17 | async-start | bytes 2359296 | tf_op jit(solution)/shard_map/all_gather | solution.py:153
  9.4 201.7 %all-gather.13.cloned.1.call-start = ((), (), s32[]{:S(2)}) async-start(), calls=%async_computation.18 | async-start | bytes 2359296 | tf_op jit(solution)/shard_map/all_gather | solution.py:154
  10.0 205.9 %all-gather.15.cloned.1.call-start = ((), (), s32[]{:S(2)}) async-start(), calls=%async_computation.19 | async-start | bytes 9437184 | tf_op jit(solution)/shard_map/all_gather | solution.py:157
  11.9 88.3 %copy-start.18 = (f32[392]{0:T(512)}, f32[392]{0:T(512)S(1)}, u32[]{:S(2)}) copy-start(f32[392]{0:T(512)S(1)} %broadcast_multiply_fusion.6) | copy-start | bytes 4708
  13.4 86.8 %copy-start.25 = (f32[392]{0:T(512)}, f32[392]{0:T(512)S(1)}, u32[]{:S(2)}) copy-start(f32[392]{0:T(512)S(1)} %add_rsqrt_fusion.2) | copy-start | bytes 4708
  13.4 56.9 %copy-start.2 = (bf16[1,392,1024]{2,1,0:T(8,128)(2,1)S(1)}, bf16[1,392,1024]{2,1,0:T(8,128)(2,1)}, u32[]{:S(2)}) copy-start(bf16[1,392,1024]{2,1,0:T(8,128)(2,1)} %param.24) | copy-start | bytes 2408452
  13.4 56.9 %copy-start.30 = (f32[1024]{0:T(1024)S(1)}, f32[1024]{0:T(1024)}, u32[]{:S(2)}) copy-start(f32[1024]{0:T(1024)} %param.26) | copy-start | bytes 12292
  13.4 56.9 %copy-start.42 = (f32[1024]{0:T(1024)S(1)}, f32[1024]{0:T(1024)}, u32[]{:S(2)}) copy-start(f32[1024]{0:T(1024)} %param.27) | copy-start | bytes 12292
  44.8 30.8 %all-to-all-start = ((bf16[1,392,16,64]{1,3,0,2:T(8,128)(2,1)}), bf16[1,392,16,64]{1,3,0,2:T(8,128)(2,1)S(1)}, u32[]{:S(2)}, u32[]{:S(2)}) async-start(bf16[1,392,16,64]{1,3,0,2:T(8,128)(2,1)} %bitcast.17), calls=%async_computation | async-start | bytes 2097152 | tf_op jit(solution)/shard_map/all_to_all | solution.py:89
  49.4 50.7 %copy-start.41 = (f32[1024]{0:T(1024)S(1)}, f32[1024]{0:T(1024)}, u32[]{:S(2)}) copy-start(f32[1024]{0:T(1024)} %param.32) | copy-start | bytes 12292
  75.6 29.7 %all-to-all-start.1 = ((bf16[1,392,16,64]{1,3,0,2:T(8,128)(2,1)}), bf16[1,392,16,64]{1,3,0,2:T(8,128)(2,1)}, u32[]{:S(2)}, u32[]{:S(2)}) async-start(bf16[1,392,16,64]{1,3,0,2:T(8,128)(2,1)} %bitcast.24), calls=%async_computation.1 | async-start | bytes 2097152 | tf_op jit(solution)/shard_map/all_to_all | solution.py:90
  105.3 29.8 %all-to-all-start.2 = ((bf16[1,392,16,64]{1,3,0,2:T(8,128)(2,1)}), bf16[1,392,16,64]{1,3,0,2:T(8,128)(2,1)}, u32[]{:S(2)}, u32[]{:S(2)}) async-start(bf16[1,392,16,64]{1,3,0,2:T(8,128)(2,1)} %bitcast.31), calls=%async_computation.2 | async-start | bytes 2097152 | tf_op jit(solution)/shard_map/all_to_all | solution.py:91
  109.6 132.6 %all-gather.17.cloned.1.call-start = ((), (), s32[]{:S(2)}) async-start(), calls=%async_computation.20 | async-start | bytes 9437184 | tf_op jit(solution)/shard_map/all_gather | solution.py:158
  174.5 36.6 %copy-start.14 = (f32[1024]{0:T(1024)S(1)}, f32[1024]{0:T(1024)}, u32[]{:S(2)}) copy-start(f32[1024]{0:T(1024)} %param.34) | copy-start | bytes 12292
  178.4 24.8 %all-to-all-start.4 = ((bf16[4,2,50176]{2,1,0:T(2,128)(2,1)}), bf16[4,2,50176]{2,1,0:T(2,128)(2,1)}, u32[]{:S(2)}, u32[]{:S(2)}) async-start(bf16[4,2,50176]{2,1,0:T(2,128)(2,1)} %reshape.300), calls=%async_computation.4 | async-start | bytes 1605632 | tf_op jit(solution)/shard_map/all_to_all | solution.py:97
  211.1 4.8 copy-start.35
  211.1 4.8 copy-start.45
  214.4 44.0 %copy-start.21 = (f32[392]{0:T(512)}, f32[392]{0:T(512)S(1)}, u32[]{:S(2)}) copy-start(f32[392]{0:T(512)S(1)} %broadcast_multiply_fusion.4) | copy-start | bytes 4708
  215.9 42.5 %copy-start.28 = (f32[392]{0:T(512)}, f32[392]{0:T(512)S(1)}, u32[]{:S(2)}) copy-start(f32[392]{0:T(512)S(1)} %add_rsqrt_fusion) | copy-start | bytes 4708
  242.2 11.8 copy-start.5
  242.2 11.8 copy-start.38
  265.0 44.0 %all-to-all-start.5 = ((bf16[1,392,16,64]{1,3,0,2:T(8,128)(2,1)}), bf16[1,392,16,64]{1,3,0,2:T(8,128)(2,1)}, u32[]{:S(2)}, u32[]{:S(2)}) async-start(bf16[1,392,16,64]{1,3,0,2:T(8,128)(2,1)} %bitcast.308), calls=%async_computation.5 | async-start | bytes 2097152 | tf_op jit(solution)/shard_map/all_to_all | solution.py:209
  269.6 545.0 %reduce-scatter.13.cloned.1.call-start = ((), (), s32[]{:S(2)}) async-start(), calls=%async_computation.24 | async-start | bytes 4325376 | tf_op jit(solution)/shard_map/reduce_scatter | solution.py:272
  274.6 540.0 %reduce-scatter.7.cloned.1.call-start = ((), (), s32[]{:S(2)}) async-start(), calls=%async_computation.21 | async-start | bytes 4325376 | tf_op jit(solution)/shard_map/reduce_scatter | solution.py:267
  317.5 7.0 copy-start
  335.0 9.5 copy-start.1
  350.4 7.0 copy-start
  367.9 9.4 copy-start.1
  383.3 7.0 copy-start
  400.8 9.5 copy-start.1
  416.3 7.0 copy-start
  433.8 9.4 copy-start.1
  452.8 33.1 %copy-start.19 = (f32[392]{0:T(512)S(1)}, f32[392]{0:T(512)}, u32[]{:S(2)}) copy-start(f32[392]{0:T(512)} %copy-done.18) | copy-start | bytes 4708
  452.8 33.1 %copy-start.26 = (f32[392]{0:T(512)S(1)}, f32[392]{0:T(512)}, u32[]{:S(2)}) copy-start(f32[392]{0:T(512)} %copy-done.25) | copy-start | bytes 4708
  452.8 33.1 %copy-start.31 = (f32[1024]{0:T(1024)S(1)}, f32[1024]{0:T(1024)}, u32[]{:S(2)}) copy-start(f32[1024]{0:T(1024)} %param.26) | copy-start | bytes 12292
  452.8 33.1 %copy-start.43 = (f32[1024]{0:T(1024)S(1)}, f32[1024]{0:T(1024)}, u32[]{:S(2)}) copy-start(f32[1024]{0:T(1024)} %param.27) | copy-start | bytes 12292
  491.1 323.6 %reduce-scatter.9.cloned.1.call-start = ((), (), s32[]{:S(2)}) async-start(), calls=%async_computation.22 | async-start | bytes 4325376 | tf_op jit(solution)/shard_map/reduce_scatter | solution.py:269
  555.3 396.2 %reduce-scatter.11.cloned.1.call-start = ((), (), s32[]{:S(2)}) async-start(), calls=%async_computation.23 | async-start | bytes 4325376 | tf_op jit(solution)/shard_map/reduce_scatter | solution.py:270
  617.5 700.0 %reduce-scatter.15.cloned.1.call-start = ((), (), s32[]{:S(2)}) async-start(), calls=%async_computation.25 | async-start | bytes 17301504 | tf_op jit(solution)/shard_map/reduce_scatter | solution.py:276
  631.2 1051.2 %reduce-scatter.17.cloned.1.call-start = ((), (), s32[]{:S(2)}) async-start(), calls=%async_computation.26 | async-start | bytes 17301504 | tf_op jit(solution)/shard_map/reduce_scatter | solution.py:278
  680.6 9.3 copy-start.10
  686.0 40.6 %copy-start.3 = (bf16[1,392,1024]{2,1,0:T(8,128)(2,1)S(1)}, bf16[1,392,1024]{2,1,0:T(8,128)(2,1)}, u32[]{:S(2)}) copy-start(bf16[1,392,1024]{2,1,0:T(8,128)(2,1)} %param.24) | copy-start | bytes 2408452
  686.0 40.6 %copy-start.15 = (f32[1024]{0:T(1024)S(1)}, f32[1024]{0:T(1024)}, u32[]{:S(2)}) copy-start(f32[1024]{0:T(1024)} %param.34) | copy-start | bytes 12292
  686.0 37.8 %all-to-all-start.3 = ((bf16[4,2,50176]{2,1,0:T(2,128)(2,1)}), bf16[4,2,50176]{2,1,0:T(2,128)(2,1)S(1)}, u32[]{:S(2)}, u32[]{:S(2)}) async-start(bf16[4,2,50176]{2,1,0:T(2,128)(2,1)} %reshape.298), calls=%async_computation.3 | async-start | bytes 1605632 | tf_op jit(solution)/shard_map/all_to_all | solution.py:97
  729.7 26.4 %copy-start.11 = (bf16[1,4,392,4,64]{2,4,3,1,0:T(8,128)(2,1)S(1)}, bf16[1,4,392,4,64]{2,4,3,1,0:T(8,128)(2,1)}, u32[]{:S(2)}) copy-start(bf16[1,4,392,4,64]{2,4,3,1,0:T(8,128)(2,1)} %copy.69) | copy-start | bytes 2408452
  763.1 48.4 %copy-start.7 = (f32[392,1024]{1,0:T(8,128)S(1)}, f32[392,1024]{1,0:T(8,128)}, u32[]{:S(2)}) copy-start(f32[392,1024]{1,0:T(8,128)} %copy-done.6) | copy-start | bytes 4816900
  (25 other events, 59.1 us)
Sparse Core Ops, SparseCore 0:
  9.9 30.5 all-gather.6
  42.4 27.8 all-gather.8
  72.2 27.8 all-gather.10
  101.9 27.8 all-gather.12
  131.6 54.4 all-gather.14
  187.8 54.3 all-gather.16
  274.7 153.7 reduce-scatter.12
  491.2 155.7 reduce-scatter.6
  649.9 152.2 reduce-scatter.8
  804.8 146.6 reduce-scatter.10
  954.4 363.0 reduce-scatter.14
  1320.2 362.1 reduce-scatter.16
where the time goes:
time: 1700 us; the launch traced here: 1690 us
  waiting for transfers between devices  1060 us (62%)
  matrix products  265 us (16%)
  blocking collectives  141 us (8%)
  local copies, waits for them, and re-layouts  119 us (7%)
  other arithmetic  65.8 us (4%)
  starting transfers between devices  27.3 us (2%)
    reduce_scatter x1, waiting for transfers between devices, on_device(): lax.psum_scatter(all_grads[11], ('fsdp', 'seq'), scatter_dimension=0, til...  366 us
    reduce_scatter x1, waiting for transfers between devices, on_device(): lax.psum_scatter(all_grads[13], ('fsdp', 'seq'), scatter_dimension=0, til...  365 us
    reduce_scatter x1, waiting for transfers between devices, on_device(): lax.psum_scatter(all_grads[5], ('fsdp', 'seq'), scatter_dimension=0, tile...  137 us
    unnamed x118, local copies, waits for them, and re-layouts  58.1 us
    all_to_all x2, waiting for transfers between devices, run_forward(): lax.all_to_all(from_pairs(mixed_pairs, clips), 'seq', split_axis=1, conca...  53.1 us
    convert_element_type x4, other arithmetic, head_backward(): grad_scores = (probs * (grad_probs - inner)).astype(jnp.bfloat16)  41.9 us
    all_to_all x1, blocking collectives, on_device(): lax.all_to_all(from_pairs(grad_k_pairs, clips), 'seq', split_axis=1, conc...  40.8 us
    unnamed x1, blocking collectives  40.2 us
  transfers between devices with their start and end apart: 18, of which 13 were waited for; matrix products, arithmetic and copies ran while one was open for 25% of the time, Pallas kernels for 0%

commit v1 on v0

v1 whole, which is shorter than its diff:
```python
import functools
import math

import jax
import jax.numpy as jnp
from jax import lax
from jax.experimental import pallas as pl
from jax.experimental.pallas import tpu as pltpu
from jax.sharding import PartitionSpec as P

HD = 64
PAIR = 2 * HD
EPSILON = 1e-06
LOG2E = math.log2(math.e)
BF16 = jnp.bfloat16
F32 = jnp.float32
NT = (((1,), (1,)), ((), ()))
NN = (((1,), (0,)), ((), ()))
TN = (((0,), (0,)), ((), ()))


def dot(a, b, dims=NN):
    return lax.dot_general(a, b, dims, preferred_element_type=F32)


def normalize(rows, gain, shift):
    center = rows - jnp.mean(rows, -1, keepdims=True)
    inverse = lax.rsqrt(jnp.mean(center * center, -1, keepdims=True) + EPSILON)
    normed = center * inverse
    return (normed * gain + shift, normed, inverse)


def norm_grad(grad, normed, inverse, gain):
    scaled = grad * gain
    inner = (
        scaled
        - jnp.mean(scaled, -1, keepdims=True)
        - normed * jnp.mean(scaled * normed, -1, keepdims=True)
    )
    return inner * inverse


def forward_kernel(scale, q_ref, k_ref, v_ref, mixed_ref, exact_ref, lse_ref, value_sc):
    @pl.when(pl.program_id(1) == 0)
    def _():
        value_sc[:, :PAIR] = v_ref[...]
        value_sc[:, PAIR:] = jnp.ones((value_sc.shape[0], PAIR), value_sc.dtype)

    query = q_ref[...]
    keys = k_ref[...]
    first = lax.broadcasted_iota(jnp.int32, query.shape, 1) < HD
    outs, sums = [], []
    for head in range(2):
        mine = first if head == 0 else jnp.logical_not(first)
        scores = dot(jnp.where(mine, query, jnp.zeros_like(query)), keys, NT)
        peak = jnp.max(scores, -1, keepdims=True)
        expo = jnp.exp2((scores - peak) * scale).astype(BF16)
        both = dot(expo, value_sc[...])
        total = both[:, PAIR:]
        outs.append(both[:, :PAIR] / total)
        sums.append(peak * scale + jnp.log2(total[:, :1]))
    exact = jnp.where(first, outs[0], outs[1])
    exact_ref[...] = exact
    mixed_ref[...] = exact.astype(BF16)
    lse_ref[...] = jnp.concatenate(sums, 1)


def attention_forward(qkv, rows):
    length, width = qkv.shape[0], qkv.shape[1] // 3
    pairs = width // PAIR
    return pl.pallas_call(
        functools.partial(forward_kernel, HD**-0.5 * LOG2E),
        grid=(pairs, length // rows),
        in_specs=[
            pl.BlockSpec((rows, PAIR), lambda p, i: (i, p)),
            pl.BlockSpec((length, PAIR), lambda p, i: (0, pairs + p)),
            pl.BlockSpec((length, PAIR), lambda p, i: (0, 2 * pairs + p)),
        ],
        out_specs=[
            pl.BlockSpec((rows, PAIR), lambda p, i: (i, p)),
            pl.BlockSpec((rows, PAIR), lambda p, i: (i, p)),
            pl.BlockSpec((None, rows, 2), lambda p, i: (p, i, 0)),
        ],
        out_shape=[
            jax.ShapeDtypeStruct((length, width), BF16),
            jax.ShapeDtypeStruct((length, width), F32),
            jax.ShapeDtypeStruct((pairs, length, 2), F32),
        ],
        scratch_shapes=[pltpu.VMEM((length, 2 * PAIR), BF16)],
        compiler_params=pltpu.CompilerParams(vmem_limit_bytes=48 << 20),
        cost_estimate=pl.CostEstimate(
            flops=16 * length * length * width,
            transcendentals=length * length * width // HD,
            bytes_accessed=14 * length * width,
        ),
        name="attention_forward",
    )(qkv, qkv, qkv)


def backward_kernel(
    scale, q_ref, k_ref, v_ref, do_ref, exact_ref, lse_ref, dq_ref, dk_ref, dv_ref, dk_sc, dv_sc
):
    step = pl.program_id(1)

    @pl.when(step == 0)
    def _():
        dk_sc[...] = jnp.zeros_like(dk_sc)
        dv_sc[...] = jnp.zeros_like(dv_sc)

    query, keys, values, grad = q_ref[...], k_ref[...], v_ref[...], do_ref[...]
    first = lax.broadcasted_iota(jnp.int32, query.shape, 1) < HD
    product = grad.astype(F32) * exact_ref[...]
    dqs = []
    for head in range(2):
        mine = first if head == 0 else jnp.logical_not(first)
        zero = jnp.zeros_like(query)
        q_one = jnp.where(mine, query, zero)
        g_one = jnp.where(mine, grad, zero)
        inner = jnp.sum(jnp.where(mine, product, 0.0), -1, keepdims=True)
        probs = jnp.exp2(dot(q_one, keys, NT) * (scale * LOG2E) - lse_ref[:, head : head + 1])
        grad_scores = (probs * (dot(g_one, values, NT) - inner)).astype(BF16)
        dqs.append(dot(grad_scores, keys))
        dv_sc[...] += dot(g_one, probs.astype(BF16), TN)
        dk_sc[...] += dot(q_one, grad_scores, TN)
    dq_ref[...] = (jnp.where(first, dqs[0], dqs[1]) * scale).astype(BF16)

    @pl.when(step == pl.num_programs(1) - 1)
    def _():
        dk_ref[...] = (dk_sc[...] * scale).T.astype(BF16)
        dv_ref[...] = dv_sc[...].T.astype(BF16)


def attention_backward(qkv, grad, exact, lse, rows):
    length, width = qkv.shape[0], qkv.shape[1] // 3
    pairs = width // PAIR
    row = pl.BlockSpec((rows, PAIR), lambda p, i: (i, p))
    full = pl.BlockSpec((length, PAIR), lambda p, i: (0, p))
    return pl.pallas_call(
        functools.partial(backward_kernel, HD**-0.5),
        grid=(pairs, length // rows),
        in_specs=[
            row,
            pl.BlockSpec((length, PAIR), lambda p, i: (0, pairs + p)),
            pl.BlockSpec((length, PAIR), lambda p, i: (0, 2 * pairs + p)),
            row,
            row,
            pl.BlockSpec((None, rows, 2), lambda p, i: (p, i, 0)),
        ],
        out_specs=[row, full, full],
        out_shape=[jax.ShapeDtypeStruct((length, width), BF16)] * 3,
        scratch_shapes=[pltpu.VMEM((PAIR, length), F32)] * 2,
        compiler_params=pltpu.CompilerParams(vmem_limit_bytes=48 << 20),
        cost_estimate=pl.CostEstimate(
            flops=40 * length * length * width,
            transcendentals=length * length * width // HD,
            bytes_accessed=18 * length * width,
        ),
        name="attention_backward",
    )(qkv, qkv, qkv, grad, exact, lse)


def flip(array, bit, size):
    return lax.ppermute(array, "fsdp", [(i, i ^ (1 << bit)) for i in range(size)])


def shift(array, by, size):
    return lax.ppermute(array, "seq", [(i, (i + by) % size) for i in range(size)])


def gather_rows(shard, size):
    if size != 8:
        return lax.all_gather(shard, "fsdp", axis=0, tiled=True)
    half = shard.shape[0] // 2
    one, two = flip(shard, 1, size), flip(shard, 2, size)
    top, low = flip(one[:half], 2, size), flip(two[half:], 1, size)
    pieces = [shard, one, two, top, low]
    other = [flip(piece, 0, size) for piece in pieces]
    me = lax.axis_index("fsdp")
    rows, columns = shard.shape
    whole = jnp.zeros((size * rows, columns), shard.dtype)
    for near, group in enumerate((pieces, other)):
        for far, start, piece in zip((0, 2, 4, 6, 6), (0, 0, 0, 0, half), group):
            place = (me ^ (far + near)) * rows + start
            whole = lax.dynamic_update_slice(whole, piece, (place, 0))
    return whole


def reduce_rows(left, right, size):
    tokens, height = left.shape
    bits = size.bit_length() - 1
    me = lax.axis_index("fsdp")
    rest = height // size
    split = left.reshape(tokens, size // 2, 2, rest)

    def half_of(which):
        return lax.dynamic_index_in_dim(split, which, 2, False).reshape(tokens, height // 2)

    mine = me & 1
    away = dot(half_of(1 - mine), right, TN).astype(BF16)
    arrived = flip(away, 0, size)
    kept = dot(half_of(mine), right, TN)
    block = (kept + arrived.astype(F32)).astype(BF16)
    columns = right.shape[1]
    block = block.reshape((2,) * (bits - 1) + (rest, columns))
    order = list(range(1, bits))
    parts = []
    for part, way in ((block[..., : columns // 2], order), (block[..., columns // 2 :], order[::-1])):
        left_over = list(range(bits - 1, 0, -1))
        for bit in way:
            axis = left_over.index(bit)
            left_over.remove(bit)
            mine = (me >> bit) & 1
            away = lax.dynamic_index_in_dim(part, 1 - mine, axis, False)
            kept = lax.dynamic_index_in_dim(part, mine, axis, False)
            arrived = flip(away, bit, size)
            part = (kept.astype(F32) + arrived.astype(F32)).astype(BF16)
        parts.append(part)
    return jnp.concatenate(parts, 1)


def reduce_seq(block, size):
    me = lax.axis_index("seq")
    parts = block.reshape(size, block.shape[0] // size, block.shape[1])
    total = lax.dynamic_index_in_dim(parts, me, 0, False).astype(F32)
    for by in range(1, size):
        away = lax.dynamic_index_in_dim(parts, (me + by) % size, 0, False)
        total = total + shift(away, by, size).astype(F32)
    return total


def swap_seq(pieces, size):
    me = lax.axis_index("seq")
    came = [pieces[0]] + [shift(pieces[by], by, size) for by in range(1, size)]
    came = came[::-1]
    return lax.dynamic_slice_in_dim(jnp.stack(came + came), (size - 1 - me) % size, size, 0)


def reduce_vectors(vectors, fsdp, seq):
    me = lax.axis_index("fsdp")
    bits = fsdp.bit_length() - 1
    sizes = [v.shape[0] // (fsdp * seq) for v in vectors]
    block = jnp.concatenate([v.reshape(fsdp, seq, -1) for v in vectors], 2)
    block = block.reshape((2,) * bits + (seq, sum(sizes)))
    for bit in range(bits):
        axis = bits - 1 - bit
        mine = (me >> bit) & 1
        away = lax.dynamic_index_in_dim(block, 1 - mine, axis, False)
        block = lax.dynamic_index_in_dim(block, mine, axis, False) + flip(away, bit, fsdp)
    total = reduce_seq(block, seq)[0]
    return jnp.split(total, [sum(sizes[: i + 1]) for i in range(len(sizes) - 1)])


def on_device(
    fsdp,
    seq,
    inputs,
    clip_mask,
    ln1_gain,
    ln1_bias,
    w_query,
    b_query,
    w_key,
    w_value,
    b_value,
    w_out,
    b_out,
    ln2_gain,
    ln2_bias,
    w_fc1,
    b_fc1,
    w_fc2,
    b_fc2,
    cotangent,
):
    clips, local, width = inputs.shape
    assert clips == 1
    me = lax.axis_index("seq")
    own = width // seq
    present = clip_mask[0].astype(F32)

    def columns(array, axis):
        return lax.dynamic_slice_in_dim(array, me * own, own, axis)

    w_heads = gather_rows(
        jnp.concatenate([columns(w, 1) for w in (w_query, w_key, w_value)], 1), fsdp
    )
    b_heads = jnp.concatenate([columns(b_query, 0), jnp.zeros((own,), F32), columns(b_value, 0)])

    tokens = [inputs[0]] + [shift(inputs[0], -by, seq) for by in range(1, seq)]
    first_parts, qkv_parts = [], []
    for part in tokens:
        normed, _, _ = normalize(part.astype(F32), ln1_gain, ln1_bias)
        first_parts.append(normed.astype(BF16))
        qkv_parts.append((dot(first_parts[-1], w_heads) + b_heads).astype(BF16))
    first_in = jnp.concatenate(first_parts, 0)
    qkv = jnp.concatenate(qkv_parts, 0)
    mixed, exact, lse = attention_forward(qkv, 2 * local)

    full_out = gather_rows(w_out, fsdp)
    full_fc1 = gather_rows(w_fc1, fsdp)
    full_fc2 = gather_rows(w_fc2, fsdp)

    attended = swap_seq([mixed[j * local : (j + 1) * local] for j in range(seq)], seq)
    attended = attended.transpose(1, 0, 2).reshape(local, width)
    rows = inputs[0].astype(F32)
    middle = rows + dot(attended, full_out) + b_out
    normed2, hat2, inv2 = normalize(middle, ln2_gain, ln2_bias)
    second_in = normed2.astype(BF16)
    hidden = dot(second_in, full_fc1) + b_fc1
    cdf = 0.5 * (1.0 + lax.erf(hidden * (0.5**0.5)))
    activ = (hidden * cdf).astype(BF16)
    slope = cdf + hidden * jnp.exp(-0.5 * hidden * hidden) * ((2.0 * math.pi) ** -0.5)
    output = ((middle + dot(activ, full_fc2) + b_fc2) * present).astype(BF16)

    grad_rows = cotangent[0].astype(F32) * present
    grad_low = grad_rows.astype(BF16)
    part_fc2 = reduce_rows(activ, grad_low, fsdp)
    grad_hidden = (dot(grad_low, full_fc2, NT) * slope).astype(BF16)
    part_fc1 = reduce_rows(second_in, grad_hidden, fsdp)
    grad_second = dot(grad_hidden, full_fc1, NT)
    grad_middle = grad_rows + norm_grad(grad_second, hat2, inv2, ln2_gain)
    grad_branch = grad_middle.astype(BF16)
    grad_mixed = dot(grad_branch, full_out, NT).astype(BF16)

    grad_parts = [columns(grad_mixed, 1)]
    for by in range(1, seq):
        theirs = lax.dynamic_slice_in_dim(grad_mixed, ((me - by) % seq) * own, own, 1)
        grad_parts.append(shift(theirs, -by, seq))
    part_out = reduce_rows(attended, grad_branch, fsdp)
    dq, dk, dv = attention_backward(qkv, jnp.concatenate(grad_parts, 0), exact, lse, 2 * local)
    dqkv = jnp.concatenate([dq, dk, dv], 1)

    full_query = gather_rows(w_query, fsdp)
    full_key = gather_rows(w_key, fsdp)
    full_value = gather_rows(w_value, fsdp)
    back = swap_seq([dqkv[j * local : (j + 1) * local] for j in range(seq)], seq)
    back = back.reshape(seq, local, 3, own).transpose(2, 1, 0, 3).reshape(3, local, width)
    grad_first = (
        dot(back[0], full_query, NT) + dot(back[1], full_key, NT) + dot(back[2], full_value, NT)
    )
    _, hat1, inv1 = normalize(rows, ln1_gain, ln1_bias)
    grad_inputs = grad_middle + norm_grad(grad_first, hat1, inv1, ln1_gain)

    part_heads = reduce_rows(first_in, dqkv, fsdp)
    strip = part_heads.shape[0] // seq
    sent = [
        lax.dynamic_slice_in_dim(part_heads, ((me + j) % seq) * strip, strip, 0)
        for j in range(seq)
    ]
    heads = swap_seq(sent, seq).astype(F32)
    heads = heads.reshape(seq, strip, 3, own).transpose(2, 1, 0, 3).reshape(3, strip, width)

    def spread(vector):
        return lax.dynamic_update_slice(jnp.zeros((width,), F32), vector, (me * own,))

    sums = reduce_vectors(
        [
            jnp.sum(grad_first * hat1, 0),
            jnp.sum(grad_first, 0),
            spread(jnp.sum(dq.astype(F32), 0)),
            spread(jnp.sum(dv.astype(F32), 0)),
            jnp.sum(grad_branch.astype(F32), 0),
            jnp.sum(grad_second * hat2, 0),
            jnp.sum(grad_second, 0),
            jnp.sum(grad_hidden.astype(F32), 0),
            jnp.sum(grad_rows, 0),
        ],
        fsdp,
        seq,
    )
    return (
        output[None],
        grad_inputs[None],
        sums[0],
        sums[1],
        heads[0],
        sums[2],
        heads[1],
        heads[2],
        sums[3],
        reduce_seq(part_out, seq),
        sums[4],
        sums[5],
        sums[6],
        reduce_seq(part_fc1, seq),
        sums[7],
        reduce_seq(part_fc2, seq),
        sums[8],
    )


def solution(mesh):
    rows, both = P("fsdp", None), P(("fsdp", "seq"))
    tokens = P("fsdp", "seq", None)
    matrix = P(("fsdp", "seq"), None)
    return jax.shard_map(
        functools.partial(on_device, mesh.shape["fsdp"], mesh.shape["seq"]),
        mesh=mesh,
        in_specs=(
            tokens,
            P("fsdp"),
            P(),
            P(),
            rows,
            P(),
            rows,
            rows,
            P(),
            rows,
            P(),
            P(),
            P(),
            rows,
            P(),
            rows,
            P(),
            tokens,
        ),
        out_specs=(
            tokens,
            tokens,
            both,
            both,
            matrix,
            both,
            matrix,
            matrix,
            both,
            matrix,
            both,
            both,
            both,
            matrix,
            both,
            matrix,
            both,
        ),
        check_vma=False,
    )
```

time: 1700 us -> 687 us (0.40)
  waiting for transfers between devices: 1060 us -> 198 us
  matrix products: 265 us -> 82.5 us
  blocking collectives: 141 us -> 0 us
  local copies, waits for them, and re-layouts: 119 us -> 223 us
  starting transfers between devices: 27.3 us -> 102 us
  Pallas kernels: 0 us -> 50.7 us
  other arithmetic: 65.8 us -> 19 us
    reduce_scatter x6 -> x0, waiting for transfers between devices: 868 us -> none  [the longest x1 366 us: on_device(): lax.psum_scatter(all_grads[11], ('fsdp', 'seq'), scatter_dimension=0, til...]
    ppermute x0 -> x113, waiting for transfers between devices: none -> 198 us  [the longest x86 107 us: flip(): return lax.ppermute(array, 'fsdp', [(i, i ^ 1 << bit) for i in range(size)])]
    dot_general x55 -> x21, matrix products: 265 us -> 82.5 us  [dot(): return lax.dot_general(a, b, dims, preferred_element_type=F32)]
    all_to_all x6 -> x0, waiting for transfers between devices: 112 us -> none  [the longest x2 53.1 us: run_forward(): lax.all_to_all(from_pairs(mixed_pairs, clips), 'seq', split_axis=1, conca...]
    ppermute x0 -> x113, starting transfers between devices: none -> 102 us  [the longest x86 58.6 us: flip(): return lax.ppermute(array, 'fsdp', [(i, i ^ 1 << bit) for i in range(size)])]
    all_to_all x3 -> x0, blocking collectives: 101 us -> none  [the longest x1 40.8 us: on_device(): lax.all_to_all(from_pairs(grad_k_pairs, clips), 'seq', split_axis=1, conc...]
    all_gather x6 -> x0, waiting for transfers between devices: 73.2 us -> none  [the longest x1 27.1 us: on_device(): lax.all_gather(w_query, 'fsdp', axis=0, tiled=True)]
    dynamic_update_slice x4 -> x71, local copies, waits for them, and re-layouts: 0.41 us -> 67.8 us  [the longest x69 66.9 us: gather_rows(): whole = lax.dynamic_update_slice(whole, piece, (place, 0))]
  transfers between devices with their start and end apart: 18 -> 113, of which waited for: 13 -> 40; matrix products, arithmetic and copies ran while one was open for 25% -> 42% of each run, Pallas kernels for 0% -> 7%
where the time goes in v1:
time: 687 us; the launch traced here: 678 us
  local copies, waits for them, and re-layouts  223 us (32%)
  waiting for transfers between devices  198 us (29%)
  starting transfers between devices  102 us (15%)
  matrix products  82.5 us (12%)
  Pallas kernels  50.7 us (7%)
  other arithmetic  19 us (3%)
    ppermute x86, waiting for transfers between devices, flip(): return lax.ppermute(array, 'fsdp', [(i, i ^ 1 << bit) for i in range(size)])  107 us
    ppermute x27, waiting for transfers between devices, shift(): lax.ppermute(array, 'seq', [(i, (i + by) % size) for i in range(size)])  91.2 us
    dot_general x21, matrix products, dot(): return lax.dot_general(a, b, dims, preferred_element_type=F32)  82.5 us
    dynamic_update_slice x69, local copies, waits for them, and re-layouts, gather_rows(): whole = lax.dynamic_update_slice(whole, piece, (place, 0))  66.9 us
    ppermute x86, starting transfers between devices, flip(): return lax.ppermute(array, 'fsdp', [(i, i ^ 1 << bit) for i in range(size)])  58.6 us
    dynamic_slice x4, local copies, waits for them, and re-layouts, half_of(): lax.dynamic_index_in_dim(split, which, 2, False)  54.8 us
    ppermute x27, starting transfers between devices, shift(): lax.ppermute(array, 'seq', [(i, (i + by) % size) for i in range(size)])  43.1 us
    unnamed x126, local copies, waits for them, and re-layouts  31.8 us
  transfers between devices with their start and end apart: 113, of which 40 were waited for; matrix products, arithmetic and copies ran while one was open for 42% of the time, Pallas kernels for 7%

profile of v1, /device:TPU:0, one launch (start us, length us, event | category | flops | bytes accessed | tf_op | source)
XLA Modules:
  0.0 678.1 jit_solution(14405241033036372503)
XLA Ops:
  5.3 2.9 collective-permute-start
  24.0 4.4 broadcast_in_dim.14
  31.0 4.4 broadcast_in_dim.15
  50.5 3.6 collective-permute-start.9
  63.4 3.2 collective-permute-done.2
  67.7 3.4 collective-permute-done.3
  84.1 2.8 collective-permute-done.59
  94.1 2.8 collective-permute-done.68
  98.6 3.3 collective-permute-done.69
  125.3 9.0 %collective-permute-done.11 = bf16[392,1024]{1,0:T(8,128)(2,1)S(1)} collective-permute-done((bf16[392,1024]{1,0:T(8,128)(2,1)S(1)}, bf16[392,1024]{1,0:T(8,128)(2,1)S(1)}, u32[]{:S(2)}, u32[]{:S(2)}) %collective-permute-start.11) | collective-permute-done | bytes 802848 | tf_op jit(solution)/shard_map/ppermute | solution.py:167
  148.7 20.6 %attention_forward.1 = (bf16[1568,256]{1,0:T(8,128)(2,1)S(1)}, f32[1568,256]{1,0:T(8,128)S(1)}, f32[2,1568,2]{2,1,0:T(8,128)S(1)}) custom-call(bf16[1568,768]{1,0:T(8,128)(2,1)} %pad_maximum_fusion.1.q_ref.k_ref.v_ref, bf16[1568,768]{1,0:T(8,128)(2,1)} %pad_maximum_fusion.1.q_ref.k_ref.v_ref, bf16[1568,768]{1,0:T(8,128)(2,1)} %pad_maximum_fusion.1.q_ref.k_ref.v_ref), custom_call_target="tpu_custom_call" | custom-call | flops 10070523904 | bytes 5619712 | tf_op jit(solution)/shard_map/attention_forward/pallas_call | solution.py:71
  171.6 8.4 %reshape.296 = bf16[1568,4,2,128]{3,2,1,0:T(2,128)(2,1)} reshape(bf16[1568,1024]{1,0:T(8,128)(2,1)} %pad_maximum_fusion) | data formatting | bytes 6422528 | tf_op jit(solution)/shard_map/reshape | solution.py:193
  180.0 10.2 %constant_dynamic-slice_fusion.2 = (bf16[1568,4,1,128]{3,2,1,0:T(2,128)(2,1)}, bf16[1568,4,1,128]{3,2,1,0:T(2,128)(2,1)}) fusion(bf16[1568,4,2,128]{3,2,1,0:T(2,128)(2,1)} %reshape.296, s32[]{:T(128)S(6)} %select_n.360, s32[]{:T(128)S(6)} %select_n.359), kind=kLoop, calls=%fused_computation.224 | loop fusion | bytes 6422536 | tf_op jit(solution)/shard_map/jit(dynamic_index_in_dim)/dynamic_slice | solution.py:196
  190.1 8.5 %copy.74 = bf16[1568,4,1,128]{0,3,1,2:T(8,128)(2,1)} copy(bf16[1568,4,1,128]{3,2,1,0:T(2,128)(2,1)} %get-tuple-element.49) | data formatting | bytes 3211264
  198.6 8.5 %copy.73 = bf16[1568,4,1,128]{0,3,1,2:T(8,128)(2,1)} copy(bf16[1568,4,1,128]{3,2,1,0:T(2,128)(2,1)} %get-tuple-element.50) | data formatting | bytes 3211264
  207.4 11.4 %collective-permute-done.13 = bf16[392,256]{1,0:T(8,128)(2,1)S(1)} collective-permute-done((bf16[392,256]{1,0:T(8,128)(2,1)S(1)}, bf16[392,256]{1,0:T(8,128)(2,1)S(1)}, u32[]{:S(2)}, u32[]{:S(2)}) %collective-permute-start.13) | collective-permute-done | bytes 200736 | tf_op jit(solution)/shard_map/ppermute | solution.py:167
  218.9 8.5 %collective-permute-done.14 = bf16[392,256]{1,0:T(8,128)(2,1)S(1)} collective-permute-done((bf16[392,256]{1,0:T(8,128)(2,1)S(1)}, bf16[392,256]{1,0:T(8,128)(2,1)S(1)}, u32[]{:S(2)}, u32[]{:S(2)}) %collective-permute-start.14) | collective-permute-done | bytes 200736 | tf_op jit(solution)/shard_map/ppermute | solution.py:167
  237.4 3.5 reshape.305
  240.8 7.3 %dynamic-slice_reduce_fusion.3 = (bf16[392,4,128]{2,1,0:T(4,128)(2,1)}, bf16[392,4,128]{2,1,0:T(4,128)(2,1)}) fusion(bf16[392,4,2,128]{3,2,1,0:T(2,128)(2,1)} %reshape.305, s32[]{:T(128)S(6)} %select_n.359, s32[]{:T(128)S(6)} %select_n.360), kind=kLoop, calls=%fused_computation.117 | loop fusion | bytes 1605640 | tf_op jit(solution)/shard_map/jit(dynamic_index_in_dim)/dynamic_slice | solution.py:196
  264.3 10.6 %collective-permute-done.35 = bf16[256,1024]{1,0:T(8,128)(2,1)} collective-permute-done((bf16[256,1024]{1,0:T(8,128)(2,1)S(1)}, bf16[256,1024]{1,0:T(8,128)(2,1)}, u32[]{:S(2)}, u32[]{:S(2)}) %collective-permute-start.35) | collective-permute-done | bytes 524320 | tf_op jit(solution)/shard_map/ppermute | solution.py:163
  280.6 7.9 %collective-permute-done.27 = bf16[64,4096]{1,0:T(8,128)(2,1)S(1)} collective-permute-done((bf16[64,4096]{1,0:T(8,128)(2,1)S(1)}, bf16[64,4096]{1,0:T(8,128)(2,1)S(1)}, u32[]{:S(2)}, u32[]{:S(2)}) %collective-permute-start.27) | collective-permute-done | bytes 524320 | tf_op jit(solution)/shard_map/ppermute | solution.py:163
  298.1 8.7 %multiply_convert_fusion = (bf16[392,4096]{1,0:T(8,128)(2,1)}, f32[392,4096]{1,0:T(8,128)}) fusion(f32[4096]{0:T(1024)S(1)} %copy-done.41, bf16[392,1024]{1,0:T(8,128)(2,1)S(1)} %copy-done.14, bf16[1024,4096]{1,0:T(8,128)(2,1)} %constant_dynamic-update-slice_fusion.51), kind=kOutput, calls=%fused_computation.10 | convolution fusion | flops 3297968128 | bytes 18841600 | tf_op jit(solution)/shard_map/dot_general | solution.py:23
  306.8 8.8 %reshape.310 = bf16[392,4,2,512]{3,2,1,0:T(2,128)(2,1)} reshape(bf16[392,4096]{1,0:T(8,128)(2,1)} %get-tuple-element.106) | data formatting | bytes 6422528 | tf_op jit(solution)/shard_map/reshape | solution.py:193
  324.1 7.8 %fusion.50 = bf16[1,392,1024]{2,1,0:T(8,128)(2,1)} fusion(f32[392,1024]{1,0:T(8,128)S(1)} %get-tuple-element.105, bf16[392,4096]{1,0:T(8,128)(2,1)S(1)} %copy-done.13, bf16[4096,1024]{1,0:T(8,128)(2,1)} %constant_dynamic-update-slice_fusion.41, f32[]{:T(128)} %bitcast.6, f32[1024]{0:T(1024)S(1)} %copy-done.43), kind=kOutput, calls=%fused_computation.99 | convolution fusion | flops 3289939968 | bytes 14012420 | tf_op jit(solution)/shard_map/dot_general | solution.py:23
  331.9 8.7 %convert_reduce_fusion = (f32[4096]{0:T(1024)S(1)}, bf16[392,4096]{1,0:T(8,128)(2,1)S(1)}) fusion(f32[392,4096]{1,0:T(8,128)} %get-tuple-element.107, f32[4096]{0:T(1024)S(1)} %copy-done.41, bf16[4096,1024]{1,0:T(8,128)(2,1)} %constant_dynamic-update-slice_fusion.41, bf16[1,392,1024]{2,1,0:T(8,128)(2,1)S(1)} %copy-done.11, f32[]{:T(128)} %bitcast.6), kind=kOutput, calls=%fused_computation.9 | convolution fusion | flops 3310407680 | bytes 18857988 | tf_op jit(solution)/shard_map/dot_general | solution.py:23
  340.6 7.8 %multiply_reduce_fusion = (f32[1024]{0:T(1024)S(1)}, f32[392]{0:T(512)S(1)}, f32[392]{0:T(512)S(1)}, f32[1024]{0:T(1024)S(1)}, f32[392,1024]{1,0:T(8,128)S(1)}) fusion(f32[392,1024]{1,0:T(8,128)S(1)} %get-tuple-element.105, f32[392]{0:T(512)S(1)} %add_rsqrt_fusion, f32[392]{0:T(512)S(1)} %broadcast_multiply_fusion.4, f32[1024]{0:T(1024)S(1)} %copy-done.36, ...), kind=kOutput, calls=%fused_computation.72 | convolution fusion | flops 3291943936 | bytes 14829696 | tf_op jit(solution)/shard_map/dot_general | solution.py:23
  350.4 3.0 convolution_convert_fusion.3
  353.7 3.8 collective-permute-start.42
  359.3 35.8 %dynamic-slice_reduce_fusion.1 = (bf16[392,4,512]{2,1,0:T(4,128)(2,1)}, bf16[392,4,512]{2,1,0:T(4,128)(2,1)S(1)}) fusion(bf16[392,4,2,512]{3,2,1,0:T(2,128)(2,1)S(1)} %copy-done.1, s32[]{:T(128)S(6)} %select_n.359, s32[]{:T(128)S(6)} %select_n.360), kind=kLoop, calls=%fused_computation.16 | loop fusion | bytes 6422536 | tf_op jit(solution)/shard_map/jit(dynamic_index_in_dim)/dynamic_slice | solution.py:196
  395.0 4.5 convolution_convert_fusion
  400.1 30.1 %attention_backward.1 = (bf16[1568,256]{1,0:T(8,128)(2,1)S(1)}, bf16[1568,256]{1,0:T(8,128)(2,1)S(1)}, bf16[1568,256]{1,0:T(8,128)(2,1)S(1)}) custom-call(bf16[1568,768]{1,0:T(8,128)(2,1)} %pad_maximum_fusion.1.q_ref.k_ref.v_ref, bf16[1568,768]{1,0:T(8,128)(2,1)} %pad_maximum_fusion.1.q_ref.k_ref.v_ref, ...), custom_call_target="tpu_custom_call" | custom-call | flops 25176309760 | bytes 7225344 | tf_op jit(solution)/shard_map/attention_backward/pallas_call | solution.py:138
  433.8 4.4 convolution_convert_fusion.1
  443.7 4.3 collective-permute-done.45
  449.1 37.9 %collective-permute-done.46 = bf16[392,768]{1,0:T(8,128)(2,1)} collective-permute-done((bf16[392,768]{1,0:T(8,128)(2,1)}, bf16[392,768]{1,0:T(8,128)(2,1)}, u32[]{:S(2)}, u32[]{:S(2)}) %collective-permute-start.46) | collective-permute-done | bytes 602144 | tf_op jit(solution)/shard_map/ppermute | solution.py:167
  494.3 6.2 reshape.295
  500.5 3.4 fusion.111
  515.1 3.2 convolution_convert_fusion.4
  519.4 3.2 collective-permute-done.76
  545.2 4.3 collective-permute-done.83
  551.0 3.1 collective-permute-done.85
  575.6 4.7 add_convert_fusion.1
  584.0 4.6 add_convert_fusion
  590.6 16.5 %collective-permute-done.100 = bf16[2,128,2048]{2,1,0:T(8,128)(2,1)S(1)} collective-permute-done((bf16[2,128,2048]{2,1,0:T(8,128)(2,1)S(1)}, bf16[2,128,2048]{2,1,0:T(8,128)(2,1)S(1)}, u32[]{:S(2)}, u32[]{:S(2)}) %collective-permute-start.100) | collective-permute-done | bytes 1048608 | tf_op jit(solution)/shard_map/ppermute | solution.py:163
  611.0 18.7 %collective-permute-done.108 = bf16[2,512,512]{2,1,0:T(8,128)(2,1)S(1)} collective-permute-done((bf16[2,512,512]{2,1,0:T(8,128)(2,1)S(1)}, bf16[2,512,512]{2,1,0:T(8,128)(2,1)S(1)}, u32[]{:S(2)}, u32[]{:S(2)}) %collective-permute-start.108) | collective-permute-done | bytes 1048608 | tf_op jit(solution)/shard_map/ppermute | solution.py:163
  633.3 7.7 %collective-permute-done.101 = bf16[128,2048]{1,0:T(8,128)(2,1)S(1)} collective-permute-done((bf16[128,2048]{1,0:T(8,128)(2,1)S(1)}, bf16[128,2048]{1,0:T(8,128)(2,1)S(1)}, u32[]{:S(2)}, u32[]{:S(2)}) %collective-permute-start.101) | collective-permute-done | bytes 524320 | tf_op jit(solution)/shard_map/ppermute | solution.py:163
  649.6 12.9 %collective-permute-start.110 = (bf16[128,1024]{1,0:T(8,128)(2,1)S(1)}, bf16[128,1024]{1,0:T(8,128)(2,1)S(1)}, u32[]{:S(2)}, u32[]{:S(2)}) collective-permute-start(bf16[128,1024]{1,0:T(8,128)(2,1)S(1)} %get-tuple-element.59), channel_id=1, source_target_pairs={{0,1},{1,2},{2,3},{3,0},{4,5},{5,6},{6,7},{7,4},{8,9},{9,10},{10,1... | collective-permute-start | bytes 786440 | tf_op jit(solution)/shard_map/ppermute | solution.py:167
  662.5 8.8 %collective-permute-done.103 = bf16[32,4096]{1,0:T(8,128)(2,1)S(1)} collective-permute-done((bf16[32,4096]{1,0:T(8,128)(2,1)S(1)}, bf16[32,4096]{1,0:T(8,128)(2,1)S(1)}, u32[]{:S(2)}, u32[]{:S(2)}) %collective-permute-start.103) | collective-permute-done | bytes 262176 | tf_op jit(solution)/shard_map/ppermute | solution.py:167
  672.3 4.7 collective-permute-done.111
  (556 shorter events, 262.0 us)
Async XLA Ops:
  5.3 33.6 %collective-permute-start = (bf16[128,768]{1,0:T(8,128)(2,1)}, bf16[128,768]{1,0:T(8,128)(2,1)}, u32[]{:S(2)}, u32[]{:S(2)}) collective-permute-start(bf16[128,768]{1,0:T(8,128)(2,1)} %get-tuple-element.87), channel_id=1, source_target_pairs={{0,8},{4,12},{8,0},{12,4},{16,24},{20,28},{24,16},{28,20},{1,9},{5... | collective-permute-start | bytes 589832 | tf_op jit(solution)/shard_map/ppermute | solution.py:163
  8.2 33.7 %collective-permute-start.1 = (bf16[128,768]{1,0:T(8,128)(2,1)}, bf16[128,768]{1,0:T(8,128)(2,1)}, u32[]{:S(2)}, u32[]{:S(2)}) collective-permute-start(bf16[128,768]{1,0:T(8,128)(2,1)} %get-tuple-element.87), channel_id=1, source_target_pairs={{0,16},{4,20},{8,24},{12,28},{16,0},{20,4},{24,8},{28,12},{1,17},{... | collective-permute-start | bytes 589832 | tf_op jit(solution)/shard_map/ppermute | solution.py:163
  9.8 36.2 %collective-permute-start.15 = (bf16[128,1024]{1,0:T(8,128)(2,1)}, bf16[128,1024]{1,0:T(8,128)(2,1)}, u32[]{:S(2)}, u32[]{:S(2)}) collective-permute-start(bf16[128,1024]{1,0:T(8,128)(2,1)} %param.27), channel_id=1, source_target_pairs={{0,8},{4,12},{8,0},{12,4},{16,24},{20,28},{24,16},{28,20},{1,9},{5... | collective-permute-start | bytes 786440 | tf_op jit(solution)/shard_map/ppermute | solution.py:163
  10.3 37.5 %collective-permute-start.16 = (bf16[128,1024]{1,0:T(8,128)(2,1)}, bf16[128,1024]{1,0:T(8,128)(2,1)S(1)}, u32[]{:S(2)}, u32[]{:S(2)}) collective-permute-start(bf16[128,1024]{1,0:T(8,128)(2,1)} %param.27), channel_id=1, source_target_pairs={{0,16},{4,20},{8,24},{12,28},{16,0},{20,4},{24,8},{28,12},{1,17},{... | collective-permute-start | bytes 786440 | tf_op jit(solution)/shard_map/ppermute | solution.py:163
  10.3 40.2 %collective-permute-start.48 = (bf16[128,1024]{1,0:T(8,128)(2,1)}, bf16[128,1024]{1,0:T(8,128)(2,1)S(1)}, u32[]{:S(2)}, u32[]{:S(2)}) collective-permute-start(bf16[128,1024]{1,0:T(8,128)(2,1)} %param.22), channel_id=1, source_target_pairs={{0,8},{4,12},{8,0},{12,4},{16,24},{20,28},{24,16},{28,20},{1,9},{5... | collective-permute-start | bytes 786440 | tf_op jit(solution)/shard_map/ppermute | solution.py:163
  38.9 15.9 %collective-permute-start.49 = (bf16[128,1024]{1,0:T(8,128)(2,1)}, bf16[128,1024]{1,0:T(8,128)(2,1)S(1)}, u32[]{:S(2)}, u32[]{:S(2)}) collective-permute-start(bf16[128,1024]{1,0:T(8,128)(2,1)} %param.22), channel_id=1, source_target_pairs={{0,16},{4,20},{8,24},{12,28},{16,0},{20,4},{24,8},{28,12},{1,17},{... | collective-permute-start | bytes 786440 | tf_op jit(solution)/shard_map/ppermute | solution.py:163
  50.5 72.3 %collective-permute-start.9 = (bf16[392,1024]{1,0:T(8,128)(2,1)S(1)}, bf16[392,1024]{1,0:T(8,128)(2,1)S(1)}, u32[]{:S(2)}, u32[]{:S(2)}) collective-permute-start(bf16[392,1024]{1,0:T(8,128)(2,1)S(1)} %bitcast.324), channel_id=1, source_target_pairs={{0,3},{1,0},{2,1},{3,2},{4,7},{5,4},{6,5},{7,6},{8,11},{9,8},{10,9... | collective-permute-start | bytes 2408456 | tf_op jit(solution)/shard_map/ppermute | solution.py:167
  54.8 68.3 %collective-permute-start.10 = (bf16[392,1024]{1,0:T(8,128)(2,1)S(1)}, bf16[392,1024]{1,0:T(8,128)(2,1)S(1)}, u32[]{:S(2)}, u32[]{:S(2)}) collective-permute-start(bf16[392,1024]{1,0:T(8,128)(2,1)S(1)} %bitcast.325), channel_id=1, source_target_pairs={{0,2},{1,3},{2,0},{3,1},{4,6},{5,7},{6,4},{7,5},{8,10},{9,11},{10,... | collective-permute-start | bytes 2408456 | tf_op jit(solution)/shard_map/ppermute | solution.py:167
  58.8 29.7 %collective-permute-start.19 = (bf16[128,1024]{1,0:T(8,128)(2,1)}, bf16[128,1024]{1,0:T(8,128)(2,1)S(1)}, u32[]{:S(2)}, u32[]{:S(2)}) collective-permute-start(bf16[128,1024]{1,0:T(8,128)(2,1)} %param.27), channel_id=1, source_target_pairs={{0,4},{4,0},{8,12},{12,8},{16,20},{20,16},{24,28},{28,24},{1,5},{5... | collective-permute-start | bytes 786440 | tf_op jit(solution)/shard_map/ppermute | solution.py:163
  111.9 22.4 %collective-permute-start.11 = (bf16[392,1024]{1,0:T(8,128)(2,1)S(1)}, bf16[392,1024]{1,0:T(8,128)(2,1)S(1)}, u32[]{:S(2)}, u32[]{:S(2)}) collective-permute-start(bf16[392,1024]{1,0:T(8,128)(2,1)S(1)} %bitcast.326), channel_id=1, source_target_pairs={{0,1},{1,2},{2,3},{3,0},{4,5},{5,6},{6,7},{7,4},{8,9},{9,10},{10,1... | collective-permute-start | bytes 2408456 | tf_op jit(solution)/shard_map/ppermute | solution.py:167
  121.4 126.7 %collective-permute-start.24 = (bf16[128,4096]{1,0:T(8,128)(2,1)}, bf16[128,4096]{1,0:T(8,128)(2,1)}, u32[]{:S(2)}, u32[]{:S(2)}) collective-permute-start(bf16[128,4096]{1,0:T(8,128)(2,1)} %param.31), channel_id=1, source_target_pairs={{0,8},{4,12},{8,0},{12,4},{16,24},{20,28},{24,16},{28,20},{1,9},{5... | collective-permute-start | bytes 3145736 | tf_op jit(solution)/shard_map/ppermute | solution.py:163
  122.4 133.5 %collective-permute-start.25 = (bf16[128,4096]{1,0:T(8,128)(2,1)}, bf16[128,4096]{1,0:T(8,128)(2,1)}, u32[]{:S(2)}, u32[]{:S(2)}) collective-permute-start(bf16[128,4096]{1,0:T(8,128)(2,1)} %param.31), channel_id=1, source_target_pairs={{0,16},{4,20},{8,24},{12,28},{16,0},{20,4},{24,8},{28,12},{1,17},{... | collective-permute-start | bytes 3145736 | tf_op jit(solution)/shard_map/ppermute | solution.py:163
  122.8 168.1 %collective-permute-start.28 = (bf16[128,4096]{1,0:T(8,128)(2,1)}, bf16[128,4096]{1,0:T(8,128)(2,1)}, u32[]{:S(2)}, u32[]{:S(2)}) collective-permute-start(bf16[128,4096]{1,0:T(8,128)(2,1)} %param.31), channel_id=1, source_target_pairs={{0,4},{4,0},{8,12},{12,8},{16,20},{20,16},{24,28},{28,24},{1,5},{5... | collective-permute-start | bytes 3145736 | tf_op jit(solution)/shard_map/ppermute | solution.py:163
  123.1 126.1 %collective-permute-start.33 = (bf16[512,1024]{1,0:T(8,128)(2,1)}, bf16[512,1024]{1,0:T(8,128)(2,1)}, u32[]{:S(2)}, u32[]{:S(2)}) collective-permute-start(bf16[512,1024]{1,0:T(8,128)(2,1)} %param.33), channel_id=1, source_target_pairs={{0,8},{4,12},{8,0},{12,4},{16,24},{20,28},{24,16},{28,20},{1,9},{5... | collective-permute-start | bytes 3145736 | tf_op jit(solution)/shard_map/ppermute | solution.py:163
  170.5 36.6 %collective-permute-start.12 = (bf16[392,256]{1,0:T(8,128)(2,1)S(1)}, bf16[392,256]{1,0:T(8,128)(2,1)S(1)}, u32[]{:S(2)}, u32[]{:S(2)}) collective-permute-start(bf16[392,256]{1,0:T(8,128)(2,1)S(1)} %get-tuple-element.75), channel_id=1, source_target_pairs={{0,3},{1,0},{2,1},{3,2},{4,7},{5,4},{6,5},{7,6},{8,11},{9,8},{10,9... | collective-permute-start | bytes 602120 | tf_op jit(solution)/shard_map/ppermute | solution.py:167
  227.4 24.4 %collective-permute-start.34 = (bf16[512,1024]{1,0:T(8,128)(2,1)}, bf16[512,1024]{1,0:T(8,128)(2,1)}, u32[]{:S(2)}, u32[]{:S(2)}) collective-permute-start(bf16[512,1024]{1,0:T(8,128)(2,1)} %param.33), channel_id=1, source_target_pairs={{0,16},{4,20},{8,24},{12,28},{16,0},{20,4},{24,8},{28,12},{1,17},{... | collective-permute-start | bytes 3145736 | tf_op jit(solution)/shard_map/ppermute | solution.py:163
  248.1 41.3 %collective-permute-start.37 = (bf16[512,1024]{1,0:T(8,128)(2,1)}, bf16[512,1024]{1,0:T(8,128)(2,1)S(1)}, u32[]{:S(2)}, u32[]{:S(2)}) collective-permute-start(bf16[512,1024]{1,0:T(8,128)(2,1)} %param.33), channel_id=1, source_target_pairs={{0,4},{4,0},{8,12},{12,8},{16,20},{20,16},{24,28},{28,24},{1,5},{5... | collective-permute-start | bytes 3145736 | tf_op jit(solution)/shard_map/ppermute | solution.py:163
  249.2 30.0 %collective-permute-start.26 = (bf16[64,4096]{1,0:T(8,128)(2,1)S(1)}, bf16[64,4096]{1,0:T(8,128)(2,1)S(1)}, u32[]{:S(2)}, u32[]{:S(2)}) collective-permute-start(bf16[64,4096]{1,0:T(8,128)(2,1)S(1)} %slice.163), channel_id=1, source_target_pairs={{0,16},{4,20},{8,24},{12,28},{16,0},{20,4},{24,8},{28,12},{1,17},{... | collective-permute-start | bytes 1572872 | tf_op jit(solution)/shard_map/ppermute | solution.py:163
  251.8 23.2 %collective-permute-start.35 = (bf16[256,1024]{1,0:T(8,128)(2,1)S(1)}, bf16[256,1024]{1,0:T(8,128)(2,1)}, u32[]{:S(2)}, u32[]{:S(2)}) collective-permute-start(bf16[256,1024]{1,0:T(8,128)(2,1)S(1)} %slice.165), channel_id=1, source_target_pairs={{0,16},{4,20},{8,24},{12,28},{16,0},{20,4},{24,8},{28,12},{1,17},{... | collective-permute-start | bytes 1572872 | tf_op jit(solution)/shard_map/ppermute | solution.py:163
  255.8 21.5 %collective-permute-start.36 = (bf16[256,1024]{1,0:T(8,128)(2,1)S(1)}, bf16[256,1024]{1,0:T(8,128)(2,1)}, u32[]{:S(2)}, u32[]{:S(2)}) collective-permute-start(bf16[256,1024]{1,0:T(8,128)(2,1)S(1)} %slice.166), channel_id=1, source_target_pairs={{0,8},{4,12},{8,0},{12,4},{16,24},{20,28},{24,16},{28,20},{1,9},{5... | collective-permute-start | bytes 1572872 | tf_op jit(solution)/shard_map/ppermute | solution.py:163
  277.4 15.9 %collective-permute-start.29 = (bf16[128,4096]{1,0:T(8,128)(2,1)}, bf16[128,4096]{1,0:T(8,128)(2,1)S(1)}, u32[]{:S(2)}, u32[]{:S(2)}) collective-permute-start(bf16[128,4096]{1,0:T(8,128)(2,1)} %collective-permute-done.24), channel_id=1, source_target_pairs={{0,4},{4,0},{8,12},{12,8},{16,20},{20,16},{24,28},{28,24},{1,5},{5... | collective-permute-start | bytes 3145736 | tf_op jit(solution)/shard_map/ppermute | solution.py:163
  288.5 27.1 %collective-permute-start.38 = (bf16[512,1024]{1,0:T(8,128)(2,1)}, bf16[512,1024]{1,0:T(8,128)(2,1)}, u32[]{:S(2)}, u32[]{:S(2)}) collective-permute-start(bf16[512,1024]{1,0:T(8,128)(2,1)} %collective-permute-done.33), channel_id=1, source_target_pairs={{0,4},{4,0},{8,12},{12,8},{16,20},{20,16},{24,28},{28,24},{1,5},{5... | collective-permute-start | bytes 3145736 | tf_op jit(solution)/shard_map/ppermute | solution.py:163
  289.4 28.5 %collective-permute-start.39 = (bf16[512,1024]{1,0:T(8,128)(2,1)}, bf16[512,1024]{1,0:T(8,128)(2,1)}, u32[]{:S(2)}, u32[]{:S(2)}) collective-permute-start(bf16[512,1024]{1,0:T(8,128)(2,1)} %collective-permute-done.34), channel_id=1, source_target_pairs={{0,4},{4,0},{8,12},{12,8},{16,20},{20,16},{24,28},{28,24},{1,5},{5... | collective-permute-start | bytes 3145736 | tf_op jit(solution)/shard_map/ppermute | solution.py:163
  294.8 25.5 %collective-permute-start.40 = (bf16[256,1024]{1,0:T(8,128)(2,1)}, bf16[256,1024]{1,0:T(8,128)(2,1)}, u32[]{:S(2)}, u32[]{:S(2)}) collective-permute-start(bf16[256,1024]{1,0:T(8,128)(2,1)} %collective-permute-done.35), channel_id=1, source_target_pairs={{0,4},{4,0},{8,12},{12,8},{16,20},{20,16},{24,28},{28,24},{1,5},{5... | collective-permute-start | bytes 1572872 | tf_op jit(solution)/shard_map/ppermute | solution.py:163
  295.9 26.3 %collective-permute-start.41 = (bf16[256,1024]{1,0:T(8,128)(2,1)}, bf16[256,1024]{1,0:T(8,128)(2,1)}, u32[]{:S(2)}, u32[]{:S(2)}) collective-permute-start(bf16[256,1024]{1,0:T(8,128)(2,1)} %collective-permute-done.36), channel_id=1, source_target_pairs={{0,4},{4,0},{8,12},{12,8},{16,20},{20,16},{24,28},{28,24},{1,5},{5... | collective-permute-start | bytes 1572872 | tf_op jit(solution)/shard_map/ppermute | solution.py:163
  353.5 46.5 %collective-permute-start.44 = (bf16[392,256]{1,0:T(8,128)(2,1)S(1)}, bf16[392,256]{1,0:T(8,128)(2,1)S(1)}, u32[]{:S(2)}, u32[]{:S(2)}) collective-permute-start(bf16[392,256]{1,0:T(8,128)(2,1)S(1)} %get-tuple-element.70), channel_id=1, source_target_pairs={{0,1},{1,2},{2,3},{3,0},{4,5},{5,6},{6,7},{7,4},{8,9},{9,10},{10,1... | collective-permute-start | bytes 602120 | tf_op jit(solution)/shard_map/ppermute | solution.py:167
  353.6 46.4 %collective-permute-start.43 = (bf16[392,256]{1,0:T(8,128)(2,1)S(1)}, bf16[392,256]{1,0:T(8,128)(2,1)S(1)}, u32[]{:S(2)}, u32[]{:S(2)}) collective-permute-start(bf16[392,256]{1,0:T(8,128)(2,1)S(1)} %get-tuple-element.71), channel_id=1, source_target_pairs={{0,2},{1,3},{2,0},{3,1},{4,6},{5,7},{6,4},{7,5},{8,10},{9,11},{10,... | collective-permute-start | bytes 602120 | tf_op jit(solution)/shard_map/ppermute | solution.py:167
  353.7 46.3 %collective-permute-start.42 = (bf16[392,256]{1,0:T(8,128)(2,1)S(1)}, bf16[392,256]{1,0:T(8,128)(2,1)S(1)}, u32[]{:S(2)}, u32[]{:S(2)}) collective-permute-start(bf16[392,256]{1,0:T(8,128)(2,1)S(1)} %get-tuple-element.72), channel_id=1, source_target_pairs={{0,3},{1,0},{2,1},{3,2},{4,7},{5,4},{6,5},{7,6},{8,11},{9,8},{10,9... | collective-permute-start | bytes 602120 | tf_op jit(solution)/shard_map/ppermute | solution.py:167
  359.3 178.5 %collective-permute-start.89 = (bf16[512,1024]{1,0:T(8,128)(2,1)}, bf16[512,1024]{1,0:T(8,128)(2,1)}, u32[]{:S(2)}, u32[]{:S(2)}) collective-permute-start(bf16[512,1024]{1,0:T(8,128)(2,1)} %convolution_convert_fusion.2), channel_id=1, source_target_pairs={{0,4},{4,0},{8,12},{12,8},{16,20},{20,16},{24,28},{28,24},{1,5},{5... | collective-permute-start | bytes 3145736 | tf_op jit(solution)/shard_map/ppermute | solution.py:163
  431.7 16.3 %collective-permute-start.45 = (bf16[392,768]{1,0:T(8,128)(2,1)}, bf16[392,768]{1,0:T(8,128)(2,1)}, u32[]{:S(2)}, u32[]{:S(2)}) collective-permute-start(bf16[392,768]{1,0:T(8,128)(2,1)} %get-tuple-element.56), channel_id=1, source_target_pairs={{0,3},{1,0},{2,1},{3,2},{4,7},{5,4},{6,5},{7,6},{8,11},{9,8},{10,9... | collective-permute-start | bytes 1806344 | tf_op jit(solution)/shard_map/ppermute | solution.py:167
  432.3 54.7 %collective-permute-start.46 = (bf16[392,768]{1,0:T(8,128)(2,1)}, bf16[392,768]{1,0:T(8,128)(2,1)}, u32[]{:S(2)}, u32[]{:S(2)}) collective-permute-start(bf16[392,768]{1,0:T(8,128)(2,1)} %get-tuple-element.55), channel_id=1, source_target_pairs={{0,2},{1,3},{2,0},{3,1},{4,6},{5,7},{6,4},{7,5},{8,10},{9,11},{10,... | collective-permute-start | bytes 1806344 | tf_op jit(solution)/shard_map/ppermute | solution.py:167
  440.1 48.0 %collective-permute-start.47 = (bf16[392,768]{1,0:T(8,128)(2,1)}, bf16[392,768]{1,0:T(8,128)(2,1)}, u32[]{:S(2)}, u32[]{:S(2)}) collective-permute-start(bf16[392,768]{1,0:T(8,128)(2,1)} %get-tuple-element.54), channel_id=1, source_target_pairs={{0,1},{1,2},{2,3},{3,0},{4,5},{5,6},{6,7},{7,4},{8,9},{9,10},{10,1... | collective-permute-start | bytes 1806344 | tf_op jit(solution)/shard_map/ppermute | solution.py:167
  530.4 45.2 %collective-permute-start.97 = (bf16[512,4096]{1,0:T(8,128)(2,1)}, bf16[512,4096]{1,0:T(8,128)(2,1)}, u32[]{:S(2)}, u32[]{:S(2)}) collective-permute-start(bf16[512,4096]{1,0:T(8,128)(2,1)} %convolution_convert_fusion), channel_id=1, source_target_pairs={{0,4},{4,0},{8,12},{12,8},{16,20},{20,16},{24,28},{28,24},{1,5},{5... | collective-permute-start | bytes 12582920 | tf_op jit(solution)/shard_map/ppermute | solution.py:163
  530.9 53.1 %collective-permute-start.105 = (bf16[2048,1024]{1,0:T(8,128)(2,1)}, bf16[2048,1024]{1,0:T(8,128)(2,1)}, u32[]{:S(2)}, u32[]{:S(2)}) collective-permute-start(bf16[2048,1024]{1,0:T(8,128)(2,1)} %convolution_convert_fusion.1), channel_id=1, source_target_pairs={{0,4},{4,0},{8,12},{12,8},{16,20},{20,16},{24,28},{28,24},{1,5},{5... | collective-permute-start | bytes 12582920 | tf_op jit(solution)/shard_map/ppermute | solution.py:163
  539.9 16.4 %collective-permute-start.92 = (bf16[2,128,512]{2,1,0:T(8,128)(2,1)S(1)}, bf16[2,128,512]{2,1,0:T(8,128)(2,1)S(1)}, u32[]{:S(2)}, u32[]{:S(2)}) collective-permute-start(bf16[2,128,512]{2,1,0:T(8,128)(2,1)S(1)} %dynamic-slice_bitcast_fusion.16), channel_id=1, source_target_pairs={{0,16},{4,20},{8,24},{12,28},{16,0},{20,4},{24,8},{28,12},{1,17},{... | collective-permute-start | bytes 786440 | tf_op jit(solution)/shard_map/ppermute | solution.py:163
  541.3 16.3 %collective-permute-start.90 = (bf16[2,128,512]{2,1,0:T(8,128)(2,1)S(1)}, bf16[2,128,512]{2,1,0:T(8,128)(2,1)S(1)}, u32[]{:S(2)}, u32[]{:S(2)}) collective-permute-start(bf16[2,128,512]{2,1,0:T(8,128)(2,1)S(1)} %dynamic-slice_bitcast_fusion.17), channel_id=1, source_target_pairs={{0,8},{4,12},{8,0},{12,4},{16,24},{20,28},{24,16},{28,20},{1,9},{5... | collective-permute-start | bytes 786440 | tf_op jit(solution)/shard_map/ppermute | solution.py:163
  581.0 26.2 %collective-permute-start.100 = (bf16[2,128,2048]{2,1,0:T(8,128)(2,1)S(1)}, bf16[2,128,2048]{2,1,0:T(8,128)(2,1)S(1)}, u32[]{:S(2)}, u32[]{:S(2)}) collective-permute-start(bf16[2,128,2048]{2,1,0:T(8,128)(2,1)S(1)} %dynamic-slice_bitcast_fusion.2), channel_id=1, source_target_pairs={{0,16},{4,20},{8,24},{12,28},{16,0},{20,4},{24,8},{28,12},{1,17},{... | collective-permute-start | bytes 3145736 | tf_op jit(solution)/shard_map/ppermute | solution.py:163
  582.7 26.3 %collective-permute-start.98 = (bf16[2,128,2048]{2,1,0:T(8,128)(2,1)S(1)}, bf16[2,128,2048]{2,1,0:T(8,128)(2,1)S(1)}, u32[]{:S(2)}, u32[]{:S(2)}) collective-permute-start(bf16[2,128,2048]{2,1,0:T(8,128)(2,1)S(1)} %dynamic-slice_bitcast_fusion.3), channel_id=1, source_target_pairs={{0,8},{4,12},{8,0},{12,4},{16,24},{20,28},{24,16},{28,20},{1,9},{5... | collective-permute-start | bytes 3145736 | tf_op jit(solution)/shard_map/ppermute | solution.py:163
  589.1 40.5 %collective-permute-start.108 = (bf16[2,512,512]{2,1,0:T(8,128)(2,1)S(1)}, bf16[2,512,512]{2,1,0:T(8,128)(2,1)S(1)}, u32[]{:S(2)}, u32[]{:S(2)}) collective-permute-start(bf16[2,512,512]{2,1,0:T(8,128)(2,1)S(1)} %dynamic-slice_bitcast_fusion), channel_id=1, source_target_pairs={{0,16},{4,20},{8,24},{12,28},{16,0},{20,4},{24,8},{28,12},{1,17},{... | collective-permute-start | bytes 3145736 | tf_op jit(solution)/shard_map/ppermute | solution.py:163
  589.8 41.5 %collective-permute-start.106 = (bf16[2,512,512]{2,1,0:T(8,128)(2,1)S(1)}, bf16[2,512,512]{2,1,0:T(8,128)(2,1)S(1)}, u32[]{:S(2)}, u32[]{:S(2)}) collective-permute-start(bf16[2,512,512]{2,1,0:T(8,128)(2,1)S(1)} %dynamic-slice_bitcast_fusion.1), channel_id=1, source_target_pairs={{0,8},{4,12},{8,0},{12,4},{16,24},{20,28},{24,16},{28,20},{1,9},{5... | collective-permute-start | bytes 3145736 | tf_op jit(solution)/shard_map/ppermute | solution.py:163
  607.6 33.3 %collective-permute-start.101 = (bf16[128,2048]{1,0:T(8,128)(2,1)S(1)}, bf16[128,2048]{1,0:T(8,128)(2,1)S(1)}, u32[]{:S(2)}, u32[]{:S(2)}) collective-permute-start(bf16[128,2048]{1,0:T(8,128)(2,1)S(1)} %dynamic-slice_bitcast_fusion.8), channel_id=1, source_target_pairs={{0,8},{4,12},{8,0},{12,4},{16,24},{20,28},{24,16},{28,20},{1,9},{5... | collective-permute-start | bytes 1572872 | tf_op jit(solution)/shard_map/ppermute | solution.py:163
  609.4 31.7 %collective-permute-start.99 = (bf16[128,2048]{1,0:T(8,128)(2,1)S(1)}, bf16[128,2048]{1,0:T(8,128)(2,1)S(1)}, u32[]{:S(2)}, u32[]{:S(2)}) collective-permute-start(bf16[128,2048]{1,0:T(8,128)(2,1)S(1)} %dynamic-slice_bitcast_fusion.9), channel_id=1, source_target_pairs={{0,16},{4,20},{8,24},{12,28},{16,0},{20,4},{24,8},{28,12},{1,17},{... | collective-permute-start | bytes 1572872 | tf_op jit(solution)/shard_map/ppermute | solution.py:163
  630.0 16.5 %collective-permute-start.109 = (bf16[512,512]{1,0:T(8,128)(2,1)S(1)}, bf16[512,512]{1,0:T(8,128)(2,1)S(1)}, u32[]{:S(2)}, u32[]{:S(2)}) collective-permute-start(bf16[512,512]{1,0:T(8,128)(2,1)S(1)} %dynamic-slice_bitcast_fusion.6), channel_id=1, source_target_pairs={{0,8},{4,12},{8,0},{12,4},{16,24},{20,28},{24,16},{28,20},{1,9},{5... | collective-permute-start | bytes 1572872 | tf_op jit(solution)/shard_map/ppermute | solution.py:163
  642.8 28.5 %collective-permute-start.103 = (bf16[32,4096]{1,0:T(8,128)(2,1)S(1)}, bf16[32,4096]{1,0:T(8,128)(2,1)S(1)}, u32[]{:S(2)}, u32[]{:S(2)}) collective-permute-start(bf16[32,4096]{1,0:T(8,128)(2,1)S(1)} %get-tuple-element.64), channel_id=1, source_target_pairs={{0,2},{1,3},{2,0},{3,1},{4,6},{5,7},{6,4},{7,5},{8,10},{9,11},{10,... | collective-permute-start | bytes 786440 | tf_op jit(solution)/shard_map/ppermute | solution.py:167
  643.5 27.8 %collective-permute-start.102 = (bf16[32,4096]{1,0:T(8,128)(2,1)S(1)}, bf16[32,4096]{1,0:T(8,128)(2,1)S(1)}, u32[]{:S(2)}, u32[]{:S(2)}) collective-permute-start(bf16[32,4096]{1,0:T(8,128)(2,1)S(1)} %get-tuple-element.62), channel_id=1, source_target_pairs={{0,1},{1,2},{2,3},{3,0},{4,5},{5,6},{6,7},{7,4},{8,9},{9,10},{10,1... | collective-permute-start | bytes 786440 | tf_op jit(solution)/shard_map/ppermute | solution.py:167
  647.1 25.2 %collective-permute-start.112 = (bf16[128,1024]{1,0:T(8,128)(2,1)S(1)}, bf16[128,1024]{1,0:T(8,128)(2,1)S(1)}, u32[]{:S(2)}, u32[]{:S(2)}) collective-permute-start(bf16[128,1024]{1,0:T(8,128)(2,1)S(1)} %get-tuple-element.60), channel_id=1, source_target_pairs={{0,3},{1,0},{2,1},{3,2},{4,7},{5,4},{6,5},{7,6},{8,11},{9,8},{10,9... | collective-permute-start | bytes 786440 | tf_op jit(solution)/shard_map/ppermute | solution.py:167
  648.5 28.4 %collective-permute-start.111 = (bf16[128,1024]{1,0:T(8,128)(2,1)S(1)}, bf16[128,1024]{1,0:T(8,128)(2,1)S(1)}, u32[]{:S(2)}, u32[]{:S(2)}) collective-permute-start(bf16[128,1024]{1,0:T(8,128)(2,1)S(1)} %get-tuple-element.61), channel_id=1, source_target_pairs={{0,2},{1,3},{2,0},{3,1},{4,6},{5,7},{6,4},{7,5},{8,10},{9,11},{10,... | collective-permute-start | bytes 786440 | tf_op jit(solution)/shard_map/ppermute | solution.py:167
  649.6 27.4 %collective-permute-start.110 = (bf16[128,1024]{1,0:T(8,128)(2,1)S(1)}, bf16[128,1024]{1,0:T(8,128)(2,1)S(1)}, u32[]{:S(2)}, u32[]{:S(2)}) collective-permute-start(bf16[128,1024]{1,0:T(8,128)(2,1)S(1)} %get-tuple-element.59), channel_id=1, source_target_pairs={{0,1},{1,2},{2,3},{3,0},{4,5},{5,6},{6,7},{7,4},{8,9},{9,10},{10,1... | collective-permute-start | bytes 786440 | tf_op jit(solution)/shard_map/ppermute | solution.py:167
  (111 other events, 1028.5 us)

commit v2 on v1

v2 whole, which is shorter than its diff:
```python
import functools
import math

import jax
import jax.numpy as jnp
from jax import lax
from jax.experimental import pallas as pl
from jax.experimental.pallas import tpu as pltpu
from jax.sharding import PartitionSpec as P

HD = 64
PAIR = 2 * HD
EPSILON = 1e-06
LOG2E = math.log2(math.e)
BF16 = jnp.bfloat16
F32 = jnp.float32
NT = (((1,), (1,)), ((), ()))
NN = (((1,), (0,)), ((), ()))
TN = (((0,), (0,)), ((), ()))
ANY = pl.BlockSpec(memory_space=pl.ANY)
SCALARS = pl.BlockSpec(memory_space=pltpu.SMEM)


def dot(a, b, dims=NN):
    return lax.dot_general(a, b, dims, preferred_element_type=F32)


def like(shape, dtype):
    return pltpu.HBM(shape, dtype)


def placed(*arrays):
    return [pltpu.with_memory_space_constraint(a, pltpu.HBM) for a in arrays]


def standard(rows):
    center = rows - jnp.mean(rows, -1, keepdims=True)
    inverse = lax.rsqrt(jnp.mean(center * center, -1, keepdims=True) + EPSILON)
    return center * inverse, inverse


def norm_grad(grad, normed, inverse, gain):
    scaled = grad * gain
    inner = (
        scaled
        - jnp.mean(scaled, -1, keepdims=True)
        - normed * jnp.mean(scaled * normed, -1, keepdims=True)
    )
    return inner * inverse


def params(mib):
    return pltpu.CompilerParams(vmem_limit_bytes=mib << 20)


def cost(flops, moved, special=0):
    return pl.CostEstimate(flops=flops // 64, bytes_accessed=moved // 64, transcendentals=0)


def piece_table(size):
    if size != 8:
        return [(None, None)]
    return [(far + near, half) for near in (0, 1) for far, half in
            ((0, None), (2, None), (4, None), (6, 0), (6, 1))]


def flip(array, bit, size):
    return lax.ppermute(array, "fsdp", [(i, i ^ (1 << bit)) for i in range(size)])


def shift(array, by, size):
    return lax.ppermute(array, "seq", [(i, (i + by) % size) for i in range(size)])


def gather_near(shard, size):
    return (flip(shard, 1, size), flip(shard, 2, size)) if size == 8 else ()


def gather_pieces(shard, near, size):
    if size != 8:
        return [lax.all_gather(shard, "fsdp", axis=0, tiled=True)]
    half = shard.shape[0] // 2
    one, two = near
    top, low = flip(one[:half], 2, size), flip(two[half:], 1, size)
    pieces = [shard, one, two, top, low]
    return pieces + [flip(piece, 0, size) for piece in pieces]


def piece_copies(table, me, refs, first, target, sems):
    width = target.shape[1]
    copies = []
    for i, ((rel, half), ref) in enumerate(zip(table, refs)):
        count = ref.shape[0]
        if rel is None:
            start = 0
        elif half is None:
            start = jnp.bitwise_xor(me, rel) * count
        else:
            start = jnp.bitwise_xor(me, rel) * (2 * count) + half * count
        source = ref.at[:, pl.ds(first, width)]
        place = target.at[pl.ds(start, count), :]
        copies.append(pltpu.make_async_copy(source, place, sems.at[i]))
    return copies


def block_copies(ref, first, target, sems):
    count = sems.shape[0]
    rows, width = target.shape[0] // count, target.shape[1]
    return [
        pltpu.make_async_copy(
            ref.at[pl.ds(i * rows, rows), pl.ds(first, width)],
            target.at[pl.ds(i * rows, rows), :],
            sems.at[i],
        )
        for i in range(count)
    ]


def project_kernel(seq, table, where_ref, *refs):
    own_ref, down_refs, up_refs = refs[0], refs[1:seq], refs[seq : 2 * seq - 1]
    refs = refs[2 * seq - 1 :]
    w_refs, refs = refs[: len(table)], refs[len(table) :]
    gain_ref, shift_ref, bias_ref, first_ref, qkv_ref, x_sc, w_sc, x_sem, w_sem = refs
    step = pl.program_id(0)
    copies = piece_copies(table, where_ref[0], w_refs, 0, w_sc, w_sem)

    @pl.when(step == 0)
    def _():
        for copy in copies:
            copy.start()
        pltpu.make_async_copy(own_ref, x_sc.at[0], x_sem.at[0]).start()
        for j in range(1, seq):
            inside = where_ref[1] + j < seq

            @pl.when(inside)
            def _(j=j):
                pltpu.make_async_copy(down_refs[j - 1], x_sc.at[j], x_sem.at[j]).start()

            @pl.when(jnp.logical_not(inside))
            def _(j=j):
                pltpu.make_async_copy(up_refs[seq - j - 1], x_sc.at[j], x_sem.at[j]).start()

        for copy in copies:
            copy.wait()

    pltpu.make_async_copy(own_ref, x_sc.at[step], x_sem.at[step]).wait()
    hat, _ = standard(x_sc[step].astype(F32))
    first = (hat * gain_ref[...] + shift_ref[...]).astype(BF16)
    first_ref[...] = first
    qkv_ref[...] = (dot(first, w_sc[...]) + bias_ref[...]).astype(BF16)


def project(where, seq, table, tokens, pieces, gain, shift_by, bias):
    local, width = tokens[0].shape
    columns = pieces[0].shape[1]
    vector = pl.BlockSpec((1, width), lambda i: (0, 0))
    return pl.pallas_call(
        functools.partial(project_kernel, seq, table),
        grid=(seq,),
        in_specs=[SCALARS] + [ANY] * (len(tokens) + len(pieces))
        + [vector, vector, pl.BlockSpec((1, columns), lambda i: (0, 0))],
        out_specs=[
            pl.BlockSpec((local, width), lambda i: (i, 0)),
            pl.BlockSpec((local, columns), lambda i: (i, 0)),
        ],
        out_shape=[
            like((seq * local, width), BF16),
            jax.ShapeDtypeStruct((seq * local, columns), BF16),
        ],
        scratch_shapes=[
            pltpu.VMEM((seq, local, width), BF16),
            pltpu.VMEM((width, columns), BF16),
            pltpu.SemaphoreType.DMA((seq,)),
            pltpu.SemaphoreType.DMA((len(table),)),
        ],
        compiler_params=params(32),
        cost_estimate=cost(2 * seq * local * width * columns, 6 * seq * local * width),
        name="project",
    )(where, *placed(*tokens, *pieces), gain[None], shift_by[None], bias[None])


def forward_kernel(scale, seq, q_ref, k_ref, v_ref, *refs):
    mixed_refs, (exact_ref, lse_ref, value_sc) = refs[:seq], refs[seq:]
    step = pl.program_id(0)

    @pl.when(step == 0)
    def _():
        value_sc[:, :PAIR] = v_ref[...]
        value_sc[:, PAIR:] = jnp.ones((value_sc.shape[0], PAIR), value_sc.dtype)

    query = q_ref[...]
    keys = k_ref[...]
    first = lax.broadcasted_iota(jnp.int32, query.shape, 1) < HD
    outs, sums = [], []
    for head in range(2):
        mine = first if head == 0 else jnp.logical_not(first)
        scores = dot(jnp.where(mine, query, jnp.zeros_like(query)), keys, NT)
        peak = jnp.max(scores, -1, keepdims=True)
        expo = jnp.exp2((scores - peak) * scale).astype(BF16)
        both = dot(expo, value_sc[...])
        total = both[:, PAIR:]
        outs.append(both[:, :PAIR] / total)
        sums.append(peak * scale + jnp.log2(total[:, :1]))
    exact = jnp.where(first, outs[0], outs[1])
    exact_ref[...] = exact
    lse_ref[...] = jnp.concatenate(sums, 1)
    for j in range(seq):

        @pl.when(step == j)
        def _(j=j):
            mixed_refs[j][...] = exact.astype(BF16)


def attention_forward(qkv, pair, pairs, seq):
    length = qkv.shape[0]
    rows = length // seq
    row = pl.BlockSpec((rows, PAIR), lambda i: (i, 0))
    return pl.pallas_call(
        functools.partial(forward_kernel, HD**-0.5 * LOG2E, seq),
        grid=(seq,),
        in_specs=[
            pl.BlockSpec((rows, PAIR), lambda i: (i, pair)),
            pl.BlockSpec((length, PAIR), lambda i: (0, pairs + pair)),
            pl.BlockSpec((length, PAIR), lambda i: (0, 2 * pairs + pair)),
        ],
        out_specs=[pl.BlockSpec((rows, PAIR), lambda i: (0, 0))] * seq
        + [row, pl.BlockSpec((rows, 2), lambda i: (i, 0))],
        out_shape=[like((rows, PAIR), BF16)] * seq
        + [like((length, PAIR), F32), like((length, 2), F32)],
        scratch_shapes=[pltpu.VMEM((length, 2 * PAIR), BF16)],
        compiler_params=params(32),
        cost_estimate=cost(
            16 * length * length * PAIR, 14 * length * PAIR, 2 * length * length
        ),
        name="attention_forward",
    )(qkv, qkv, qkv)


def backward_kernel(scale, seq, q_ref, k_ref, v_ref, *refs):
    grad_refs, (exact_ref, lse_ref), refs = refs[:seq], refs[seq : seq + 2], refs[seq + 2 :]
    out_refs, (dk_sc, dv_sc, grad_sc) = refs[:seq], refs[seq:]
    step = pl.program_id(0)

    @pl.when(step == 0)
    def _():
        dk_sc[...] = jnp.zeros_like(dk_sc)
        dv_sc[...] = jnp.zeros_like(dv_sc)

    for j in range(seq):

        @pl.when(step == j)
        def _(j=j):
            grad_sc[...] = grad_refs[j][...]

    query, keys, values, grad = q_ref[...], k_ref[...], v_ref[...], grad_sc[...]
    first = lax.broadcasted_iota(jnp.int32, query.shape, 1) < HD
    product = grad.astype(F32) * exact_ref[...]
    dqs = []
    for head in range(2):
        mine = first if head == 0 else jnp.logical_not(first)
        zero = jnp.zeros_like(query)
        q_one = jnp.where(mine, query, zero)
        g_one = jnp.where(mine, grad, zero)
        inner = jnp.sum(jnp.where(mine, product, 0.0), -1, keepdims=True)
        probs = jnp.exp2(dot(q_one, keys, NT) * (scale * LOG2E) - lse_ref[:, head : head + 1])
        grad_scores = (probs * (dot(g_one, values, NT) - inner)).astype(BF16)
        dqs.append(dot(grad_scores, keys))
        dv_sc[...] += dot(g_one, probs.astype(BF16), TN)
        dk_sc[...] += dot(q_one, grad_scores, TN)
    dq = (jnp.where(first, dqs[0], dqs[1]) * scale).astype(BF16)
    for j in range(seq):

        @pl.when(step == j)
        def _(j=j):
            out_refs[j][:, :PAIR] = dq

    @pl.when(step == pl.num_programs(0) - 1)
    def _():
        dk = (dk_sc[...] * scale).T.astype(BF16)
        dv = dv_sc[...].T.astype(BF16)
        rows = dk.shape[0] // seq
        for j in range(seq):
            out_refs[j][:, PAIR : 2 * PAIR] = dk[j * rows : (j + 1) * rows]
            out_refs[j][:, 2 * PAIR :] = dv[j * rows : (j + 1) * rows]


def attention_backward(qkv, grads, exact, lse, pair, pairs, seq):
    length = qkv.shape[0]
    rows = length // seq
    row = pl.BlockSpec((rows, PAIR), lambda i: (i, 0))
    return pl.pallas_call(
        functools.partial(backward_kernel, HD**-0.5, seq),
        grid=(seq,),
        in_specs=[
            pl.BlockSpec((rows, PAIR), lambda i: (i, pair)),
            pl.BlockSpec((length, PAIR), lambda i: (0, pairs + pair)),
            pl.BlockSpec((length, PAIR), lambda i: (0, 2 * pairs + pair)),
        ]
        + [pl.BlockSpec((rows, PAIR), lambda i: (0, pair))] * seq
        + [row, pl.BlockSpec((rows, 2), lambda i: (i, 0))],
        out_specs=[pl.BlockSpec((rows, 3 * PAIR), lambda i: (0, 0))] * seq,
        out_shape=[like((rows, 3 * PAIR), BF16)] * seq,
        scratch_shapes=[pltpu.VMEM((PAIR, length), F32)] * 2 + [pltpu.VMEM((rows, PAIR), BF16)],
        compiler_params=params(32),
        cost_estimate=cost(
            40 * length * length * PAIR, 20 * length * PAIR, 2 * length * length
        ),
        name="attention_backward",
    )(qkv, qkv, qkv, *placed(*grads, exact, lse))


def block_of(where_ref, j, seq):
    return lax.rem(where_ref[1] + (seq - j), seq)


def hidden_kernel(seq, pairs, where_ref, *refs):
    count = seq * pairs
    mixed_refs, w_ref = refs[:count], refs[count]
    (x_ref, bout_ref, gain_ref, shift_ref, bfc1_ref, attended_ref, middle_ref, second_ref,
     activ_ref, slope_ref, att_sc, wout_sc, wfc1_sc, mixed_sem, wout_sem, wfc1_sem) = refs[count + 1 :]
    step = pl.program_id(0)
    width = x_ref.shape[1]

    @pl.when(step == 0)
    def _():
        out_copies = block_copies(w_ref, 0, wout_sc, wout_sem)
        for j in range(seq):
            for p in range(pairs):
                place = (block_of(where_ref, j, seq) * pairs + p) * PAIR
                out_copies.append(
                    pltpu.make_async_copy(
                        mixed_refs[j * pairs + p],
                        att_sc.at[:, pl.ds(pl.multiple_of(place, PAIR), PAIR)],
                        mixed_sem.at[j * pairs + p],
                    )
                )
        fc1_copies = block_copies(w_ref, width, wfc1_sc, wfc1_sem)
        for copy in out_copies + fc1_copies:
            copy.start()
        for copy in out_copies:
            copy.wait()
        attended = att_sc[...]
        attended_ref[...] = attended
        middle = x_ref[...].astype(F32) + (dot(attended, wout_sc[...]) + bout_ref[...])
        middle_ref[...] = middle
        hat, _ = standard(middle)
        second_ref[...] = (hat * gain_ref[...] + shift_ref[...]).astype(BF16)
        for copy in fc1_copies:
            copy.wait()

    block = bfc1_ref.shape[1]
    start = pl.multiple_of(step * block, block)
    hidden = dot(second_ref[...], wfc1_sc[:, pl.ds(start, block)]) + bfc1_ref[...]
    cdf = 0.5 * (1.0 + lax.erf(hidden * (0.5**0.5)))
    activ_ref[...] = (hidden * cdf).astype(BF16)
    slope_ref[...] = cdf + hidden * jnp.exp(-0.5 * hidden * hidden) * ((2.0 * math.pi) ** -0.5)


def hidden_layer(where, seq, mixed, weights, x, b_out, gain, shift_by, b_fc1, block):
    local, width = x.shape
    high = b_fc1.shape[0]
    pairs = len(mixed) // seq
    fixed = lambda i: (0, 0)
    tall = pl.BlockSpec((local, width), fixed)
    vector = pl.BlockSpec((1, width), fixed)
    wide = pl.BlockSpec((local, block), lambda i: (0, i))
    return pl.pallas_call(
        functools.partial(hidden_kernel, seq, pairs),
        grid=(high // block,),
        in_specs=[SCALARS] + [ANY] * (len(mixed) + 1)
        + [tall, vector, vector, vector, pl.BlockSpec((1, block), lambda i: (0, i))],
        out_specs=[tall, tall, tall, wide, wide],
        out_shape=[
            like((local, width), BF16),
            like((local, width), F32),
            like((local, width), BF16),
            like((local, high), BF16),
            like((local, high), F32),
        ],
        scratch_shapes=[
            pltpu.VMEM((local, width), BF16),
            pltpu.VMEM((width, width), BF16),
            pltpu.VMEM((width, high), BF16),
            pltpu.SemaphoreType.DMA((len(mixed),)),
            pltpu.SemaphoreType.DMA((4,)),
            pltpu.SemaphoreType.DMA((4,)),
        ],
        compiler_params=params(40),
        cost_estimate=cost(2 * local * width * (width + high), 8 * local * high, local * high),
        name="hidden_layer",
    )(where, *placed(*mixed, weights, x), b_out[None], gain[None], shift_by[None], b_fc1[None])


def output_kernel(blocks, where_ref, present_ref, w_ref, activ_ref, slope_ref, middle_ref, cot_ref,
                  bfc2_ref, out_ref, ghid_ref, sum_ref, final_sc, glow_sc, w_sc, w_sem):
    step = pl.program_id(0)
    present = present_ref[0]
    copies = block_copies(w_ref, 0, w_sc, w_sem)

    @pl.when(step == 0)
    def _():
        for copy in copies:
            copy.start()
        glow_sc[...] = (cot_ref[...].astype(F32) * present).astype(BF16)
        final_sc[...] = middle_ref[...] + bfc2_ref[...]

    for i in range(blocks):

        @pl.when(step == i)
        def _(i=i):
            copies[i].wait()

    block = activ_ref.shape[1]
    below = w_sc[pl.ds(pl.multiple_of(step * block, block), block), :]
    final_sc[...] += dot(activ_ref[...], below)
    grad_hidden = (dot(glow_sc[...], below, NT) * slope_ref[...]).astype(BF16)
    ghid_ref[...] = grad_hidden
    sum_ref[...] = jnp.sum(grad_hidden.astype(F32), 0, keepdims=True)

    @pl.when(step == blocks - 1)
    def _():
        out_ref[...] = (final_sc[...] * present).astype(BF16)


def output_layer(where, present, weights, activ, slope, middle, cot, b_fc2):
    local, width = middle.shape
    high = activ.shape[1]
    blocks = 8
    fixed = lambda i: (0, 0)
    tall = pl.BlockSpec((local, width), fixed)
    wide = pl.BlockSpec((local, high // blocks), lambda i: (0, i))
    return pl.pallas_call(
        functools.partial(output_kernel, blocks),
        grid=(blocks,),
        in_specs=[SCALARS, SCALARS, ANY, wide, wide, tall, tall, pl.BlockSpec((1, width), fixed)],
        out_specs=[tall, wide, pl.BlockSpec((1, high // blocks), lambda i: (0, i))],
        out_shape=[like((local, width), BF16), like((local, high), BF16), like((1, high), F32)],
        scratch_shapes=[
            pltpu.VMEM((local, width), F32),
            pltpu.VMEM((local, width), BF16),
            pltpu.VMEM((high, width), BF16),
            pltpu.SemaphoreType.DMA((blocks,)),
        ],
        compiler_params=params(40),
        cost_estimate=cost(4 * local * width * high, 12 * local * high),
        name="output_layer",
    )(where, present, *placed(weights, activ, slope, middle, cot), b_fc2[None])


def middle_kernel(seq, blocks, where_ref, present_ref, w_ref, ghid_ref, middle_ref, cot_ref,
                  gain_ref, gmid_ref, gbranch_ref, *refs):
    gmixed_refs, (sums_ref, gsecond_sc, wout_sc, wfc1_sc, wout_sem, wfc1_sem) = refs[:seq], refs[seq:]
    step = pl.program_id(0)
    width = middle_ref.shape[1]
    present = present_ref[0]
    upper = block_copies(w_ref, width, wfc1_sc, wfc1_sem)
    outer = block_copies(w_ref, 0, wout_sc, wout_sem)

    @pl.when(step == 0)
    def _():
        for copy in upper + outer:
            copy.start()
        gsecond_sc[...] = jnp.zeros_like(gsecond_sc)
        for copy in upper:
            copy.wait()

    block = ghid_ref.shape[1]
    start = pl.multiple_of(step * block, block)
    gsecond_sc[...] += dot(ghid_ref[...], wfc1_sc[:, pl.ds(start, block)], NT)

    @pl.when(step == blocks - 1)
    def _():
        for copy in outer:
            copy.wait()
        hat, inverse = standard(middle_ref[...])
        grad_second = gsecond_sc[...]
        grad_rows = cot_ref[...].astype(F32) * present
        grad_middle = grad_rows + norm_grad(grad_second, hat, inverse, gain_ref[...])
        gmid_ref[...] = grad_middle
        grad_branch = grad_middle.astype(BF16)
        gbranch_ref[...] = grad_branch
        sums_ref[...] = jnp.concatenate(
            [
                jnp.sum(grad_branch.astype(F32), 0, keepdims=True),
                jnp.sum(grad_second * hat, 0, keepdims=True),
                jnp.sum(grad_second, 0, keepdims=True),
                jnp.sum(grad_rows, 0, keepdims=True),
            ],
            0,
        )
        own = width // seq
        for j in range(seq):
            rows = pl.multiple_of(block_of(where_ref, j, seq) * own, own)
            gmixed_refs[j][...] = dot(grad_branch, wout_sc[pl.ds(rows, own), :], NT).astype(BF16)


def middle_layer(where, present, seq, weights, grad_hidden, middle, cot, gain):
    local, width = middle.shape
    high = grad_hidden.shape[1]
    blocks = 4
    fixed = lambda i: (0, 0)
    tall = pl.BlockSpec((local, width), fixed)
    own = width // seq
    return pl.pallas_call(
        functools.partial(middle_kernel, seq, blocks),
        grid=(blocks,),
        in_specs=[
            SCALARS,
            SCALARS,
            ANY,
            pl.BlockSpec((local, high // blocks), lambda i: (0, i)),
            tall,
            tall,
            pl.BlockSpec((1, width), fixed),
        ],
        out_specs=[tall, tall]
        + [pl.BlockSpec((local, own), fixed)] * seq
        + [pl.BlockSpec((4, width), fixed)],
        out_shape=[like((local, width), F32), like((local, width), BF16)]
        + [like((local, own), BF16)] * seq
        + [like((4, width), F32)],
        scratch_shapes=[
            pltpu.VMEM((local, width), F32),
            pltpu.VMEM((width, width), BF16),
            pltpu.VMEM((width, high), BF16),
            pltpu.SemaphoreType.DMA((4,)),
            pltpu.SemaphoreType.DMA((4,)),
        ],
        compiler_params=params(40),
        cost_estimate=cost(2 * local * width * (width + high), 12 * local * high),
        name="middle_layer",
    )(where, present, *placed(weights, grad_hidden, middle, cot), gain[None])


def last_kernel(seq, pairs, where_ref, *refs):
    count = seq * pairs
    grad_refs, w_ref = refs[:count], refs[count]
    x_ref, gmid_ref, gain_ref, out_ref, sums_ref, grad_sc, w_sc, grad_sem, w_sem = refs[count + 1 :]
    width = x_ref.shape[1]
    copies = block_copies(w_ref, 0, w_sc, w_sem)
    for j in range(seq):
        for p in range(pairs):
            place = (block_of(where_ref, j, seq) * pairs + p) * PAIR
            for t in range(3):
                copies.append(
                    pltpu.make_async_copy(
                        grad_refs[j * pairs + p].at[:, pl.ds(t * PAIR, PAIR)],
                        grad_sc.at[:, pl.ds(pl.multiple_of(t * width + place, PAIR), PAIR)],
                        grad_sem.at[(j * pairs + p) * 3 + t],
                    )
                )
    for copy in copies:
        copy.start()
    hat, inverse = standard(x_ref[...].astype(F32))
    for copy in copies:
        copy.wait()
    grad_first = dot(grad_sc[...], w_sc[...], NT)
    out_ref[...] = gmid_ref[...] + norm_grad(grad_first, hat, inverse, gain_ref[...])
    sums_ref[...] = jnp.concatenate(
        [jnp.sum(grad_first * hat, 0, keepdims=True), jnp.sum(grad_first, 0, keepdims=True)], 0
    )


def last_layer(where, seq, grads, weights, x, grad_middle, gain):
    local, width = x.shape
    pairs = len(grads) // seq
    whole = pl.BlockSpec(memory_space=pltpu.VMEM)
    return pl.pallas_call(
        functools.partial(last_kernel, seq, pairs),
        in_specs=[SCALARS] + [ANY] * (len(grads) + 1) + [whole] * 3,
        out_specs=[whole, whole],
        out_shape=[like((local, width), F32), like((2, width), F32)],
        scratch_shapes=[
            pltpu.VMEM((local, 3 * width), BF16),
            pltpu.VMEM((width, 3 * width), BF16),
            pltpu.SemaphoreType.DMA((3 * len(grads),)),
            pltpu.SemaphoreType.DMA((4,)),
        ],
        compiler_params=params(56),
        cost_estimate=cost(6 * local * width * width, 6 * width * width),
        name="last_layer",
    )(where, *placed(*grads, weights, x, grad_middle), gain[None])


def product(sides, refs):
    parts = []
    for count in sides:
        left, right_refs, refs = refs[0][...], refs[1 : 1 + count], refs[1 + count :]
        rows = right_refs[0].shape[0]
        groups = left.shape[0] // rows
        total = None
        for g in range(groups):
            blocks = [r[...] for r in right_refs[g::groups]]
            right = blocks[0] if len(blocks) == 1 else jnp.concatenate(blocks, 1)
            term = dot(left[g * rows : (g + 1) * rows], right, TN)
            total = term if total is None else total + term
        parts.append(total)
    return parts[0] if len(parts) == 1 else jnp.concatenate(parts, 1)


def away_kernel(sides, where_ref, *refs):
    refs[-1][0] = product(sides, refs[:-1]).astype(BF16)


def kept_kernel(sides, where_ref, *refs):
    refs, (arrived_ref, far1, keep1, far2, keep2) = refs[:-5], refs[-5:]
    step = pl.program_id(0)
    total = (product(sides, refs) + arrived_ref[0].astype(F32)).astype(BF16)
    half = total.shape[1] // 2

    @pl.when(step % 2 == 1)
    def _():
        far1[0] = total[:, :half]

    @pl.when(step % 2 == 0)
    def _():
        keep1[0] = total[:, :half]

    @pl.when(step >= 2)
    def _():
        far2[0] = total[:, half:]

    @pl.when(step < 2)
    def _():
        keep2[0] = total[:, half:]


def weight_shape(job):
    columns = [sum(r.shape[1] for r in rights) * rights[0].shape[0] // left.shape[0]
               for left, rights in job]
    return job[0][0].shape[1] // 8, sum(columns)


def weight_call(where, job, kernel, odd, more, out_specs, out_shape, name):
    rest, columns = weight_shape(job)
    specs, args = [], []
    for left, rights in job:
        specs.append(
            pl.BlockSpec(
                (left.shape[0], rest), lambda i, w: (0, jnp.bitwise_xor(w[0], 2 * i + odd))
            )
        )
        specs += [pl.BlockSpec(r.shape, lambda i, w: (0, 0)) for r in rights]
        args += [left, *rights]
    return pl.pallas_call(
        functools.partial(kernel, [len(rights) for _, rights in job]),
        grid_spec=pltpu.PrefetchScalarGridSpec(
            num_scalar_prefetch=1,
            grid=(4,),
            in_specs=specs
            + [pl.BlockSpec((1, rest, columns), lambda i, w: (i, 0, 0)) for _ in more],
            out_specs=out_specs,
        ),
        out_shape=out_shape,
        compiler_params=params(48),
        cost_estimate=cost(job[0][0].shape[0] * 8 * rest * columns, 8 * rest * columns),
        name=name,
    )(where, *placed(*args, *more))


def weight_away(where, job):
    rest, columns = weight_shape(job)
    return weight_call(
        where,
        job,
        away_kernel,
        1,
        [],
        pl.BlockSpec((1, rest, columns), lambda i, w: (i, 0, 0)),
        like((4, rest, columns), BF16),
        "weight_away",
    )


def weight_kept(where, job, arrived):
    rest, columns = weight_shape(job)
    two = like((2, rest, columns // 2), BF16)

    def spec(which):
        return pl.BlockSpec((1, rest, columns // 2), lambda i, w: (which(i), 0, 0))

    far1, keep1, far2, keep2 = weight_call(
        where,
        job,
        kept_kernel,
        0,
        [arrived],
        [
            spec(lambda i: i // 2),
            spec(lambda i: i // 2),
            spec(lambda i: jnp.maximum(i - 2, 0)),
            spec(lambda i: jnp.minimum(i, 1)),
        ],
        [two] * 4,
        "weight_kept",
    )
    return (keep1, flip(far1, 1, 8)), (keep2, flip(far2, 2, 8))


def second_kernel(keep1_ref, came1_ref, keep2_ref, came2_ref, *out_refs):
    far1, stay1, far2, stay2 = out_refs
    for keep_ref, came_ref, far, stay in (
        (keep1_ref, came1_ref, far1, stay1),
        (keep2_ref, came2_ref, far2, stay2),
    ):
        total = (keep_ref[...].astype(F32) + came_ref[...].astype(F32)).astype(BF16)
        stay[...] = total[0]
        far[...] = total[1]


def second_sums(first, before, ahead):
    (keep1, came1), (keep2, came2) = first
    keep1 = after(keep1, before)
    _, rest, half = keep1.shape
    rows = rest // 4
    spec = pl.BlockSpec((2, rows, half), lambda i: (0, i, 0))
    out = pl.BlockSpec((rows, half), lambda i: (i, 0))
    far1, stay1, far2, stay2 = pl.pallas_call(
        second_kernel,
        grid=(4,),
        in_specs=[spec] * 4,
        out_specs=[out] * 4,
        out_shape=[like((rest, half), BF16)] * 4,
        compiler_params=params(32),
        cost_estimate=cost(4 * rest * half, 24 * rest * half),
        name="second_sums",
    )(*placed(keep1, came1, keep2, came2))
    far1, far2 = after((far1, far2), ahead)
    return (stay1, flip(far1, 2, 8)), (stay2, flip(far2, 1, 8))


def spread_kernel(seq, where_ref, *refs):
    ins, outs = refs[:-seq], refs[-seq:]
    both = jnp.concatenate(
        [a[...].astype(F32) + b[...].astype(F32) for a, b in zip(ins[0::2], ins[1::2])], 1
    )
    for j, out_ref in enumerate(outs):

        @pl.when(pl.program_id(0) == j)
        def _(out_ref=out_ref):
            out_ref[...] = both.astype(out_ref.dtype)


def seq_spread(where, seconds, seq):
    arrays = [array for second in seconds for part in second for array in part]
    rest = arrays[0].shape[0]
    rows = rest // seq
    columns = sum(a.shape[1] for a in arrays[::2])
    blocks = [
        pl.BlockSpec((rows, a.shape[1]), lambda i, w: (lax.rem(w[1] + i, seq), 0)) for a in arrays
    ]
    out = pl.BlockSpec((rows, columns), lambda i, w: (0, 0))
    return pl.pallas_call(
        functools.partial(spread_kernel, seq),
        grid_spec=pltpu.PrefetchScalarGridSpec(
            num_scalar_prefetch=1, grid=(seq,), in_specs=blocks, out_specs=[out] * seq
        ),
        out_shape=[like((rows, columns), F32)] + [like((rows, columns), BF16)] * (seq - 1),
        compiler_params=params(32),
        cost_estimate=cost(rest * columns, 8 * rest * columns),
        name="seq_spread",
    )(where, *placed(*arrays))


def plain_sums(job, seq):
    blocks = []
    for left, rights in job:
        groups = left.shape[0] // rights[0].shape[0]
        right = jnp.concatenate([jnp.concatenate(rights[g::groups], 1) for g in range(groups)], 0)
        product = dot(left, right, TN)
        blocks.append(lax.psum_scatter(product, "fsdp", scatter_dimension=0, tiled=True))
    me = lax.axis_index("seq")
    parts = jnp.concatenate(blocks, 1)
    parts = parts.reshape(seq, parts.shape[0] // seq, parts.shape[1])
    chunks = [lax.dynamic_index_in_dim(parts, (me + j) % seq, 0, False) for j in range(seq)]
    return [chunks[0]] + [c.astype(BF16) for c in chunks[1:]]


def sum_vectors(vectors, fsdp, seq):
    me = lax.axis_index("fsdp")
    bits = fsdp.bit_length() - 1
    sizes = [v.shape[0] // (fsdp * seq) for v in vectors]
    block = jnp.concatenate([v.reshape(fsdp, seq, -1) for v in vectors], 2)
    block = block.reshape((2,) * bits + (seq, sum(sizes)))
    for bit in range(bits):
        axis = bits - 1 - bit
        mine = (me >> bit) & 1
        away = lax.dynamic_index_in_dim(block, 1 - mine, axis, False)
        block = lax.dynamic_index_in_dim(block, mine, axis, False) + flip(away, bit, fsdp)
    return block, sizes


def split_vectors(block, sizes, seq):
    place = lax.axis_index("seq")
    total = lax.dynamic_index_in_dim(block, place, 0, False)
    for by in range(1, seq):
        away = lax.dynamic_index_in_dim(block, (place + by) % seq, 0, False)
        total = total + shift(away, by, seq)
    return jnp.split(total, [sum(sizes[: i + 1]) for i in range(len(sizes) - 1)])


def after(value, *others):
    return lax.optimization_barrier((value, others))[0]


def spread_pairs(parts, seq):
    arrived = []
    for blocks in parts:
        if arrived:
            blocks = after(blocks, arrived[-1][1:])
        arrived.append([blocks[0]] + [shift(blocks[j], j, seq) for j in range(1, seq)])
    return [pair[j] for j in range(seq) for pair in arrived]


def on_device(
    fsdp,
    seq,
    inputs,
    clip_mask,
    ln1_gain,
    ln1_bias,
    w_query,
    b_query,
    w_key,
    w_value,
    b_value,
    w_out,
    b_out,
    ln2_gain,
    ln2_bias,
    w_fc1,
    b_fc1,
    w_fc2,
    b_fc2,
    cotangent,
):
    clips, local, width = inputs.shape
    assert clips == 1
    me = lax.axis_index("seq")
    where = jnp.stack([lax.axis_index("fsdp"), me]).astype(jnp.int32)
    present = clip_mask.astype(F32)
    own = width // seq
    pairs = own // PAIR
    table = piece_table(fsdp)
    x, cot = inputs[0], cotangent[0]
    grad_low = (cot.astype(F32) * present).astype(BF16)

    def columns(array, axis):
        return lax.dynamic_slice_in_dim(array, me * own, own, axis)

    shard_heads = jnp.concatenate([columns(w, 1) for w in (w_query, w_key, w_value)], 1)
    near_heads = gather_near(shard_heads, fsdp)
    down, up = [x], [x]
    for hop in range(1, seq):
        if hop == 2:
            down[-1], up[-1], near_heads = after((down[-1], up[-1], near_heads))
            w_heads = gather_pieces(shard_heads, near_heads, fsdp)
        if hop == 3:
            down[-1], up[-1] = after((down[-1], up[-1]), w_heads)
        down.append(lax.ppermute(down[-1], "seq", [(i, i - 1) for i in range(1, seq + 1 - hop)]))
        up.append(lax.ppermute(up[-1], "seq", [(i, i + 1) for i in range(hop - 1, seq - 1)]))
    b_heads = jnp.concatenate([columns(b_query, 0), jnp.zeros((own,), F32), columns(b_value, 0)])
    one = lax.all_gather(jnp.concatenate([w_out, w_fc1], 1), "fsdp", axis=0, tiled=True)
    two = lax.all_gather(after(w_fc2, down[1], up[1]), "fsdp", axis=0, tiled=True)
    shard_three = jnp.concatenate([w_query, w_key, w_value], 1)

    first_in, qkv = project(
        where,
        seq,
        table,
        [x] + down[1:] + up[1:],
        w_heads,
        ln1_gain,
        ln1_bias,
        b_heads,
    )
    forward = [attention_forward(qkv, 0, pairs, seq)]
    for p in range(1, pairs):
        forward.append(attention_forward(qkv, p, pairs, seq))
    mixed = spread_pairs([part[:seq] for part in forward], seq)
    attended, middle, second_in, activ, slope = hidden_layer(
        where, seq, mixed, one, x, b_out, ln2_gain, ln2_bias, b_fc1, 512
    )
    parts = {}

    def away(name, job, before):
        if fsdp == 8:
            parts[name] = weight_away(after(where, before), job)
        else:
            parts[name] = plain_sums(job, seq)
        return parts[name]

    def kept(name, job, before, ahead=()):
        if fsdp != 8:
            return ()
        arrived = flip(after(parts[name], ahead), 0, 8)
        parts[name] = weight_kept(after(where, before), job, arrived)
        return parts[name][0][0]

    def second(name, before, ahead=()):
        if fsdp != 8:
            return ()
        parts[name] = second_sums(parts[name], before, ahead)
        return parts[name][0][0]

    def chunks(names, before):
        if fsdp == 8:
            return seq_spread(after(where, before), [parts[n] for n in names], seq)
        return [jnp.concatenate(blocks, 1) for blocks in zip(*[parts[n] for n in names])]

    def came(name):
        return (parts[name][0][1], parts[name][1][1]) if fsdp == 8 else ()

    def send(blocks, ahead):
        if ahead:
            blocks = after(blocks, ahead)
        return [blocks[0]] + [shift(blocks[j], j, seq) for j in range(1, seq)]

    low = [(activ, [grad_low])]
    step = away("low", low, ())
    output, grad_hidden, sum_fc1 = output_layer(
        after(where, step), present, two, activ, slope, middle, cot, b_fc2
    )
    step = kept("low", low, grad_hidden)
    high = [(second_in, [grad_hidden])]
    step = away("high", high, step)
    results = middle_layer(
        after(where, step), present, seq, one, grad_hidden, middle, cot, ln2_gain
    )
    grad_middle, grad_branch = results[:2]
    grad_mixed, sums2 = results[2 : 2 + seq], results[2 + seq]
    grads = [grad_mixed[0]] + [shift(grad_mixed[j], -j, seq) for j in range(1, seq)]
    low_came = came("low")
    step = second("low", grad_branch)
    step = kept("high", high, (step, grads, came("low")), (low_came, grad_branch))
    low_rows = chunks(["low"], step)
    step = low_rows[1]
    low_rows = send(low_rows, ())
    back, home = [], []
    for p in range(pairs):
        exact, lse = forward[p][seq:]
        back.append(attention_backward(qkv, grads, exact, after(lse, step), p, pairs, seq))
        home.append(send(back[-1], home[-1][1:] if home else low_rows[1:]))
        step = back[-1][0]
        if p == 0:
            step = second("high", step, low_rows[1:])
            three = lax.all_gather(after(shard_three, step, low_rows[1:]), "fsdp", axis=0, tiled=True)
    total_low = sum(rows.astype(F32) for rows in low_rows)
    late = [(first_in, [b for pair in back for b in pair]), (attended, [grad_branch])]
    step = away("late", late, (step, came("high")))
    step = kept("late", late, step, home[0])
    step = second("late", step)
    rows = chunks(["late", "high"], step)
    grad_inputs, sums1 = last_layer(
        after(where, rows[0]),
        seq,
        [pair[j] for j in range(seq) for pair in home],
        three,
        x,
        grad_middle,
        ln1_gain,
    )
    def spread(which):
        vector = jnp.concatenate(
            [
                sum(
                    jnp.sum(block[:, which * PAIR : (which + 1) * PAIR].astype(F32), 0)
                    for block in back[p]
                )
                for p in range(pairs)
            ]
        )
        return lax.dynamic_update_slice(jnp.zeros((width,), F32), vector, (me * own,))

    block, sizes = sum_vectors(
        [sums1[0], sums1[1], spread(0), spread(2)] + [sums2[i] for i in range(4)] + [sum_fc1[0]],
        fsdp,
        seq,
    )
    split = 3 * own
    rows = after(send(rows, home[-1][1:]), block)
    total_rows = sum(part[:, split:].astype(F32) for part in rows)
    total_out, total_high = total_rows[:, :width], total_rows[:, width:]
    heads = [part[:, :split].astype(F32) for part in rows[::-1]]
    grad_heads = lax.dynamic_slice_in_dim(jnp.stack(heads + heads), (seq - 1 - me) % seq, seq, 0)
    strip = grad_heads.shape[1]
    grad_heads = grad_heads.reshape(seq, strip, pairs, 3, PAIR).transpose(3, 1, 0, 2, 4)
    grad_heads = grad_heads.reshape(3, strip, width)

    sums = split_vectors(block, sizes, seq)
    return (
        output[None],
        grad_inputs[None],
        sums[0],
        sums[1],
        grad_heads[0],
        sums[2],
        grad_heads[1],
        grad_heads[2],
        sums[3],
        total_out,
        sums[4],
        sums[5],
        sums[6],
        total_high,
        sums[8],
        total_low,
        sums[7],
    )


def solution(mesh):
    rows, both = P("fsdp", None), P(("fsdp", "seq"))
    tokens = P("fsdp", "seq", None)
    matrix = P(("fsdp", "seq"), None)
    return jax.shard_map(
        functools.partial(on_device, mesh.shape["fsdp"], mesh.shape["seq"]),
        mesh=mesh,
        in_specs=(
            tokens,
            P("fsdp"),
            P(),
            P(),
            rows,
            P(),
            rows,
            rows,
            P(),
            rows,
            P(),
            P(),
            P(),
            rows,
            P(),
            rows,
            P(),
            tokens,
        ),
        out_specs=(
            tokens,
            tokens,
            both,
            both,
            matrix,
            both,
            matrix,
            matrix,
            both,
            matrix,
            both,
            both,
            both,
            matrix,
            both,
            matrix,
            both,
        ),
        check_vma=False,
    )
```

time: 687 us -> 423 us (0.62)
  local copies, waits for them, and re-layouts: 223 us -> 20.7 us
  Pallas kernels: 50.7 us -> 188 us
  waiting for transfers between devices: 198 us -> 92.3 us
  matrix products: 82.5 us -> 0 us
  between operations: 3.41 us -> 15.9 us
  starting transfers between devices: 102 us -> 90.5 us
  other arithmetic: 19 us -> 7.63 us
    pallas_call x2 -> x20, Pallas kernels: 50.7 us -> 188 us  [the longest x6 44.8 us: weight_call(): pl.pallas_call(functools.partial(kernel, [len(rights) for _, rights in jo...]
    dot_general x21 -> x0, matrix products: 82.5 us -> none  [dot(): return lax.dot_general(a, b, dims, preferred_element_type=F32)]
    ppermute x86 -> x27, waiting for transfers between devices: 107 us -> 30.8 us  [flip(): return lax.ppermute(array, 'fsdp', [(i, i ^ 1 << bit) for i in range(size)])]
    dynamic_update_slice x71 -> x0, local copies, waits for them, and re-layouts: 67.8 us -> none  [the longest x69 66.9 us: gather_rows(): whole = lax.dynamic_update_slice(whole, piece, (place, 0))]
    ppermute x27 -> x24, waiting for transfers between devices: 91.2 us -> 31.5 us  [shift(): lax.ppermute(array, 'seq', [(i, (i + by) % size) for i in range(size)])]
    dynamic_slice x5 -> x2, local copies, waits for them, and re-layouts: 56.5 us -> 0.08 us  [the longest x1 0.04 us: split_vectors(): away = lax.dynamic_index_in_dim(block, (place + by) % seq, 0, False)]
    ppermute x86 -> x27, starting transfers between devices: 58.6 us -> 22.9 us  [flip(): return lax.ppermute(array, 'fsdp', [(i, i ^ 1 << bit) for i in range(size)])]
    ppermute x0 -> x6, waiting for transfers between devices: none -> 29.9 us  [the longest x3 28.7 us: on_device(): lax.ppermute(down[-1], 'seq', [(i, i - 1) for i in range(1, seq + 1 - hop)])]
  transfers between devices with their start and end apart: 113 -> 60, of which waited for: 40 -> 26; matrix products, arithmetic and copies ran while one was open for 42% -> 3% of each run, Pallas kernels for 7% -> 39%
where the time goes in v2:
time: 423 us; the launch traced here: 415 us
  Pallas kernels  188 us (44%)
  waiting for transfers between devices  92.3 us (22%)
  starting transfers between devices  90.5 us (21%)
  local copies, waits for them, and re-layouts  20.7 us (5%)
  between operations  15.9 us (4%)
  other arithmetic  7.63 us (2%)
    ppermute x24, starting transfers between devices, shift(): lax.ppermute(array, 'seq', [(i, (i + by) % size) for i in range(size)])  54.9 us
    pallas_call x6, Pallas kernels, weight_call(): pl.pallas_call(functools.partial(kernel, [len(rights) for _, rights in jo...  44.8 us
    pallas_call x2, Pallas kernels, attention_backward(): pl.pallas_call(functools.partial(backward_kernel, HD ** (-0.5), seq), gri...  35 us
    ppermute x24, waiting for transfers between devices, shift(): lax.ppermute(array, 'seq', [(i, (i + by) % size) for i in range(size)])  31.5 us
    ppermute x27, waiting for transfers between devices, flip(): return lax.ppermute(array, 'fsdp', [(i, i ^ 1 << bit) for i in range(size)])  30.8 us
    ppermute x3, waiting for transfers between devices, on_device(): lax.ppermute(down[-1], 'seq', [(i, i - 1) for i in range(1, seq + 1 - hop)])  28.7 us
    pallas_call x2, Pallas kernels, attention_forward(): pl.pallas_call(functools.partial(forward_kernel, HD ** (-0.5) * LOG2E, se...  23.5 us
    ppermute x27, starting transfers between devices, flip(): return lax.ppermute(array, 'fsdp', [(i, i ^ 1 << bit) for i in range(size)])  22.9 us
  transfers between devices with their start and end apart: 60, of which 26 were waited for; matrix products, arithmetic and copies ran while one was open for 3% of the time, Pallas kernels for 39%

profile of v2, /device:TPU:0, one launch (start us, length us, event | category | flops | bytes accessed | tf_op | source)
XLA Modules:
  0.0 414.7 jit_solution(14591583089922683109)
XLA Ops:
  7.2 2.5 pad_maximum_fusion
  11.1 5.6 %collective-permute-start.1 = (bf16[392,1024]{1,0:T(8,128)(2,1)S(1)}, bf16[392,1024]{1,0:T(8,128)(2,1)S(1)}, u32[]{:S(2)}, u32[]{:S(2)}) collective-permute-start(bf16[392,1024]{1,0:T(8,128)(2,1)S(1)} %bitcast.59), channel_id=1, source_target_pairs={{0,1},{1,2},{2,3},{4,5},{5,6},{6,7},{8,9},{9,10},{10,11},{12,13},{... | collective-permute-start | bytes 2408456 | tf_op jit(solution)/shard_map/ppermute | solution.py:861
  18.5 2.0 collective-permute-start.2
  22.0 6.1 %collective-permute-done.2.refs_8_ = bf16[128,768]{1,0:T(8,128)(2,1)S(1)} collective-permute-done((bf16[128,768]{1,0:T(8,128)(2,1)S(1)}, bf16[128,768]{1,0:T(8,128)(2,1)S(1)}, u32[]{:S(2)}, u32[]{:S(2)}) %collective-permute-start.2) | collective-permute-done | bytes 196640 | tf_op jit(solution)/shard_map/ppermute | solution.py:68
  29.9 2.8 collective-permute-done.refs_1_
  40.3 2.1 collective-permute-done.6.refs_10_
  45.3 10.1 %collective-permute-done.4.refs_2_ = bf16[392,1024]{1,0:T(8,128)(2,1)S(1)} collective-permute-done((bf16[392,1024]{1,0:T(8,128)(2,1)S(1)}, bf16[392,1024]{1,0:T(8,128)(2,1)S(1)}, u32[]{:S(2)}, u32[]{:S(2)}) %collective-permute-start.4) | collective-permute-done | bytes 802848 | tf_op jit(solution)/shard_map/ppermute | solution.py:860
  59.9 15.8 %collective-permute-done.13.refs_3_ = bf16[392,1024]{1,0:T(8,128)(2,1)} collective-permute-done((bf16[392,1024]{1,0:T(8,128)(2,1)S(1)}, bf16[392,1024]{1,0:T(8,128)(2,1)}, u32[]{:S(2)}, u32[]{:S(2)}) %collective-permute-start.13) | collective-permute-done | bytes 802848 | tf_op jit(solution)/shard_map/ppermute | solution.py:860
  75.8 8.3 %project.1 = (bf16[1568,1024]{1,0:T(8,128)(2,1)}, bf16[1568,768]{1,0:T(8,128)(2,1)S(1)}) custom-call(s32[2]{0:T(128)S(1)} %pad_add_fusion.where_ref, bf16[392,1024]{1,0:T(8,128)(2,1)} %bitcast.55, bf16[392,1024]{1,0:T(8,128)(2,1)} %copy-done.28, bf16[392,1024]{1,0:T(8,128)(2,1)} %copy-done.30, bf16[392,1024]{1,0:T(8,128)(2,1)} %collective-permute-done.13.refs_3_, ...), custom_call_target="tpu_custom_call" | custom-call | flops 38535168 | bytes 150528 | tf_op jit(solution)/shard_map/project/pallas_call | solution.py:157
  84.1 11.8 %attention_forward.2 = (bf16[392,128]{1,0:T(8,128)(2,1)}, bf16[392,128]{1,0:T(8,128)(2,1)}, bf16[392,128]{1,0:T(8,128)(2,1)}, bf16[392,128]{1,0:T(8,128)(2,1)}, f32[1568,128]{1,0:T(8,128)}, /*index=5*/f32[1568,2]{1,0:T(8,128)}) custom-call(bf16[1568,768]{1,0:T(8,128)(2,1)S(1)} %get-tuple-element.144.q_ref.k_ref.v_ref, ...), custom_call_target="tpu_custom_call" | custom-call | flops 78675968 | bytes 43904 | tf_op jit(solution)/shard_map/attention_forward/pallas_call | solution.py:218
  95.9 6.3 %collective-permute-start.16 = (bf16[392,128]{1,0:T(8,128)(2,1)}, bf16[392,128]{1,0:T(8,128)(2,1)S(1)}, u32[]{:S(2)}, u32[]{:S(2)}) collective-permute-start(bf16[392,128]{1,0:T(8,128)(2,1)} %get-tuple-element.151), channel_id=1, source_target_pairs={{0,2},{1,3},{2,0},{3,1},{4,6},{5,7},{6,4},{7,5},{8,10},{9,11},{10,... | collective-permute-start | bytes 301064 | tf_op jit(solution)/shard_map/ppermute | solution.py:72
  103.4 11.8 %attention_forward.3 = (bf16[392,128]{1,0:T(8,128)(2,1)}, bf16[392,128]{1,0:T(8,128)(2,1)}, bf16[392,128]{1,0:T(8,128)(2,1)}, bf16[392,128]{1,0:T(8,128)(2,1)}, f32[1568,128]{1,0:T(8,128)}, /*index=5*/f32[1568,2]{1,0:T(8,128)}) custom-call(bf16[1568,768]{1,0:T(8,128)(2,1)S(1)} %get-tuple-element.144.q_ref.k_ref.v_ref, ...), custom_call_target="tpu_custom_call" | custom-call | flops 78675968 | bytes 43904 | tf_op jit(solution)/shard_map/attention_forward/pallas_call | solution.py:218
  116.9 2.6 collective-permute-start.20
  122.0 2.1 collective-permute-done.19.refs_5_
  124.8 15.7 %hidden_layer.1 = (bf16[392,1024]{1,0:T(8,128)(2,1)}, f32[392,1024]{1,0:T(8,128)}, bf16[392,1024]{1,0:T(8,128)(2,1)}, bf16[392,4096]{1,0:T(8,128)(2,1)}, f32[392,4096]{1,0:T(8,128)}) custom-call(s32[2]{0:T(128)S(1)} %pad_add_fusion.where_ref, bf16[392,128]{1,0:T(8,128)(2,1)} %get-tuple-element.145.refs_0_, bf16[392,128]{1,0:T(8,128)(2,1)} %get-tuple-element.153.refs_1_, ...), custom_call_target="tpu_custom_call" | custom-call | flops 64225280 | bytes 200704 | tf_op jit(solution)/shard_map/hidden_layer/pallas_call | solution.py:367
  140.5 6.5 %weight_away.3 = bf16[4,512,1024]{2,1,0:T(8,128)(2,1)} custom-call(s32[2]{0:T(128)S(1)} %pad_add_fusion.where_ref, bf16[392,4096]{1,0:T(8,128)(2,1)} %get-tuple-element.157.refs_0_.activ_ref, bf16[392,1024]{1,0:T(8,128)(2,1)} %multiply_convert_fusion.refs_1_), custom_call_target="tpu_custom_call" | custom-call | flops 25690112 | bytes 65536 | tf_op jit(solution)/shard_map/weight_away/pallas_call | solution.py:645
  147.0 14.5 %output_layer.1 = (bf16[392,1024]{1,0:T(8,128)(2,1)}, bf16[392,4096]{1,0:T(8,128)(2,1)}, f32[1,4096]{1,0:T(1,128)}) custom-call(s32[2]{0:T(128)S(1)} %pad_add_fusion.where_ref, f32[1]{0:T(128)} %convert_element_type.79.present_ref, bf16[4096,1024]{1,0:T(8,128)(2,1)} %all-gather.6.cloned.1.call-done.w_ref, ...), custom_call_target="tpu_custom_call" | custom-call | flops 102760448 | bytes 301056 | tf_op jit(solution)/shard_map/output_layer/pallas_call | solution.py:432
  161.5 8.0 %weight_kept.3 = (bf16[2,512,512]{2,1,0:T(8,128)(2,1)}, bf16[2,512,512]{2,1,0:T(8,128)(2,1)}, bf16[2,512,512]{2,1,0:T(8,128)(2,1)}, bf16[2,512,512]{2,1,0:T(8,128)(2,1)}) custom-call(s32[2]{0:T(128)S(1)} %pad_add_fusion.where_ref, bf16[392,4096]{1,0:T(8,128)(2,1)} %get-tuple-element.157.refs_0_.activ_ref, bf16[392,1024]{1,0:T(8,128)(2,1)} %multiply_convert_fusion.refs_1_, ...), custom_call_target="tpu_custom_call" | custom-call | flops 25690112 | bytes 65536 | tf_op jit(solution)/shard_map/weight_kept/pallas_call | solution.py:645
  172.1 7.0 %weight_away.4 = bf16[4,128,4096]{2,1,0:T(8,128)(2,1)} custom-call(s32[2]{0:T(128)S(1)} %pad_add_fusion.where_ref, bf16[392,1024]{1,0:T(8,128)(2,1)} %get-tuple-element.167.refs_0_, bf16[392,4096]{1,0:T(8,128)(2,1)} %get-tuple-element.163.refs_1_.ghid_ref), custom_call_target="tpu_custom_call" | custom-call | flops 25690112 | bytes 65536 | tf_op jit(solution)/shard_map/weight_away/pallas_call | solution.py:645
  179.1 14.4 %middle_layer.1 = (f32[392,1024]{1,0:T(8,128)}, bf16[392,1024]{1,0:T(8,128)(2,1)}, bf16[392,256]{1,0:T(8,128)(2,1)}, bf16[392,256]{1,0:T(8,128)(2,1)}, bf16[392,...) custom-call(s32[2]{0:T(128)S(1)} %pad_add_fusion.where_ref, f32[1]{0:T(128)} %convert_element_type.79.present_ref, ...), custom_call_target="tpu_custom_call" | custom-call | flops 64225280 | bytes 301056 | tf_op jit(solution)/shard_map/middle_layer/pallas_call | solution.py:504
  197.1 4.2 %second_sums.3 = (bf16[512,512]{1,0:T(8,128)(2,1)}, bf16[512,512]{1,0:T(8,128)(2,1)}, bf16[512,512]{1,0:T(8,128)(2,1)}, bf16[512,512]{1,0:T(8,128)(2,1)}) custom-call(bf16[2,512,512]{2,1,0:T(8,128)(2,1)} %get-tuple-element.176.keep1_ref, bf16[2,512,512]{2,1,0:T(8,128)(2,1)} %copy-done.25, bf16[2,512,512]{2,1,0:T(8,128)(2,1)} %get-tuple-element.178.keep2_ref, ...), custom_call_target="tpu_custom_call" | custom-call | flops 16384 | bytes 98304 | tf_op jit(solution)/shard_map/second_sums/pallas_call | solution.py:718
  203.5 2.7 collective-permute-start.22
  206.5 5.0 %collective-permute-done.22.refs_1_ = bf16[392,256]{1,0:T(8,128)(2,1)S(1)} collective-permute-done((bf16[392,256]{1,0:T(8,128)(2,1)S(1)}, bf16[392,256]{1,0:T(8,128)(2,1)S(1)}, u32[]{:S(2)}, u32[]{:S(2)}) %collective-permute-start.22) | collective-permute-done | bytes 200736 | tf_op jit(solution)/shard_map/ppermute | solution.py:72
  211.6 10.0 %collective-permute-start.24 = (bf16[392,256]{1,0:T(8,128)(2,1)S(1)}, bf16[392,256]{1,0:T(8,128)(2,1)S(1)}, u32[]{:S(2)}, u32[]{:S(2)}) collective-permute-start(bf16[392,256]{1,0:T(8,128)(2,1)S(1)} %copy-done.73), channel_id=1, source_target_pairs={{0,1},{1,2},{2,3},{3,0},{4,5},{5,6},{6,7},{7,4},{8,9},{9,10},{10,1... | collective-permute-start | bytes 602120 | tf_op jit(solution)/shard_map/ppermute | solution.py:72
  221.6 1.9 collective-permute-done.23.refs_2_
  225.5 2.0 copy-done.11
  227.5 8.6 %weight_kept.4 = (bf16[2,128,2048]{2,1,0:T(8,128)(2,1)}, bf16[2,128,2048]{2,1,0:T(8,128)(2,1)}, bf16[2,128,2048]{2,1,0:T(8,128)(2,1)}, bf16[2,128,2048]{2,1,0:T(8,128)(2,1)}) custom-call(s32[2]{0:T(128)S(1)} %pad_add_fusion.where_ref, bf16[392,1024]{1,0:T(8,128)(2,1)} %get-tuple-element.167.refs_0_, bf16[392,4096]{1,0:T(8,128)(2,1)} %get-tuple-element.163.refs_1_.ghid_ref, ...), custom_call_target="tpu_custom_call" | custom-call | flops 25690112 | bytes 65536 | tf_op jit(solution)/shard_map/weight_kept/pallas_call | solution.py:645
  238.1 4.2 %seq_spread.2 = (f32[128,1024]{1,0:T(8,128)}, bf16[128,1024]{1,0:T(8,128)(2,1)}, bf16[128,1024]{1,0:T(8,128)(2,1)}, bf16[128,1024]{1,0:T(8,128)(2,1)}) custom-call(s32[2]{0:T(128)S(1)} %pad_add_fusion.where_ref, bf16[512,512]{1,0:T(8,128)(2,1)} %get-tuple-element.180.refs_0_, bf16[512,512]{1,0:T(8,128)(2,1)} %copy-done.38, ...), custom_call_target="tpu_custom_call" | custom-call | flops 8192 | bytes 65536 | tf_op jit(solution)/shard_map/seq_spread/pallas_call | solution.py:753
  242.3 2.5 collective-permute-start.32
  244.8 2.6 collective-permute-start.34
  248.3 17.5 %attention_backward.2 = (bf16[392,384]{1,0:T(8,128)(2,1)}, bf16[392,384]{1,0:T(8,128)(2,1)}, bf16[392,384]{1,0:T(8,128)(2,1)}, bf16[392,384]{1,0:T(8,128)(2,1)}) custom-call(bf16[1568,768]{1,0:T(8,128)(2,1)S(1)} %get-tuple-element.144.q_ref.k_ref.v_ref, bf16[1568,768]{1,0:T(8,128)(2,1)S(1)} %get-tuple-element.144.q_ref.k_ref.v_ref, ...), custom_call_target="tpu_custom_call" | custom-call | flops 196689920 | bytes 62720 | tf_op jit(solution)/shard_map/attention_backward/pallas_call | solution.py:291
  266.8 4.2 %second_sums.4 = (bf16[128,2048]{1,0:T(8,128)(2,1)}, bf16[128,2048]{1,0:T(8,128)(2,1)}, bf16[128,2048]{1,0:T(8,128)(2,1)}, bf16[128,2048]{1,0:T(8,128)(2,1)}) custom-call(bf16[2,128,2048]{2,1,0:T(8,128)(2,1)} %get-tuple-element.195.keep1_ref, bf16[2,128,2048]{2,1,0:T(8,128)(2,1)} %copy-done.24, bf16[2,128,2048]{2,1,0:T(8,128)(2,1)} %get-tuple-element.197.keep2_ref, ...), custom_call_target="tpu_custom_call" | custom-call | flops 16384 | bytes 98304 | tf_op jit(solution)/shard_map/second_sums/pallas_call | solution.py:718
  273.3 2.5 collective-permute-start.38
  277.2 17.6 %attention_backward.3 = (bf16[392,384]{1,0:T(8,128)(2,1)}, bf16[392,384]{1,0:T(8,128)(2,1)}, bf16[392,384]{1,0:T(8,128)(2,1)}, bf16[392,384]{1,0:T(8,128)(2,1)}) custom-call(bf16[1568,768]{1,0:T(8,128)(2,1)S(1)} %get-tuple-element.144.q_ref.k_ref.v_ref, bf16[1568,768]{1,0:T(8,128)(2,1)S(1)} %get-tuple-element.144.q_ref.k_ref.v_ref, ...), custom_call_target="tpu_custom_call" | custom-call | flops 196689920 | bytes 62720 | tf_op jit(solution)/shard_map/attention_backward/pallas_call | solution.py:291
  295.8 7.0 %weight_away.5 = bf16[4,128,1792]{2,1,0:T(8,128)(2,1)} custom-call(s32[2]{0:T(128)S(1)} %pad_add_fusion.where_ref, bf16[1568,1024]{1,0:T(8,128)(2,1)} %get-tuple-element.209.refs_0_, bf16[392,384]{1,0:T(8,128)(2,1)} %get-tuple-element.218.refs_1_.refs_0_, bf16[392,384]{1,0:T(8,128)(2,1)} %get-tuple-element.219.refs_2_, ...), custom_call_target="tpu_custom_call" | custom-call | flops 44957696 | bytes 28672 | tf_op jit(solution)/shard_map/weight_away/pallas_call | solution.py:645
  305.2 3.2 collective-permute-done.40.refs_11_
  308.4 7.8 %weight_kept.5 = (bf16[2,128,896]{2,1,0:T(8,128)(2,1)}, bf16[2,128,896]{2,1,0:T(8,128)(2,1)}, bf16[2,128,896]{2,1,0:T(8,128)(2,1)}, bf16[2,128,896]{2,1,0:T(8,128)(2,1)}) custom-call(s32[2]{0:T(128)S(1)} %pad_add_fusion.where_ref, bf16[1568,1024]{1,0:T(8,128)(2,1)} %get-tuple-element.209.refs_0_, bf16[392,384]{1,0:T(8,128)(2,1)} %get-tuple-element.218.refs_1_.refs_0_, ...), custom_call_target="tpu_custom_call" | custom-call | flops 44957696 | bytes 28672 | tf_op jit(solution)/shard_map/weight_kept/pallas_call | solution.py:645
  321.3 3.1 collective-permute-start.47
  324.7 4.3 %collective-permute-done.41.came1_ref = bf16[2,128,896]{2,1,0:T(8,128)(2,1)S(1)} collective-permute-done((bf16[2,128,896]{2,1,0:T(8,128)(2,1)}, bf16[2,128,896]{2,1,0:T(8,128)(2,1)S(1)}, u32[]{:S(2)}, u32[]{:S(2)}) %collective-permute-start.41) | collective-permute-done | bytes 458784 | tf_op jit(solution)/shard_map/ppermute | solution.py:68
  330.9 3.6 second_sums.5
  336.7 4.5 %collective-permute-done.43.refs_1_ = bf16[128,896]{1,0:T(8,128)(2,1)S(1)} collective-permute-done((bf16[128,896]{1,0:T(8,128)(2,1)}, bf16[128,896]{1,0:T(8,128)(2,1)S(1)}, u32[]{:S(2)}, u32[]{:S(2)}) %collective-permute-start.43) | collective-permute-done | bytes 229408 | tf_op jit(solution)/shard_map/ppermute | solution.py:68
  342.8 4.9 %seq_spread.3 = (f32[32,5888]{1,0:T(8,128)}, bf16[32,5888]{1,0:T(8,128)(2,1)}, bf16[32,5888]{1,0:T(8,128)(2,1)}, bf16[32,5888]{1,0:T(8,128)(2,1)}) custom-call(s32[2]{0:T(128)S(1)} %pad_add_fusion.where_ref, bf16[128,896]{1,0:T(8,128)(2,1)} %get-tuple-element.227.refs_0_, bf16[128,896]{1,0:T(8,128)(2,1)} %copy-done.53, ...), custom_call_target="tpu_custom_call" | custom-call | flops 11776 | bytes 94208 | tf_op jit(solution)/shard_map/seq_spread/pallas_call | solution.py:753
  348.6 10.1 %last_layer.1 = (f32[392,1024]{1,0:T(8,128)}, f32[2,1024]{1,0:T(2,128)}) custom-call(s32[2]{0:T(128)} %copy-done, bf16[392,384]{1,0:T(8,128)(2,1)} %get-tuple-element.218.refs_1_.refs_0_, bf16[392,384]{1,0:T(8,128)(2,1)} %get-tuple-element.237.refs_5_.refs_1_, bf16[392,384]{1,0:T(8,128)(2,1)} %copy-done.47, bf16[392,384]{1,0:T(8,128)(2,1)} %copy-done.50, ...), custom_call_target="tpu_custom_call" | custom-call | flops 38535168 | bytes 98304 | tf_op jit(solution)/shard_map/last_layer/pallas_call | solution.py:568
  364.7 2.6 collective-permute-start.56
  368.3 2.0 convert_add_fusion.1
  371.1 4.6 %collective-permute-done.54 = bf16[32,5888]{1,0:T(8,128)(2,1)S(1)} collective-permute-done((bf16[32,5888]{1,0:T(8,128)(2,1)S(1)}, bf16[32,5888]{1,0:T(8,128)(2,1)S(1)}, u32[]{:S(2)}, u32[]{:S(2)}) %collective-permute-start.54) | collective-permute-done | bytes 376864 | tf_op jit(solution)/shard_map/ppermute | solution.py:72
  375.7 15.0 %collective-permute-done.55 = bf16[32,5888]{1,0:T(8,128)(2,1)S(1)} collective-permute-done((bf16[32,5888]{1,0:T(8,128)(2,1)S(1)}, bf16[32,5888]{1,0:T(8,128)(2,1)S(1)}, u32[]{:S(2)}, u32[]{:S(2)}) %collective-permute-start.55) | collective-permute-done | bytes 376864 | tf_op jit(solution)/shard_map/ppermute | solution.py:72
  391.3 8.6 %collective-permute-start.51 = (f32[384]{0:T(512)S(1)}, f32[384]{0:T(512)S(1)}, u32[]{:S(2)}, u32[]{:S(2)}) collective-permute-start(f32[384]{0:T(512)S(1)} %get-tuple-element.281), channel_id=1, source_target_pairs={{0,1},{1,2},{2,3},{3,0},{4,5},{5,6},{6,7},{7,4},{8,9},{9,10},{10,1... | collective-permute-start | bytes 4616 | tf_op jit(solution)/shard_map/ppermute | solution.py:72
  (319 shorter events, 75.9 us)
Async XLA Ops:
  7.2 116.9 %all-gather.4.cloned.1.call-start = ((), (), s32[]{:S(2)}) async-start(), calls=%async_computation | async-start | bytes 11796480 | tf_op jit(solution)/shard_map/all_gather | solution.py:863
  9.7 137.2 %all-gather.6.cloned.1.call-start = ((), (), s32[]{:S(2)}) async-start(), calls=%async_computation.1 | async-start | bytes 9437184 | tf_op jit(solution)/shard_map/all_gather | solution.py:864
  9.8 22.8 %collective-permute-start = (bf16[392,1024]{1,0:T(8,128)(2,1)S(1)}, bf16[392,1024]{1,0:T(8,128)(2,1)S(1)}, u32[]{:S(2)}, u32[]{:S(2)}) collective-permute-start(bf16[392,1024]{1,0:T(8,128)(2,1)S(1)} %bitcast.58), channel_id=1, source_target_pairs={{1,0},{2,1},{3,2},{5,4},{6,5},{7,6},{9,8},{10,9},{11,10},{13,12},{... | collective-permute-start | bytes 2408456 | tf_op jit(solution)/shard_map/ppermute | solution.py:860
  11.1 22.7 %collective-permute-start.1 = (bf16[392,1024]{1,0:T(8,128)(2,1)S(1)}, bf16[392,1024]{1,0:T(8,128)(2,1)S(1)}, u32[]{:S(2)}, u32[]{:S(2)}) collective-permute-start(bf16[392,1024]{1,0:T(8,128)(2,1)S(1)} %bitcast.59), channel_id=1, source_target_pairs={{0,1},{1,2},{2,3},{4,5},{5,6},{6,7},{8,9},{9,10},{10,11},{12,13},{... | collective-permute-start | bytes 2408456 | tf_op jit(solution)/shard_map/ppermute | solution.py:861
  18.5 9.6 %collective-permute-start.2 = (bf16[128,768]{1,0:T(8,128)(2,1)S(1)}, bf16[128,768]{1,0:T(8,128)(2,1)S(1)}, u32[]{:S(2)}, u32[]{:S(2)}) collective-permute-start(bf16[128,768]{1,0:T(8,128)(2,1)S(1)} %pad_maximum_fusion.2.refs_7_), channel_id=1, source_target_pairs={{0,8},{4,12},{8,0},{12,4},{16,24},{20,28},{24,16},{28,20},{1,9},{5... | collective-permute-start | bytes 589832 | tf_op jit(solution)/shard_map/ppermute | solution.py:68
  20.5 9.4 %collective-permute-start.3 = (bf16[128,768]{1,0:T(8,128)(2,1)S(1)}, bf16[128,768]{1,0:T(8,128)(2,1)S(1)}, u32[]{:S(2)}, u32[]{:S(2)}) collective-permute-start(bf16[128,768]{1,0:T(8,128)(2,1)S(1)} %pad_maximum_fusion.2.refs_7_), channel_id=1, source_target_pairs={{0,16},{4,20},{8,24},{12,28},{16,0},{20,4},{24,8},{28,12},{1,17},{... | collective-permute-start | bytes 589832 | tf_op jit(solution)/shard_map/ppermute | solution.py:68
  33.8 313.9 %all-gather.8.cloned.1.call-start = ((), (), s32[]{:S(2)}) async-start(), calls=%async_computation.2 | async-start | bytes 7077888 | tf_op jit(solution)/shard_map/all_gather | solution.py:947
  33.9 21.5 %collective-permute-start.4 = (bf16[392,1024]{1,0:T(8,128)(2,1)S(1)}, bf16[392,1024]{1,0:T(8,128)(2,1)S(1)}, u32[]{:S(2)}, u32[]{:S(2)}) collective-permute-start(bf16[392,1024]{1,0:T(8,128)(2,1)S(1)} %collective-permute-done.refs_1_), channel_id=1, source_target_pairs={{1,0},{2,1},{5,4},{6,5},{9,8},{10,9},{13,12},{14,13},{17,16},{18,1... | collective-permute-start | bytes 2408456 | tf_op jit(solution)/shard_map/ppermute | solution.py:860
  35.2 20.2 %collective-permute-start.5 = (bf16[392,1024]{1,0:T(8,128)(2,1)S(1)}, bf16[392,1024]{1,0:T(8,128)(2,1)}, u32[]{:S(2)}, u32[]{:S(2)}) collective-permute-start(bf16[392,1024]{1,0:T(8,128)(2,1)S(1)} %collective-permute-done.1.refs_4_), channel_id=1, source_target_pairs={{1,2},{2,3},{5,6},{6,7},{9,10},{10,11},{13,14},{14,15},{17,18},{18... | collective-permute-start | bytes 2408456 | tf_op jit(solution)/shard_map/ppermute | solution.py:861
  55.4 20.3 %collective-permute-start.13 = (bf16[392,1024]{1,0:T(8,128)(2,1)S(1)}, bf16[392,1024]{1,0:T(8,128)(2,1)}, u32[]{:S(2)}, u32[]{:S(2)}) collective-permute-start(bf16[392,1024]{1,0:T(8,128)(2,1)S(1)} %collective-permute-done.4.refs_2_), channel_id=1, source_target_pairs={{1,0},{5,4},{9,8},{13,12},{17,16},{21,20},{25,24},{29,28}} | collective-permute-start | bytes 2408456 | tf_op jit(solution)/shard_map/ppermute | solution.py:860
  56.7 19.0 %collective-permute-start.14 = (bf16[392,1024]{1,0:T(8,128)(2,1)}, bf16[392,1024]{1,0:T(8,128)(2,1)}, u32[]{:S(2)}, u32[]{:S(2)}) collective-permute-start(bf16[392,1024]{1,0:T(8,128)(2,1)} %collective-permute-done.5.refs_5_), channel_id=1, source_target_pairs={{2,3},{6,7},{10,11},{14,15},{18,19},{22,23},{26,27},{30,31}} | collective-permute-start | bytes 2408456 | tf_op jit(solution)/shard_map/ppermute | solution.py:861
  95.9 19.3 %collective-permute-start.15 = (bf16[392,128]{1,0:T(8,128)(2,1)}, bf16[392,128]{1,0:T(8,128)(2,1)S(1)}, u32[]{:S(2)}, u32[]{:S(2)}) collective-permute-start(bf16[392,128]{1,0:T(8,128)(2,1)} %get-tuple-element.150), channel_id=1, source_target_pairs={{0,1},{1,2},{2,3},{3,0},{4,5},{5,6},{6,7},{7,4},{8,9},{9,10},{10,1... | collective-permute-start | bytes 301064 | tf_op jit(solution)/shard_map/ppermute | solution.py:72
  95.9 19.3 %collective-permute-start.16 = (bf16[392,128]{1,0:T(8,128)(2,1)}, bf16[392,128]{1,0:T(8,128)(2,1)S(1)}, u32[]{:S(2)}, u32[]{:S(2)}) collective-permute-start(bf16[392,128]{1,0:T(8,128)(2,1)} %get-tuple-element.151), channel_id=1, source_target_pairs={{0,2},{1,3},{2,0},{3,1},{4,6},{5,7},{6,4},{7,5},{8,10},{9,11},{10,... | collective-permute-start | bytes 301064 | tf_op jit(solution)/shard_map/ppermute | solution.py:72
  102.3 12.9 %collective-permute-start.17 = (bf16[392,128]{1,0:T(8,128)(2,1)}, bf16[392,128]{1,0:T(8,128)(2,1)S(1)}, u32[]{:S(2)}, u32[]{:S(2)}) collective-permute-start(bf16[392,128]{1,0:T(8,128)(2,1)} %get-tuple-element.152), channel_id=1, source_target_pairs={{0,3},{1,0},{2,1},{3,2},{4,7},{5,4},{6,5},{7,6},{8,11},{9,8},{10,9... | collective-permute-start | bytes 301064 | tf_op jit(solution)/shard_map/ppermute | solution.py:72
  115.2 6.8 %collective-permute-start.18 = (bf16[392,128]{1,0:T(8,128)(2,1)}, bf16[392,128]{1,0:T(8,128)(2,1)S(1)}, u32[]{:S(2)}, u32[]{:S(2)}) collective-permute-start(bf16[392,128]{1,0:T(8,128)(2,1)} %get-tuple-element.154), channel_id=1, source_target_pairs={{0,1},{1,2},{2,3},{3,0},{4,5},{5,6},{6,7},{7,4},{8,9},{9,10},{10,1... | collective-permute-start | bytes 301064 | tf_op jit(solution)/shard_map/ppermute | solution.py:72
  116.9 7.2 %collective-permute-start.19 = (bf16[392,128]{1,0:T(8,128)(2,1)}, bf16[392,128]{1,0:T(8,128)(2,1)S(1)}, u32[]{:S(2)}, u32[]{:S(2)}) collective-permute-start(bf16[392,128]{1,0:T(8,128)(2,1)} %get-tuple-element.155), channel_id=1, source_target_pairs={{0,2},{1,3},{2,0},{3,1},{4,6},{5,7},{6,4},{7,5},{8,10},{9,11},{10,... | collective-permute-start | bytes 301064 | tf_op jit(solution)/shard_map/ppermute | solution.py:72
  116.9 7.2 %collective-permute-start.20 = (bf16[392,128]{1,0:T(8,128)(2,1)}, bf16[392,128]{1,0:T(8,128)(2,1)S(1)}, u32[]{:S(2)}, u32[]{:S(2)}) collective-permute-start(bf16[392,128]{1,0:T(8,128)(2,1)} %get-tuple-element.156), channel_id=1, source_target_pairs={{0,3},{1,0},{2,1},{3,2},{4,7},{5,4},{6,5},{7,6},{8,11},{9,8},{10,9... | collective-permute-start | bytes 301064 | tf_op jit(solution)/shard_map/ppermute | solution.py:72
  147.0 14.6 %collective-permute-start.21 = (bf16[4,512,1024]{2,1,0:T(8,128)(2,1)}, bf16[4,512,1024]{2,1,0:T(8,128)(2,1)}, u32[]{:S(2)}, u32[]{:S(2)}) collective-permute-start(bf16[4,512,1024]{2,1,0:T(8,128)(2,1)} %weight_away.3), channel_id=1, source_target_pairs={{0,4},{4,0},{8,12},{12,8},{16,20},{20,16},{24,28},{28,24},{1,5},{5... | collective-permute-start | bytes 12582920 | tf_op jit(solution)/shard_map/ppermute | solution.py:68
  169.5 25.8 %collective-permute-start.25 = (bf16[2,512,512]{2,1,0:T(8,128)(2,1)}, bf16[2,512,512]{2,1,0:T(8,128)(2,1)S(1)}, u32[]{:S(2)}, u32[]{:S(2)}) collective-permute-start(bf16[2,512,512]{2,1,0:T(8,128)(2,1)} %get-tuple-element.177), channel_id=1, source_target_pairs={{0,8},{4,12},{8,0},{12,4},{16,24},{20,28},{24,16},{28,20},{1,9},{5... | collective-permute-start | bytes 3145736 | tf_op jit(solution)/shard_map/ppermute | solution.py:68
  170.6 25.5 %collective-permute-start.26 = (bf16[2,512,512]{2,1,0:T(8,128)(2,1)}, bf16[2,512,512]{2,1,0:T(8,128)(2,1)S(1)}, u32[]{:S(2)}, u32[]{:S(2)}) collective-permute-start(bf16[2,512,512]{2,1,0:T(8,128)(2,1)} %get-tuple-element.179), channel_id=1, source_target_pairs={{0,16},{4,20},{8,24},{12,28},{16,0},{20,4},{24,8},{28,12},{1,17},{... | collective-permute-start | bytes 3145736 | tf_op jit(solution)/shard_map/ppermute | solution.py:68
  196.1 29.4 %collective-permute-start.29 = (bf16[4,128,4096]{2,1,0:T(8,128)(2,1)S(1)}, bf16[4,128,4096]{2,1,0:T(8,128)(2,1)S(1)}, u32[]{:S(2)}, u32[]{:S(2)}) collective-permute-start(bf16[4,128,4096]{2,1,0:T(8,128)(2,1)S(1)} %copy-done.10), channel_id=1, source_target_pairs={{0,4},{4,0},{8,12},{12,8},{16,20},{20,16},{24,28},{28,24},{1,5},{5... | collective-permute-start | bytes 12582920 | tf_op jit(solution)/shard_map/ppermute | solution.py:68
  201.3 23.5 %collective-permute-start.27 = (bf16[512,512]{1,0:T(8,128)(2,1)}, bf16[512,512]{1,0:T(8,128)(2,1)S(1)}, u32[]{:S(2)}, u32[]{:S(2)}) collective-permute-start(bf16[512,512]{1,0:T(8,128)(2,1)} %get-tuple-element.183), channel_id=1, source_target_pairs={{0,16},{4,20},{8,24},{12,28},{16,0},{20,4},{24,8},{28,12},{1,17},{... | collective-permute-start | bytes 1572872 | tf_op jit(solution)/shard_map/ppermute | solution.py:68
  202.8 22.0 %collective-permute-start.28 = (bf16[512,512]{1,0:T(8,128)(2,1)}, bf16[512,512]{1,0:T(8,128)(2,1)S(1)}, u32[]{:S(2)}, u32[]{:S(2)}) collective-permute-start(bf16[512,512]{1,0:T(8,128)(2,1)} %get-tuple-element.184), channel_id=1, source_target_pairs={{0,8},{4,12},{8,0},{12,4},{16,24},{20,28},{24,16},{28,20},{1,9},{5... | collective-permute-start | bytes 1572872 | tf_op jit(solution)/shard_map/ppermute | solution.py:68
  203.5 8.1 %collective-permute-start.22 = (bf16[392,256]{1,0:T(8,128)(2,1)S(1)}, bf16[392,256]{1,0:T(8,128)(2,1)S(1)}, u32[]{:S(2)}, u32[]{:S(2)}) collective-permute-start(bf16[392,256]{1,0:T(8,128)(2,1)S(1)} %copy-done.75), channel_id=1, source_target_pairs={{0,3},{1,0},{2,1},{3,2},{4,7},{5,4},{6,5},{7,6},{8,11},{9,8},{10,9... | collective-permute-start | bytes 602120 | tf_op jit(solution)/shard_map/ppermute | solution.py:72
  206.1 17.3 %collective-permute-start.23 = (bf16[392,256]{1,0:T(8,128)(2,1)S(1)}, bf16[392,256]{1,0:T(8,128)(2,1)S(1)}, u32[]{:S(2)}, u32[]{:S(2)}) collective-permute-start(bf16[392,256]{1,0:T(8,128)(2,1)S(1)} %copy-done.74), channel_id=1, source_target_pairs={{0,2},{1,3},{2,0},{3,1},{4,6},{5,7},{6,4},{7,5},{8,10},{9,11},{10,... | collective-permute-start | bytes 602120 | tf_op jit(solution)/shard_map/ppermute | solution.py:72
  211.6 13.3 %collective-permute-start.24 = (bf16[392,256]{1,0:T(8,128)(2,1)S(1)}, bf16[392,256]{1,0:T(8,128)(2,1)S(1)}, u32[]{:S(2)}, u32[]{:S(2)}) collective-permute-start(bf16[392,256]{1,0:T(8,128)(2,1)S(1)} %copy-done.73), channel_id=1, source_target_pairs={{0,1},{1,2},{2,3},{3,0},{4,5},{5,6},{6,7},{7,4},{8,9},{9,10},{10,1... | collective-permute-start | bytes 602120 | tf_op jit(solution)/shard_map/ppermute | solution.py:72
  236.1 29.7 %collective-permute-start.30 = (bf16[2,128,2048]{2,1,0:T(8,128)(2,1)}, bf16[2,128,2048]{2,1,0:T(8,128)(2,1)S(1)}, u32[]{:S(2)}, u32[]{:S(2)}) collective-permute-start(bf16[2,128,2048]{2,1,0:T(8,128)(2,1)} %get-tuple-element.196), channel_id=1, source_target_pairs={{0,8},{4,12},{8,0},{12,4},{16,24},{20,28},{24,16},{28,20},{1,9},{5... | collective-permute-start | bytes 3145736 | tf_op jit(solution)/shard_map/ppermute | solution.py:68
  237.5 28.3 %collective-permute-start.31 = (bf16[2,128,2048]{2,1,0:T(8,128)(2,1)}, bf16[2,128,2048]{2,1,0:T(8,128)(2,1)}, u32[]{:S(2)}, u32[]{:S(2)}) collective-permute-start(bf16[2,128,2048]{2,1,0:T(8,128)(2,1)} %get-tuple-element.198), channel_id=1, source_target_pairs={{0,16},{4,20},{8,24},{12,28},{16,0},{20,4},{24,8},{28,12},{1,17},{... | collective-permute-start | bytes 3145736 | tf_op jit(solution)/shard_map/ppermute | solution.py:68
  242.3 28.7 %collective-permute-start.32 = (bf16[128,1024]{1,0:T(8,128)(2,1)}, bf16[128,1024]{1,0:T(8,128)(2,1)}, u32[]{:S(2)}, u32[]{:S(2)}) collective-permute-start(bf16[128,1024]{1,0:T(8,128)(2,1)} %get-tuple-element.192), channel_id=1, source_target_pairs={{0,1},{1,2},{2,3},{3,0},{4,5},{5,6},{6,7},{7,4},{8,9},{9,10},{10,1... | collective-permute-start | bytes 786440 | tf_op jit(solution)/shard_map/ppermute | solution.py:72
  244.8 26.2 %collective-permute-start.33 = (bf16[128,1024]{1,0:T(8,128)(2,1)}, bf16[128,1024]{1,0:T(8,128)(2,1)}, u32[]{:S(2)}, u32[]{:S(2)}) collective-permute-start(bf16[128,1024]{1,0:T(8,128)(2,1)} %get-tuple-element.204), channel_id=1, source_target_pairs={{0,2},{1,3},{2,0},{3,1},{4,6},{5,7},{6,4},{7,5},{8,10},{9,11},{10,... | collective-permute-start | bytes 786440 | tf_op jit(solution)/shard_map/ppermute | solution.py:72
  244.8 26.2 %collective-permute-start.34 = (bf16[128,1024]{1,0:T(8,128)(2,1)}, bf16[128,1024]{1,0:T(8,128)(2,1)}, u32[]{:S(2)}, u32[]{:S(2)}) collective-permute-start(bf16[128,1024]{1,0:T(8,128)(2,1)} %get-tuple-element.205), channel_id=1, source_target_pairs={{0,3},{1,0},{2,1},{3,2},{4,7},{5,4},{6,5},{7,6},{8,11},{9,8},{10,9... | collective-permute-start | bytes 786440 | tf_op jit(solution)/shard_map/ppermute | solution.py:72
  271.1 23.7 %collective-permute-start.35 = (bf16[128,2048]{1,0:T(8,128)(2,1)}, bf16[128,2048]{1,0:T(8,128)(2,1)S(1)}, u32[]{:S(2)}, u32[]{:S(2)}) collective-permute-start(bf16[128,2048]{1,0:T(8,128)(2,1)} %get-tuple-element.206), channel_id=1, source_target_pairs={{0,16},{4,20},{8,24},{12,28},{16,0},{20,4},{24,8},{28,12},{1,17},{... | collective-permute-start | bytes 1572872 | tf_op jit(solution)/shard_map/ppermute | solution.py:68
  272.6 22.1 %collective-permute-start.36 = (bf16[128,2048]{1,0:T(8,128)(2,1)}, bf16[128,2048]{1,0:T(8,128)(2,1)S(1)}, u32[]{:S(2)}, u32[]{:S(2)}) collective-permute-start(bf16[128,2048]{1,0:T(8,128)(2,1)} %get-tuple-element.207), channel_id=1, source_target_pairs={{0,8},{4,12},{8,0},{12,4},{16,24},{20,28},{24,16},{28,20},{1,9},{5... | collective-permute-start | bytes 1572872 | tf_op jit(solution)/shard_map/ppermute | solution.py:68
  273.3 29.5 %collective-permute-start.37 = (bf16[392,384]{1,0:T(8,128)(2,1)S(1)}, bf16[392,384]{1,0:T(8,128)(2,1)S(1)}, u32[]{:S(2)}, u32[]{:S(2)}) collective-permute-start(bf16[392,384]{1,0:T(8,128)(2,1)S(1)} %copy-done.18), channel_id=1, source_target_pairs={{0,1},{1,2},{2,3},{3,0},{4,5},{5,6},{6,7},{7,4},{8,9},{9,10},{10,1... | collective-permute-start | bytes 903176 | tf_op jit(solution)/shard_map/ppermute | solution.py:72
  273.3 29.5 %collective-permute-start.38 = (bf16[392,384]{1,0:T(8,128)(2,1)S(1)}, bf16[392,384]{1,0:T(8,128)(2,1)S(1)}, u32[]{:S(2)}, u32[]{:S(2)}) collective-permute-start(bf16[392,384]{1,0:T(8,128)(2,1)S(1)} %copy-done.20), channel_id=1, source_target_pairs={{0,2},{1,3},{2,0},{3,1},{4,6},{5,7},{6,4},{7,5},{8,10},{9,11},{10,... | collective-permute-start | bytes 903176 | tf_op jit(solution)/shard_map/ppermute | solution.py:72
  275.8 27.0 %collective-permute-start.39 = (bf16[392,384]{1,0:T(8,128)(2,1)S(1)}, bf16[392,384]{1,0:T(8,128)(2,1)S(1)}, u32[]{:S(2)}, u32[]{:S(2)}) collective-permute-start(bf16[392,384]{1,0:T(8,128)(2,1)S(1)} %copy-done.22), channel_id=1, source_target_pairs={{0,3},{1,0},{2,1},{3,2},{4,7},{5,4},{6,5},{7,6},{8,11},{9,8},{10,9... | collective-permute-start | bytes 903176 | tf_op jit(solution)/shard_map/ppermute | solution.py:72
  316.2 12.8 %collective-permute-start.41 = (bf16[2,128,896]{2,1,0:T(8,128)(2,1)}, bf16[2,128,896]{2,1,0:T(8,128)(2,1)S(1)}, u32[]{:S(2)}, u32[]{:S(2)}) collective-permute-start(bf16[2,128,896]{2,1,0:T(8,128)(2,1)} %get-tuple-element.224), channel_id=1, source_target_pairs={{0,8},{4,12},{8,0},{12,4},{16,24},{20,28},{24,16},{28,20},{1,9},{5... | collective-permute-start | bytes 1376264 | tf_op jit(solution)/shard_map/ppermute | solution.py:68
  317.7 12.5 %collective-permute-start.42 = (bf16[2,128,896]{2,1,0:T(8,128)(2,1)}, bf16[2,128,896]{2,1,0:T(8,128)(2,1)S(1)}, u32[]{:S(2)}, u32[]{:S(2)}) collective-permute-start(bf16[2,128,896]{2,1,0:T(8,128)(2,1)} %get-tuple-element.226), channel_id=1, source_target_pairs={{0,16},{4,20},{8,24},{12,28},{16,0},{20,4},{24,8},{28,12},{1,17},{... | collective-permute-start | bytes 1376264 | tf_op jit(solution)/shard_map/ppermute | solution.py:68
  318.8 28.9 %collective-permute-start.45 = (bf16[392,384]{1,0:T(8,128)(2,1)S(1)}, bf16[392,384]{1,0:T(8,128)(2,1)S(1)}, u32[]{:S(2)}, u32[]{:S(2)}) collective-permute-start(bf16[392,384]{1,0:T(8,128)(2,1)S(1)} %copy-done.17), channel_id=1, source_target_pairs={{0,1},{1,2},{2,3},{3,0},{4,5},{5,6},{6,7},{7,4},{8,9},{9,10},{10,1... | collective-permute-start | bytes 903176 | tf_op jit(solution)/shard_map/ppermute | solution.py:72
  319.8 27.9 %collective-permute-start.46 = (bf16[392,384]{1,0:T(8,128)(2,1)S(1)}, bf16[392,384]{1,0:T(8,128)(2,1)S(1)}, u32[]{:S(2)}, u32[]{:S(2)}) collective-permute-start(bf16[392,384]{1,0:T(8,128)(2,1)S(1)} %copy-done.15), channel_id=1, source_target_pairs={{0,2},{1,3},{2,0},{3,1},{4,6},{5,7},{6,4},{7,5},{8,10},{9,11},{10,... | collective-permute-start | bytes 903176 | tf_op jit(solution)/shard_map/ppermute | solution.py:72
  321.3 26.5 %collective-permute-start.47 = (bf16[392,384]{1,0:T(8,128)(2,1)S(1)}, bf16[392,384]{1,0:T(8,128)(2,1)S(1)}, u32[]{:S(2)}, u32[]{:S(2)}) collective-permute-start(bf16[392,384]{1,0:T(8,128)(2,1)S(1)} %copy-done.14), channel_id=1, source_target_pairs={{0,3},{1,0},{2,1},{3,2},{4,7},{5,4},{6,5},{7,6},{8,11},{9,8},{10,9... | collective-permute-start | bytes 903176 | tf_op jit(solution)/shard_map/ppermute | solution.py:72
  334.5 6.7 %collective-permute-start.43 = (bf16[128,896]{1,0:T(8,128)(2,1)}, bf16[128,896]{1,0:T(8,128)(2,1)S(1)}, u32[]{:S(2)}, u32[]{:S(2)}) collective-permute-start(bf16[128,896]{1,0:T(8,128)(2,1)} %get-tuple-element.231), channel_id=1, source_target_pairs={{0,16},{4,20},{8,24},{12,28},{16,0},{20,4},{24,8},{28,12},{1,17},{... | collective-permute-start | bytes 688136 | tf_op jit(solution)/shard_map/ppermute | solution.py:68
  335.6 6.4 %collective-permute-start.44 = (bf16[128,896]{1,0:T(8,128)(2,1)}, bf16[128,896]{1,0:T(8,128)(2,1)S(1)}, u32[]{:S(2)}, u32[]{:S(2)}) collective-permute-start(bf16[128,896]{1,0:T(8,128)(2,1)} %get-tuple-element.233), channel_id=1, source_target_pairs={{0,8},{4,12},{8,0},{12,4},{16,24},{20,28},{24,16},{28,20},{1,9},{5... | collective-permute-start | bytes 688136 | tf_op jit(solution)/shard_map/ppermute | solution.py:68
  362.1 13.6 %collective-permute-start.54 = (bf16[32,5888]{1,0:T(8,128)(2,1)S(1)}, bf16[32,5888]{1,0:T(8,128)(2,1)S(1)}, u32[]{:S(2)}, u32[]{:S(2)}) collective-permute-start(bf16[32,5888]{1,0:T(8,128)(2,1)S(1)} %copy-done.72), channel_id=1, source_target_pairs={{0,1},{1,2},{2,3},{3,0},{4,5},{5,6},{6,7},{7,4},{8,9},{9,10},{10,1... | collective-permute-start | bytes 1130504 | tf_op jit(solution)/shard_map/ppermute | solution.py:72
  363.5 27.3 %collective-permute-start.55 = (bf16[32,5888]{1,0:T(8,128)(2,1)S(1)}, bf16[32,5888]{1,0:T(8,128)(2,1)S(1)}, u32[]{:S(2)}, u32[]{:S(2)}) collective-permute-start(bf16[32,5888]{1,0:T(8,128)(2,1)S(1)} %copy-done.71), channel_id=1, source_target_pairs={{0,2},{1,3},{2,0},{3,1},{4,6},{5,7},{6,4},{7,5},{8,10},{9,11},{10,... | collective-permute-start | bytes 1130504 | tf_op jit(solution)/shard_map/ppermute | solution.py:72
  364.7 26.0 %collective-permute-start.56 = (bf16[32,5888]{1,0:T(8,128)(2,1)S(1)}, bf16[32,5888]{1,0:T(8,128)(2,1)S(1)}, u32[]{:S(2)}, u32[]{:S(2)}) collective-permute-start(bf16[32,5888]{1,0:T(8,128)(2,1)S(1)} %copy-done.70), channel_id=1, source_target_pairs={{0,3},{1,0},{2,1},{3,2},{4,7},{5,4},{6,5},{7,6},{8,11},{9,8},{10,9... | collective-permute-start | bytes 1130504 | tf_op jit(solution)/shard_map/ppermute | solution.py:72
  391.3 15.2 %collective-permute-start.51 = (f32[384]{0:T(512)S(1)}, f32[384]{0:T(512)S(1)}, u32[]{:S(2)}, u32[]{:S(2)}) collective-permute-start(f32[384]{0:T(512)S(1)} %get-tuple-element.281), channel_id=1, source_target_pairs={{0,1},{1,2},{2,3},{3,0},{4,5},{5,6},{6,7},{7,4},{8,9},{9,10},{10,1... | collective-permute-start | bytes 4616 | tf_op jit(solution)/shard_map/ppermute | solution.py:72
  399.9 6.6 %collective-permute-start.52 = (f32[384]{0:T(512)S(1)}, f32[384]{0:T(512)S(1)}, u32[]{:S(2)}, u32[]{:S(2)}) collective-permute-start(f32[384]{0:T(512)S(1)} %get-tuple-element.283), channel_id=1, source_target_pairs={{0,2},{1,3},{2,0},{3,1},{4,6},{5,7},{6,4},{7,5},{8,10},{9,11},{10,... | collective-permute-start | bytes 4616 | tf_op jit(solution)/shard_map/ppermute | solution.py:72
  (88 other events, 1377.2 us)
Sparse Core Ops, SparseCore 0:
  10.5 66.9 all-gather.3
  79.4 54.3 all-gather.5
  271.2 44.2 all-gather.7
